TPU v7x, 128 devices: a whole 4x4x4 slice. The times are simulated.
128 devices in a mesh: ctx: 32 (over x, y, core), tp: 4 (over z).
Axes of the slice: x: 4, y: 4, z: 4, core: 2. Of those that a mesh axis runs over, the one named last changes fastest.
Arguments:
- tokens: bfloat16 [32768, 2048], P('ctx'), may hold values from -6 to 6
- w_value: bfloat16 [2048, 4096], P(None, 'tp'), may hold values from -0.125 to 0.125
- w_gate: bfloat16 [2048, 4096], P(None, 'tp'), may hold values from -0.125 to 0.125
- w_state: bfloat16 [2048, 256], replicated, may hold values from -0.125 to 0.125
- w_level: bfloat16 [2048, 512], P(None, 'tp'), may hold values from -0.125 to 0.125
- log_decay: float32 [32768, 64], P('ctx', 'tp'), may hold values from -1.6 to 0
- skip_weight: float32 [64], P('tp'), may hold values from 0.5 to 1.5
- norm_gain: float32 [4096], P('tp'), may hold values from 0.5 to 1.5
- doc_ids: int32 [128], replicated, may hold values from 0 to 3, as said below
- w_out: bfloat16 [4096, 2048], P('tp'), may hold values from -0.09375 to 0.09375
Outputs:
- mixed: bfloat16 [32768, 2048], P('ctx', 'tp')
Inputs may be any that keep to these rules, and one draw needn't show every extreme that they name: `doc_ids`: is non-decreasing along the stretches; each document is a run of whole stretches; all 4 documents occur; the longest holds exactly 65 stretches.
All inputs are finite; a program needn't handle non-finite values.
Results may differ from a plain program's by a relative error of at most 0.022.
Values may be sent and summed in bfloat16 or wider, within the bound.
No kernel may reach another device: no remote copies, remote signals or barrier semaphores. Data moves between devices by JAX's collectives and lax.ppermute only.
A program may use at most 128 MiB of HBM per device.

v0:
```python
import functools

import jax
import jax.numpy as jnp
from jax import lax
from jax.experimental import pallas as pl
from jax.experimental.pallas import tpu as pltpu
from jax.sharding import PartitionSpec as P

STRETCH = 256
STEPS = 4
HEAD = 64
STATE = 128
LEVELS = 8
BLOCK = 256
F32 = jnp.float32
BF16 = jnp.bfloat16
HIGHEST = lax.Precision.HIGHEST
NT = (((1,), (1,)), ((), ()))
CHUNKS = ((0, 2), (2, 4))
SMEM = pl.BlockSpec(memory_space=pltpu.SMEM)
VMEM = pl.BlockSpec(memory_space=pltpu.VMEM)
FAR = pl.BlockSpec(memory_space=pltpu.HBM)


def dot(a, b):
    return jnp.dot(a, b, preferred_element_type=F32)


def dot_nt(a, b):
    return lax.dot_general(a, b, NT, preferred_element_type=F32)


def iota(shape, dim):
    return lax.broadcasted_iota(jnp.int32, shape, dim)


def far(x):
    return pltpu.with_memory_space_constraint(x, pltpu.HBM)


def twice(x):
    return jnp.concatenate([x, x], axis=1)


def upper_ones():
    shape = (STRETCH, STRETCH)
    return (iota(shape, 0) <= iota(shape, 1)).astype(F32)


def running_sums(decays):
    return jnp.dot(decays, upper_ones(), precision=HIGHEST, preferred_element_type=F32)


def lanes(column):
    return jnp.broadcast_to(column, (column.shape[0], STATE))


def store_total(ref, top, total):
    heads = total.shape[0]
    high = total.astype(BF16)
    rest = total - high.astype(F32)
    middle = rest.astype(BF16)
    low = (rest - middle.astype(F32)).astype(BF16)
    ref[pl.ds(top, heads), :] = high
    ref[pl.ds(top + heads, heads), :] = middle
    ref[pl.ds(top + 2 * heads, heads), :] = low


def load_total(ref, top, heads):
    parts = [ref[pl.ds(top + k * heads, heads), :].astype(F32) for k in range(3)]
    return (parts[0] + parts[1]) + parts[2]


def call(kernel, name, in_specs, out_shape, args, scratch=(), mib=8, flops=1 << 20, moved=1 << 20, out_specs=None):
    return pl.pallas_call(
        kernel,
        name=name,
        in_specs=in_specs,
        out_specs=[VMEM] * len(out_shape),
        out_shape=[jax.ShapeDtypeStruct(*x) for x in out_shape],
        scratch_shapes=list(scratch),
        compiler_params=pltpu.CompilerParams(vmem_limit_bytes=mib << 20),
        cost_estimate=pl.CostEstimate(flops=flops, bytes_accessed=moved, transcendentals=0),
    )(*args)


def project_kernel(
    meta, docs, decays, tok_hbm, value_hbm, state_hbm, gate_hbm, tok, gate, sp, v, local, pay, w_value, w_state, tail,
    grow, scaled, sems,
):
    heads = decays.shape[0]
    blocks = w_value.shape[1] // BLOCK
    per_block = BLOCK // HEAD

    def token_copy(i):
        at = pl.ds(i * STRETCH, STRETCH)
        return pltpu.make_async_copy(tok_hbm.at[at, :], tok.at[at, :], sems.at[i])

    def value_copy(k):
        at = pl.ds(pl.multiple_of(k * BLOCK, BLOCK), BLOCK)
        return pltpu.make_async_copy(value_hbm.at[:, at], w_value.at[:, at], sems.at[STEPS + k])

    state_copy = pltpu.make_async_copy(state_hbm, w_state, sems.at[STEPS + blocks])
    gate_copy = pltpu.make_async_copy(gate_hbm, gate, sems.at[STEPS + blocks + 1])
    token_copy(0).start()
    state_copy.start()
    for i in range(1, STEPS):
        token_copy(i).start()
    value_copy(0).start()

    stacked = jnp.concatenate([decays[:, i * STRETCH : (i + 1) * STRETCH] for i in range(STEPS)], axis=0)
    cum = running_sums(stacked)
    total = lanes(cum[:, STRETCH - 1 :])
    rest = jnp.exp(twice(total) - cum)
    first = meta[0] * STEPS
    whole = jnp.zeros((heads, STATE), F32)
    for i in range(STEPS):
        rows = slice(i * heads, (i + 1) * heads)
        tail[:, pl.ds(i * STRETCH, STRETCH)] = rest[rows]
        same = (docs[first + max(i - 1, 0)] == docs[first + i]).astype(F32)
        grow[i] = jnp.exp(total[rows]) * same
        whole = whole + total[rows]
    store_total(pay, heads * HEAD, whole)

    state_copy.wait()
    for i in range(STEPS):
        token_copy(i).wait()
        at = pl.ds(i * STRETCH, STRETCH)
        sp[at, :] = dot(tok[at, :], w_state[...]).astype(BF16)

    @pl.loop(0, blocks)
    def _(k):
        value_copy(k).wait()

        @pl.when(k + 1 < blocks)
        def _():
            value_copy(k + 1).start()

        @pl.when(k == 1)
        def _():
            gate_copy.start()

        at = pl.ds(pl.multiple_of(k * BLOCK, BLOCK), BLOCK)
        v[at, :] = jnp.transpose(dot(tok[...], w_value[:, at]).astype(BF16))
        for h in range(per_block):
            rows = pl.ds(pl.multiple_of(k * BLOCK + h * HEAD, HEAD), HEAD)
            scaled[pl.ds(h * HEAD, HEAD), :] = (
                v[rows, :].astype(F32) * tail[pl.ds(k * per_block + h, 1), :]
            ).astype(BF16)
        run = None
        for i in range(STEPS):
            here = pl.ds(i * STRETCH, STRETCH)
            state = dot(scaled[:, here], sp[here, :STATE])
            if i == 0:
                run = state
                local[0, at, :] = state.astype(BF16)
                continue
            factor = jnp.concatenate(
                [
                    jnp.broadcast_to(grow[i, pl.ds(k * per_block + h, 1), :], (HEAD, STATE))
                    for h in range(per_block)
                ],
                axis=0,
            )
            run = run * factor + state
            if i == 1:
                local[1, at, :] = run.astype(BF16)
            if i == 2:
                local[2, at, :] = state.astype(BF16)
        pay[at, :] = run.astype(BF16)

    gate_copy.wait()


def project(meta, docs, decays, tokens, w_value, w_state, w_gate):
    rows, depth = tokens.shape
    heads = decays.shape[0]
    width = w_value.shape[1]
    return call(
        project_kernel,
        "project",
        [SMEM, SMEM, VMEM, FAR, FAR, FAR, FAR],
        [
            ((rows, depth), BF16),
            ((depth, width), BF16),
            ((rows, 2 * STATE), BF16),
            ((width, rows), BF16),
            ((3, width, STATE), BF16),
            ((width + 3 * heads, STATE), BF16),
        ],
        (meta, docs, decays, *(far(x) for x in (tokens, w_value, w_state, w_gate))),
        [
            pltpu.VMEM((depth, width), BF16),
            pltpu.VMEM((depth, 2 * STATE), BF16),
            pltpu.VMEM((heads, rows), F32),
            pltpu.VMEM((STEPS, heads, STATE), F32),
            pltpu.VMEM((BLOCK, rows), BF16),
            pltpu.SemaphoreType.DMA((STEPS + width // BLOCK + 2,)),
        ],
        mib=16,
        flops=2 * rows * depth * (width + 2 * STATE),
        moved=2 * (rows * depth + 2 * depth * width),
    )


def joined(docs, last_first, last_second):
    return (docs[last_first] == docs[last_second]).astype(F32)


def near_kernel(meta, docs, own, peer, pay, earlier):
    heads = earlier.shape[0]
    top = heads * HEAD
    ctx = meta[0]
    second = (ctx & 1) == 1
    pair = ctx >> 1
    total_own, total_peer = load_total(own, top, heads), load_total(peer, top, heads)
    keep = joined(docs, pair * 2 * STEPS + STEPS - 1, pair * 2 * STEPS + 2 * STEPS - 1)
    factor = jnp.exp(jnp.where(second, total_own, total_peer)) * keep
    own_by = jnp.where(second, 1.0, factor)
    peer_by = jnp.where(second, factor, 1.0)
    for h in range(heads):
        at = pl.ds(h * HEAD, HEAD)
        pay[at, :] = (own[at, :].astype(F32) * own_by[h : h + 1] + peer[at, :].astype(F32) * peer_by[h : h + 1]).astype(
            BF16
        )
    store_total(pay, top, total_own + total_peer)
    earlier[...] = jnp.where(second, total_peer, 0.0)


def middle_kernel(meta, docs, own, one, two, three, before, pay, left, earlier):
    heads = before.shape[0]
    top = heads * HEAD
    ctx = meta[0]
    chip = ctx >> 1
    odd, high = (chip & 1) == 1, (chip & 2) == 2
    t_own, t_one, t_two, t_three = (load_total(x, top, heads) for x in (own, one, two, three))
    last = lambda at: (at + 1) * 2 * STEPS - 1
    base, mine, theirs = (chip >> 2) << 2, (chip >> 1) << 1, ((chip >> 1) ^ 1) << 1
    keep_mine = joined(docs, last(mine), last(mine + 1))
    keep_theirs = joined(docs, last(theirs), last(theirs + 1))
    keep_all = joined(docs, last(base + 1), last(base + 3))
    by_mine = jnp.exp(jnp.where(odd, t_own, t_one)) * keep_mine
    by_theirs = jnp.exp(jnp.where(odd, t_two, t_three)) * keep_theirs
    own_by, one_by = jnp.where(odd, 1.0, by_mine), jnp.where(odd, by_mine, 1.0)
    two_by, three_by = jnp.where(odd, 1.0, by_theirs), jnp.where(odd, by_theirs, 1.0)
    by_all = jnp.exp(jnp.where(high, t_own + t_one, t_two + t_three)) * keep_all
    mine_by, theirs_by = jnp.where(high, 1.0, by_all), jnp.where(high, by_all, 1.0)
    for h in range(heads):
        at = pl.ds(h * HEAD, HEAD)
        row = slice(h, h + 1)
        here = own[at, :].astype(F32) * own_by[row] + one[at, :].astype(F32) * one_by[row]
        there = two[at, :].astype(F32) * two_by[row] + three[at, :].astype(F32) * three_by[row]
        left[at, :] = there.astype(BF16)
        pay[at, :] = (here * mine_by[row] + there * theirs_by[row]).astype(BF16)
    store_total(pay, top, (t_own + t_one) + (t_two + t_three))
    second = before[...] + jnp.where(odd, t_one, 0.0)
    earlier[pl.ds(0, heads), :] = second
    earlier[pl.ds(heads, heads), :] = second + jnp.where(high, t_two + t_three, 0.0)


def far_kernel(meta, docs, one, two, three, before, left, earlier):
    heads = earlier.shape[0]
    top = heads * HEAD
    row_of = meta[0] >> 3
    odd = (row_of & 1) == 1
    t_one, t_two, t_three = (load_total(x, top, heads) for x in (one, two, three))
    theirs = ((row_of >> 1) ^ 1) << 1
    last = lambda at: (at + 1) * 8 * STEPS - 1
    factor = jnp.exp(jnp.where(odd, t_two, t_three)) * joined(docs, last(theirs), last(theirs + 1))
    two_by, three_by = jnp.where(odd, 1.0, factor), jnp.where(odd, factor, 1.0)
    for h in range(heads):
        at = pl.ds(h * HEAD, HEAD)
        left[at, :] = (
            two[at, :].astype(F32) * two_by[h : h + 1] + three[at, :].astype(F32) * three_by[h : h + 1]
        ).astype(BF16)
    earlier[...] = before[pl.ds(heads, heads), :] + jnp.where(odd, t_one, 0.0)


def gate_kernel(tok, gate, w_level, out_hbm, gates, weight, w_out, sem):
    copy = pltpu.make_async_copy(out_hbm, w_out, sem)
    copy.start()
    cols = w_level.shape[1]
    heads = cols // LEVELS
    to_row, from_col = iota((cols, cols), 0), iota((cols, cols), 1)
    pick = ((to_row % heads) * LEVELS + to_row // heads == from_col).astype(BF16)
    turned = dot_nt(pick, dot(tok[...], w_level[...]).astype(BF16))
    weight[...] = jnp.maximum(turned, 0.0) + jnp.log1p(jnp.exp(-jnp.abs(turned)))

    @pl.loop(0, gate.shape[1] // BLOCK)
    def _(k):
        at = pl.ds(pl.multiple_of(k * BLOCK, BLOCK), BLOCK)
        gates[at, :] = jnp.transpose(dot(tok[...], gate[:, at]).astype(BF16))

    copy.wait()


def intra_kernel(meta, docs, skip, weight, decays, v, sp, local, ho, scaled_weight):
    heads = decays.shape[0]
    first = meta[0] * STEPS
    causal = iota((128, 128), 0) <= iota((128, 128), 1)
    lower = (iota((STRETCH, STRETCH), 0) >= iota((STRETCH, STRETCH), 1)).astype(F32)
    begin = jnp.zeros((heads, STATE), F32)
    previous = begin
    for index in range(STEPS):
        here = pl.ds(index * STRETCH, STRETCH)
        now = decays[:, here]
        cum = running_sums(now)
        cum_col = lax.dot_general(lower, now, NT, precision=HIGHEST, preferred_element_type=F32)
        total = lanes(cum[:, STRETCH - 1 :])
        grown = jnp.exp(cum)
        from_device = jnp.exp(cum + twice(begin))
        for level in range(3, LEVELS):
            rows = pl.ds(level * heads, heads)
            scaled_weight[rows, here] = weight[rows, here] * from_device
        b_in, c_out = sp[here, :STATE], sp[here, STATE:]
        scores = dot_nt(b_in, c_out)
        terms = []
        if index & 1:
            keep = joined(docs, first + index - 1, first + index)
            terms.append((0 if index == 1 else 2, weight[pl.ds(heads, heads), here] * grown * keep))
        if index & 2:
            keep = joined(docs, first + 1, first + index)
            factor = grown * jnp.exp(twice(previous)) if index == 3 else grown
            terms.append((1, weight[pl.ds(2 * heads, heads), here] * factor * keep))
        crosses = [(dot_nt(local[slot], c_out), row) for slot, row in terms]
        own_weight = weight[pl.ds(0, heads), here]
        for h in range(heads):
            at = slice(h * HEAD, (h + 1) * HEAD)
            col = cum_col[:, h : h + 1]
            row = cum[h : h + 1, :]

            def block(s, t, masked):
                decay = jnp.exp(
                    jnp.broadcast_to(row[:, t * 128 : t * 128 + 128], (128, 128)) - col[s * 128 : s * 128 + 128, :]
                )
                if masked:
                    decay = jnp.where(causal, decay, 0.0)
                return (scores[s * 128 : s * 128 + 128, t * 128 : t * 128 + 128] * decay).astype(BF16)

            vh = v[pl.ds(h * HEAD, HEAD), here]
            left = dot(vh[:, :128], block(0, 0, True))
            right = dot(vh, jnp.concatenate([block(0, 1, False), block(1, 1, True)], axis=0))
            out = skip[h] * vh.astype(F32) + own_weight[h : h + 1, :] * jnp.concatenate([left, right], axis=1)
            for cross, factor in crosses:
                out = out + factor[h : h + 1, :] * cross[at]
            ho[pl.ds(h * HEAD, HEAD), here] = out
        begin = begin + total
        previous = total


def finish_kernel(
    start, count, meta, docs, gain, w_out, sp, gates, ho, weight, e1, e23, e4, *refs
):
    sources = refs[:5]
    plus, minus, keep, own, acc, normed = refs[5:]
    ctx, tp = meta[0], meta[1]
    heads = e1.shape[0]
    for j in range(count):
        here = pl.ds((start + j) * STRETCH, STRETCH)
        stretch_doc = docs[ctx * STEPS + start + j]
        c_out = sp[here, STATE:]
        terms = []
        for bit in range(5):
            base = (ctx >> (bit + 1)) << (bit + 1)
            last_left = docs[(base + (1 << bit)) * STEPS - 1]
            live = ((((ctx >> bit) & 1) == 1) & (last_left == stretch_doc)).astype(F32)
            rows = weight[pl.ds((bit + 3) * heads, heads), here] * live
            if bit:
                gone = (None, e1[...], e23[pl.ds(0, heads), :], e23[pl.ds(heads, heads), :], e4[...])[bit]
                rows = rows * twice(jnp.exp(gone))
            terms.append((dot_nt(sources[bit][pl.ds(0, heads * HEAD), :], c_out), rows))
        for h in range(heads):
            at = pl.ds(h * HEAD, HEAD)
            total = ho[at, here]
            for cross, rows in terms:
                total = total + rows[h : h + 1, :] * cross[h * HEAD : (h + 1) * HEAD]
            g = gates[at, here].astype(F32)
            gated = total * (g / (1.0 + jnp.exp(-g)))
            power = jnp.sum(gated * gated, axis=0, keepdims=True) * (1.0 / HEAD)
            acc[at, :] = gated * lax.rsqrt(power + 1e-5)
        normed[pl.ds(j * STRETCH, STRETCH), :] = (jnp.transpose(acc[...]) * gain[...]).astype(BF16)
    quarter = w_out.shape[1] // 8

    def piece(shift, side):
        col = pl.multiple_of((((tp + shift) & 3) * 2 + side) * quarter, quarter)
        return dot(normed[...], w_out[:, pl.ds(col, quarter)]).astype(BF16)

    first, second = pl.ds(0, quarter), pl.ds(quarter, quarter)
    plus[:, first] = piece(2, 0)
    plus[:, second] = piece(1, 1)
    minus[:, first] = piece(2, 1)
    minus[:, second] = piece(3, 0)
    keep[:, first] = piece(1, 0)
    keep[:, second] = piece(3, 1)
    own[:, first] = piece(0, 0)
    own[:, second] = piece(0, 1)


def finish(start, stop, meta, docs, gain, w_out, *operands):
    count = stop - start
    width, depth = w_out.shape
    rows = count * STRETCH
    return call(
        functools.partial(finish_kernel, start, count),
        f"finish{start}",
        [SMEM] * 2 + [VMEM] * (2 + len(operands)),
        [((rows, depth // 4), BF16)] * 4,
        (meta, docs, gain, w_out, *operands),
        [pltpu.VMEM((width, STRETCH), F32), pltpu.VMEM((rows, width), BF16)],
        mib=16,
        flops=4 * rows * depth * width,
        moved=2 * width * depth + 8 * rows * width,
    )


def per_device(tokens, w_value, w_gate, w_state, w_level, log_decay, skip_weight, norm_gain, doc_ids, w_out):
    rows, depth = tokens.shape
    width = w_value.shape[1]
    heads = log_decay.shape[1]
    ctx, tp = lax.axis_index("ctx"), lax.axis_index("tp")
    meta = jnp.where(jnp.arange(2, dtype=jnp.int32) == 0, ctx, tp)
    decays = jnp.transpose(log_decay)
    payload = ((width + 3 * heads, STATE), BF16)
    tail = ((width, STATE), BF16)

    def across(x, by):
        return lax.ppermute(x, "ctx", [(i, i ^ by) for i in range(32)])

    def upward(x, by):
        return lax.ppermute(x, "ctx", [(i, i ^ by) for i in range(32) if i < i ^ by])

    def turn(x, by):
        return lax.ppermute(x, "tp", [(i, (i + by) % 4) for i in range(4)])

    tok, gate, sp, v, local, pay0 = project(meta, doc_ids, decays, tokens, w_value, w_state, w_gate)
    peer = across(pay0, 1)
    pay1, e1 = call(
        near_kernel, "near", [SMEM] * 2 + [VMEM] * 2, [payload, ((heads, STATE), F32)], (meta, doc_ids, pay0, peer)
    )
    ys = [across(pay1, by) for by in (4, 2, 6)]
    gates, weight, w_out_near = call(
        gate_kernel,
        "gate",
        [VMEM] * 3 + [FAR],
        [((width, rows), BF16), ((heads * LEVELS, rows), F32), (w_out.shape, BF16)],
        (tok, gate, w_level, far(w_out)),
        [pltpu.SemaphoreType.DMA(())],
        mib=12,
        flops=2 * rows * depth * (width + STATE),
        moved=2 * (rows * depth + depth * width),
    )
    y2, y1, y3 = ys
    pay2, left2, e23 = call(
        middle_kernel,
        "middle",
        [SMEM] * 2 + [VMEM] * 5,
        [payload, tail, ((2 * heads, STATE), F32)],
        (meta, doc_ids, pay1, y1, y2, y3, e1),
    )
    x2, x1, x3 = (upward(pay2, by) for by in (16, 8, 24))
    ho, scaled_weight = call(
        intra_kernel,
        "intra",
        [SMEM] * 3 + [VMEM] * 5,
        [((width, rows), F32), ((heads * LEVELS, rows), F32)],
        (meta, doc_ids, skip_weight, weight, decays, v, sp, local),
        mib=12,
        flops=6 << 30,
        moved=8 << 20,
    )
    left4, e4 = call(
        far_kernel,
        "far",
        [SMEM] * 2 + [VMEM] * 4,
        [tail, ((heads, STATE), F32)],
        (meta, doc_ids, x1, x2, x3, e23),
    )
    gain = norm_gain.reshape(1, -1)
    results = []
    half = w_out.shape[1] // 8
    for lo, hi in CHUNKS:
        plus, minus, keep, own = finish(
            lo, hi, meta, doc_ids, gain, w_out_near, sp, gates, ho, scaled_weight, e1, e23, e4, peer, y1, left2, x1, left4
        )
        from_below, from_above = turn(plus, 1), turn(minus, 3)
        on_plus = (keep[:, :half].astype(F32) + from_below[:, :half].astype(F32)).astype(BF16)
        on_minus = (keep[:, half:].astype(F32) + from_above[:, :half].astype(F32)).astype(BF16)
        last_below, last_above = turn(on_plus, 1), turn(on_minus, 3)
        first = own[:, :half].astype(F32) + from_above[:, half:].astype(F32) + last_below.astype(F32)
        second = own[:, half:].astype(F32) + from_below[:, half:].astype(F32) + last_above.astype(F32)
        results.append(jnp.concatenate([first, second], axis=1).astype(BF16))
    return jnp.concatenate(results, axis=0)


def solution(mesh):
    placed = (
        P("ctx", None),
        P(None, "tp"),
        P(None, "tp"),
        P(),
        P(None, "tp"),
        P("ctx", "tp"),
        P("tp"),
        P("tp"),
        P(),
        P("tp", None),
    )
    return jax.shard_map(per_device, mesh=mesh, in_specs=placed, out_specs=P("ctx", "tp"), check_vma=False)
```

profile of v0, /device:TPU:0, one launch (start us, length us, event | category | flops | bytes accessed | tf_op | source)
XLA Modules:
  0.0 97.8 jit_solution(4288455772302409885)
XLA Ops:
  0.7 0.8 copy-done.3
  1.5 12.8 %project.1 = (bf16[1024,2048]{1,0:T(8,128)(2,1)S(1)}, bf16[2048,1024]{1,0:T(8,128)(2,1)S(1)}, bf16[1024,256]{1,0:T(8,128)(2,1)S(1)}, bf16[1024,1024]{1,0:T(8,128...) custom-call(s32[2]{0:T(128)S(1)} %compare_select_fusion.meta, s32[128]{0:T(128)S(1)} %copy-done, ...), custom_call_target="tpu_custom_call" | custom-call | flops 5368709120 | bytes 12582912 | tf_op jit(solution)/shard_map/project/pallas_call | solution.py:76
  14.4 1.5 %collective-permute-done.peer.refs_0_ = bf16[1072,128]{1,0:T(8,128)(2,1)S(1)} collective-permute-done((bf16[1072,128]{1,0:T(8,128)(2,1)S(1)}, bf16[1072,128]{1,0:T(8,128)(2,1)S(1)}, u32[]{:S(2)}, u32[]{:S(2)}) %collective-permute-start) | collective-permute-done | bytes 274464 | tf_op jit(solution)/shard_map/ppermute | solution.py:428
  16.6 3.2 %collective-permute-start.3 = (bf16[1072,128]{1,0:T(8,128)(2,1)S(1)}, bf16[1072,128]{1,0:T(8,128)(2,1)S(1)}, u32[]{:S(2)}, u32[]{:S(2)}) collective-permute-start(bf16[1072,128]{1,0:T(8,128)(2,1)S(1)} %get-tuple-element.43.own), channel_id=1, source_target_pairs={{0,24},{4,28},{8,16},{12,20},{16,8},{20,12},{24,0},{28,4},{32,56},... | collective-permute-start | bytes 823304 | tf_op jit(solution)/shard_map/ppermute | solution.py:428
  20.8 6.9 %gate.1 = (bf16[1024,1024]{1,0:T(8,128)(2,1)S(1)}, f32[128,1024]{1,0:T(8,128)S(1)}, bf16[1024,2048]{1,0:T(8,128)(2,1)S(1)}) custom-call(bf16[1024,2048]{1,0:T(8,128)(2,1)S(1)} %get-tuple-element.31.tok, bf16[2048,1024]{1,0:T(8,128)(2,1)S(1)} %get-tuple-element.32.gate, bf16[2048,128]{1,0:T(8,128)(2,1)S(1)} %copy-done.2, bf16[1024,2048]{1,0:T(8,128)(2,1)} %out_hbm.1), custom_call_target="tpu_custom_call" | custom-call | flops 4831838208 | bytes 8388608 | tf_op jit(solution)/shard_map/gate/pallas_call | solution.py:76
  27.7 4.8 %collective-permute-done.3.three = bf16[1072,128]{1,0:T(8,128)(2,1)S(1)} collective-permute-done((bf16[1072,128]{1,0:T(8,128)(2,1)S(1)}, bf16[1072,128]{1,0:T(8,128)(2,1)S(1)}, u32[]{:S(2)}, u32[]{:S(2)}) %collective-permute-start.3) | collective-permute-done | bytes 274464 | tf_op jit(solution)/shard_map/ppermute | solution.py:428
  34.1 4.7 %collective-permute-start.6 = (bf16[1072,128]{1,0:T(8,128)(2,1)S(1)}, bf16[1072,128]{1,0:T(8,128)(2,1)S(1)}, u32[]{:S(2)}, u32[]{:S(2)}) collective-permute-start(bf16[1072,128]{1,0:T(8,128)(2,1)S(1)} %get-tuple-element.45), channel_id=1, source_target_pairs={{0,96},{4,100},{8,104},{12,108},{16,112},{20,116},{24,120},{28,124... | collective-permute-start | bytes 823304 | tf_op jit(solution)/shard_map/ppermute | solution.py:431
  38.8 1.6 %collective-permute-start.5 = (bf16[1072,128]{1,0:T(8,128)(2,1)S(1)}, bf16[1072,128]{1,0:T(8,128)(2,1)S(1)}, u32[]{:S(2)}, u32[]{:S(2)}) collective-permute-start(bf16[1072,128]{1,0:T(8,128)(2,1)S(1)} %get-tuple-element.45), channel_id=1, source_target_pairs={{0,64},{4,68},{8,72},{12,76},{16,80},{20,84},{24,88},{28,92},{32,9... | collective-permute-start | bytes 823304 | tf_op jit(solution)/shard_map/ppermute | solution.py:431
  40.3 2.7 %collective-permute-start.4 = (bf16[1072,128]{1,0:T(8,128)(2,1)S(1)}, bf16[1072,128]{1,0:T(8,128)(2,1)S(1)}, u32[]{:S(2)}, u32[]{:S(2)}) collective-permute-start(bf16[1072,128]{1,0:T(8,128)(2,1)S(1)} %get-tuple-element.45), channel_id=1, source_target_pairs={{0,32},{4,36},{8,40},{12,44},{16,48},{20,52},{24,56},{28,60},{64,9... | collective-permute-start | bytes 823304 | tf_op jit(solution)/shard_map/ppermute | solution.py:431
  43.1 6.3 %intra.1 = (f32[1024,1024]{1,0:T(8,128)S(1)}, f32[128,1024]{1,0:T(8,128)S(1)}) custom-call(s32[2]{0:T(128)S(1)} %compare_select_fusion.meta, s32[128]{0:T(128)S(1)} %copy-done.1, f32[16]{0:T(128)S(1)} %copy-done.6, f32[128,1024]{1,0:T(8,128)S(1)} %get-tuple-element.36.weight, f32[16,1024]{1,0:T(8,128)S(1)} %bitcast.3, ...), custom_call_target="tpu_custom_call" | custom-call | flops 6442450944 | bytes 8388608 | tf_op jit(solution)/shard_map/intra/pallas_call | solution.py:76
  49.8 1.6 %collective-permute-done.4.one.refs_3_ = bf16[1072,128]{1,0:T(8,128)(2,1)S(1)} collective-permute-done((bf16[1072,128]{1,0:T(8,128)(2,1)S(1)}, bf16[1072,128]{1,0:T(8,128)(2,1)S(1)}, u32[]{:S(2)}, u32[]{:S(2)}) %collective-permute-start.4) | collective-permute-done | bytes 274464 | tf_op jit(solution)/shard_map/ppermute | solution.py:431
  52.1 4.8 %finish2.1 = (bf16[512,512]{1,0:T(8,128)(2,1)S(1)}, bf16[512,512]{1,0:T(8,128)(2,1)S(1)}, bf16[512,512]{1,0:T(8,128)(2,1)S(1)}, bf16[512,512]{1,0:T(8,128)(2,1)S(1)}) custom-call(s32[2]{0:T(128)S(1)} %compare_select_fusion.meta, s32[128]{0:T(128)S(1)} %copy-done.1, f32[1,1024]{1,0:T(1,128)S(1)} %bitcast.4, bf16[1024,2048]{1,0:T(8,128)(2,1)S(1)} %get-tuple-element.33.w_out, ...), custom_call_target="tpu_custom_call" | custom-call | flops 4294967296 | bytes 8388608 | tf_op jit(solution)/shard_map/finish2/pallas_call | solution.py:76
  56.9 4.1 %collective-permute-start.11 = (bf16[512,512]{1,0:T(8,128)(2,1)S(1)}, bf16[512,512]{1,0:T(8,128)(2,1)S(1)}, u32[]{:S(2)}, u32[]{:S(2)}) collective-permute-start(bf16[512,512]{1,0:T(8,128)(2,1)S(1)} %get-tuple-element.54), channel_id=1, source_target_pairs={{0,3},{1,0},{2,1},{3,2},{4,7},{5,4},{6,5},{7,6},{8,11},{9,8},{10,9... | collective-permute-start | bytes 1572872 | tf_op jit(solution)/shard_map/ppermute | solution.py:434
  61.0 4.8 %finish0.1 = (bf16[512,512]{1,0:T(8,128)(2,1)S(1)}, bf16[512,512]{1,0:T(8,128)(2,1)S(1)}, bf16[512,512]{1,0:T(8,128)(2,1)S(1)}, bf16[512,512]{1,0:T(8,128)(2,1)S(1)}) custom-call(s32[2]{0:T(128)S(1)} %compare_select_fusion.meta, s32[128]{0:T(128)S(1)} %copy-done.1, f32[1,1024]{1,0:T(1,128)S(1)} %bitcast.5, bf16[1024,2048]{1,0:T(8,128)(2,1)S(1)} %get-tuple-element.33.w_out, ...), custom_call_target="tpu_custom_call" | custom-call | flops 4294967296 | bytes 8388608 | tf_op jit(solution)/shard_map/finish0/pallas_call | solution.py:76
  65.9 3.3 %collective-permute-start.7 = (bf16[512,512]{1,0:T(8,128)(2,1)S(1)}, bf16[512,512]{1,0:T(8,128)(2,1)S(1)}, u32[]{:S(2)}, u32[]{:S(2)}) collective-permute-start(bf16[512,512]{1,0:T(8,128)(2,1)S(1)} %get-tuple-element.50), channel_id=1, source_target_pairs={{0,3},{1,0},{2,1},{3,2},{4,7},{5,4},{6,5},{7,6},{8,11},{9,8},{10,9... | collective-permute-start | bytes 1572872 | tf_op jit(solution)/shard_map/ppermute | solution.py:434
  69.2 4.2 %collective-permute-done.11 = bf16[512,512]{1,0:T(8,128)(2,1)S(1)} collective-permute-done((bf16[512,512]{1,0:T(8,128)(2,1)S(1)}, bf16[512,512]{1,0:T(8,128)(2,1)S(1)}, u32[]{:S(2)}, u32[]{:S(2)}) %collective-permute-start.11) | collective-permute-done | bytes 524320 | tf_op jit(solution)/shard_map/ppermute | solution.py:434
  73.4 3.7 %collective-permute-done.12 = bf16[512,512]{1,0:T(8,128)(2,1)S(1)} collective-permute-done((bf16[512,512]{1,0:T(8,128)(2,1)S(1)}, bf16[512,512]{1,0:T(8,128)(2,1)S(1)}, u32[]{:S(2)}, u32[]{:S(2)}) %collective-permute-start.12) | collective-permute-done | bytes 524320 | tf_op jit(solution)/shard_map/ppermute | solution.py:434
  77.3 3.2 %collective-permute-start.14 = (bf16[512,256]{1,0:T(8,128)(2,1)S(1)}, bf16[512,256]{1,0:T(8,128)(2,1)S(1)}, u32[]{:S(2)}, u32[]{:S(2)}) collective-permute-start(bf16[512,256]{1,0:T(8,128)(2,1)S(1)} %get-tuple-element.64), channel_id=1, source_target_pairs={{0,3},{1,0},{2,1},{3,2},{4,7},{5,4},{6,5},{7,6},{8,11},{9,8},{10,9... | collective-permute-start | bytes 786440 | tf_op jit(solution)/shard_map/ppermute | solution.py:434
  80.5 4.1 %collective-permute-done.7 = bf16[512,512]{1,0:T(8,128)(2,1)S(1)} collective-permute-done((bf16[512,512]{1,0:T(8,128)(2,1)S(1)}, bf16[512,512]{1,0:T(8,128)(2,1)S(1)}, u32[]{:S(2)}, u32[]{:S(2)}) %collective-permute-start.7) | collective-permute-done | bytes 524320 | tf_op jit(solution)/shard_map/ppermute | solution.py:434
  84.6 3.7 %collective-permute-done.8 = bf16[512,512]{1,0:T(8,128)(2,1)S(1)} collective-permute-done((bf16[512,512]{1,0:T(8,128)(2,1)S(1)}, bf16[512,512]{1,0:T(8,128)(2,1)S(1)}, u32[]{:S(2)}, u32[]{:S(2)}) %collective-permute-start.8) | collective-permute-done | bytes 524320 | tf_op jit(solution)/shard_map/ppermute | solution.py:434
  88.6 3.2 %collective-permute-start.10 = (bf16[512,256]{1,0:T(8,128)(2,1)S(1)}, bf16[512,256]{1,0:T(8,128)(2,1)S(1)}, u32[]{:S(2)}, u32[]{:S(2)}) collective-permute-start(bf16[512,256]{1,0:T(8,128)(2,1)S(1)} %get-tuple-element.60), channel_id=1, source_target_pairs={{0,3},{1,0},{2,1},{3,2},{4,7},{5,4},{6,5},{7,6},{8,11},{9,8},{10,9... | collective-permute-start | bytes 786440 | tf_op jit(solution)/shard_map/ppermute | solution.py:434
  91.8 1.9 %collective-permute-done.13 = bf16[512,256]{1,0:T(8,128)(2,1)S(1)} collective-permute-done((bf16[512,256]{1,0:T(8,128)(2,1)S(1)}, bf16[512,256]{1,0:T(8,128)(2,1)S(1)}, u32[]{:S(2)}, u32[]{:S(2)}) %collective-permute-start.13) | collective-permute-done | bytes 262176 | tf_op jit(solution)/shard_map/ppermute | solution.py:434
  93.9 2.6 %collective-permute-done.9 = bf16[512,256]{1,0:T(8,128)(2,1)S(1)} collective-permute-done((bf16[512,256]{1,0:T(8,128)(2,1)S(1)}, bf16[512,256]{1,0:T(8,128)(2,1)S(1)}, u32[]{:S(2)}, u32[]{:S(2)}) %collective-permute-start.9) | collective-permute-done | bytes 262176 | tf_op jit(solution)/shard_map/ppermute | solution.py:434
  96.7 1.1 %maximum_maximum_fusion = bf16[1024,512]{1,0:T(8,128)(2,1)} fusion(bf16[512,256]{1,0:T(8,128)(2,1)S(1)} %get-tuple-element.62, bf16[512,256]{1,0:T(8,128)(2,1)S(1)} %get-tuple-element.61, bf16[512,256]{1,0:T(8,128)(2,1)S(1)} %get-tuple-element.58, bf16[512,256]{1,0:T(8,128)(2,1)S(1)} %get-tuple-element.57), kind=kLoop, calls=%fused_computation | loop fusion | flops 4194304 | bytes 2097152 | tf_op jit(solution)/shard_map/concatenate | solution.py:493
  (34 shorter events, 5.9 us)
Async XLA Ops:
  0.0 0.7 copy-start
  0.7 0.8 copy-start.3
  1.5 19.3 %copy-start.2 = (bf16[2048,128]{1,0:T(8,128)(2,1)S(1)}, bf16[2048,128]{1,0:T(8,128)(2,1)}, u32[]{:S(2)}) copy-start(bf16[2048,128]{1,0:T(8,128)(2,1)} %w_level.1) | copy-start | bytes 1572868
  14.3 1.6 %collective-permute-start = (bf16[1072,128]{1,0:T(8,128)(2,1)S(1)}, bf16[1072,128]{1,0:T(8,128)(2,1)S(1)}, u32[]{:S(2)}, u32[]{:S(2)}) collective-permute-start(bf16[1072,128]{1,0:T(8,128)(2,1)S(1)} %get-tuple-element.41.own), channel_id=1, source_target_pairs={{0,4},{4,0},{8,12},{12,8},{16,20},{20,16},{24,28},{28,24},{32,36},... | collective-permute-start | bytes 823304 | tf_op jit(solution)/shard_map/ppermute | solution.py:428
  16.6 15.9 %collective-permute-start.3 = (bf16[1072,128]{1,0:T(8,128)(2,1)S(1)}, bf16[1072,128]{1,0:T(8,128)(2,1)S(1)}, u32[]{:S(2)}, u32[]{:S(2)}) collective-permute-start(bf16[1072,128]{1,0:T(8,128)(2,1)S(1)} %get-tuple-element.43.own), channel_id=1, source_target_pairs={{0,24},{4,28},{8,16},{12,20},{16,8},{20,12},{24,0},{28,4},{32,56},... | collective-permute-start | bytes 823304 | tf_op jit(solution)/shard_map/ppermute | solution.py:428
  19.8 12.8 %collective-permute-start.2 = (bf16[1072,128]{1,0:T(8,128)(2,1)S(1)}, bf16[1072,128]{1,0:T(8,128)(2,1)S(1)}, u32[]{:S(2)}, u32[]{:S(2)}) collective-permute-start(bf16[1072,128]{1,0:T(8,128)(2,1)S(1)} %get-tuple-element.43.own), channel_id=1, source_target_pairs={{0,16},{4,20},{8,24},{12,28},{16,0},{20,4},{24,8},{28,12},{32,48},... | collective-permute-start | bytes 823304 | tf_op jit(solution)/shard_map/ppermute | solution.py:428
  20.4 12.8 %collective-permute-start.1 = (bf16[1072,128]{1,0:T(8,128)(2,1)S(1)}, bf16[1072,128]{1,0:T(8,128)(2,1)S(1)}, u32[]{:S(2)}, u32[]{:S(2)}) collective-permute-start(bf16[1072,128]{1,0:T(8,128)(2,1)S(1)} %get-tuple-element.43.own), channel_id=1, source_target_pairs={{0,8},{4,12},{8,0},{12,4},{16,24},{20,28},{24,16},{28,20},{32,40},... | collective-permute-start | bytes 823304 | tf_op jit(solution)/shard_map/ppermute | solution.py:428
  20.8 12.5 %copy-start.1 = (s32[128]{0:T(128)S(1)}, s32[128]{0:T(128)}, u32[]{:S(2)}) copy-start(s32[128]{0:T(128)} %docs.13) | copy-start | bytes 1540
  20.8 22.3 %copy-start.4 = (f32[1024,16]{0,1:T(8,128)S(1)}, f32[1024,16]{0,1:T(8,128)}, u32[]{:S(2)}) copy-start(f32[1024,16]{0,1:T(8,128)} %param.15) | copy-start | bytes 196612
  20.8 22.3 %copy-start.6 = (f32[16]{0:T(128)S(1)}, f32[16]{0:T(128)}, u32[]{:S(2)}) copy-start(f32[16]{0:T(128)} %skip.1) | copy-start | bytes 196
  34.1 15.7 %collective-permute-start.6 = (bf16[1072,128]{1,0:T(8,128)(2,1)S(1)}, bf16[1072,128]{1,0:T(8,128)(2,1)S(1)}, u32[]{:S(2)}, u32[]{:S(2)}) collective-permute-start(bf16[1072,128]{1,0:T(8,128)(2,1)S(1)} %get-tuple-element.45), channel_id=1, source_target_pairs={{0,96},{4,100},{8,104},{12,108},{16,112},{20,116},{24,120},{28,124... | collective-permute-start | bytes 823304 | tf_op jit(solution)/shard_map/ppermute | solution.py:431
  38.8 11.0 %collective-permute-start.5 = (bf16[1072,128]{1,0:T(8,128)(2,1)S(1)}, bf16[1072,128]{1,0:T(8,128)(2,1)S(1)}, u32[]{:S(2)}, u32[]{:S(2)}) collective-permute-start(bf16[1072,128]{1,0:T(8,128)(2,1)S(1)} %get-tuple-element.45), channel_id=1, source_target_pairs={{0,64},{4,68},{8,72},{12,76},{16,80},{20,84},{24,88},{28,92},{32,9... | collective-permute-start | bytes 823304 | tf_op jit(solution)/shard_map/ppermute | solution.py:431
  40.3 11.0 %collective-permute-start.4 = (bf16[1072,128]{1,0:T(8,128)(2,1)S(1)}, bf16[1072,128]{1,0:T(8,128)(2,1)S(1)}, u32[]{:S(2)}, u32[]{:S(2)}) collective-permute-start(bf16[1072,128]{1,0:T(8,128)(2,1)S(1)} %get-tuple-element.45), channel_id=1, source_target_pairs={{0,32},{4,36},{8,40},{12,44},{16,48},{20,52},{24,56},{28,60},{64,9... | collective-permute-start | bytes 823304 | tf_op jit(solution)/shard_map/ppermute | solution.py:431
  43.0 9.0 %copy-start.5 = (f32[1024]{0:T(1024)S(1)}, f32[1024]{0:T(1024)}, u32[]{:S(2)}) copy-start(f32[1024]{0:T(1024)} %param.17) | copy-start | bytes 12292
  56.9 16.5 %collective-permute-start.11 = (bf16[512,512]{1,0:T(8,128)(2,1)S(1)}, bf16[512,512]{1,0:T(8,128)(2,1)S(1)}, u32[]{:S(2)}, u32[]{:S(2)}) collective-permute-start(bf16[512,512]{1,0:T(8,128)(2,1)S(1)} %get-tuple-element.54), channel_id=1, source_target_pairs={{0,3},{1,0},{2,1},{3,2},{4,7},{5,4},{6,5},{7,6},{8,11},{9,8},{10,9... | collective-permute-start | bytes 1572872 | tf_op jit(solution)/shard_map/ppermute | solution.py:434
  61.0 16.1 %collective-permute-start.12 = (bf16[512,512]{1,0:T(8,128)(2,1)S(1)}, bf16[512,512]{1,0:T(8,128)(2,1)S(1)}, u32[]{:S(2)}, u32[]{:S(2)}) collective-permute-start(bf16[512,512]{1,0:T(8,128)(2,1)S(1)} %get-tuple-element.56), channel_id=1, source_target_pairs={{0,1},{1,2},{2,3},{3,0},{4,5},{5,6},{6,7},{7,4},{8,9},{9,10},{10,1... | collective-permute-start | bytes 1572872 | tf_op jit(solution)/shard_map/ppermute | solution.py:434
  65.9 18.8 %collective-permute-start.7 = (bf16[512,512]{1,0:T(8,128)(2,1)S(1)}, bf16[512,512]{1,0:T(8,128)(2,1)S(1)}, u32[]{:S(2)}, u32[]{:S(2)}) collective-permute-start(bf16[512,512]{1,0:T(8,128)(2,1)S(1)} %get-tuple-element.50), channel_id=1, source_target_pairs={{0,3},{1,0},{2,1},{3,2},{4,7},{5,4},{6,5},{7,6},{8,11},{9,8},{10,9... | collective-permute-start | bytes 1572872 | tf_op jit(solution)/shard_map/ppermute | solution.py:434
  69.2 19.2 %collective-permute-start.8 = (bf16[512,512]{1,0:T(8,128)(2,1)S(1)}, bf16[512,512]{1,0:T(8,128)(2,1)S(1)}, u32[]{:S(2)}, u32[]{:S(2)}) collective-permute-start(bf16[512,512]{1,0:T(8,128)(2,1)S(1)} %get-tuple-element.52), channel_id=1, source_target_pairs={{0,1},{1,2},{2,3},{3,0},{4,5},{5,6},{6,7},{7,4},{8,9},{9,10},{10,1... | collective-permute-start | bytes 1572872 | tf_op jit(solution)/shard_map/ppermute | solution.py:434
  77.2 16.5 %collective-permute-start.13 = (bf16[512,256]{1,0:T(8,128)(2,1)S(1)}, bf16[512,256]{1,0:T(8,128)(2,1)S(1)}, u32[]{:S(2)}, u32[]{:S(2)}) collective-permute-start(bf16[512,256]{1,0:T(8,128)(2,1)S(1)} %get-tuple-element.63), channel_id=1, source_target_pairs={{0,1},{1,2},{2,3},{3,0},{4,5},{5,6},{6,7},{7,4},{8,9},{9,10},{10,1... | collective-permute-start | bytes 786440 | tf_op jit(solution)/shard_map/ppermute | solution.py:434
  77.3 16.4 %collective-permute-start.14 = (bf16[512,256]{1,0:T(8,128)(2,1)S(1)}, bf16[512,256]{1,0:T(8,128)(2,1)S(1)}, u32[]{:S(2)}, u32[]{:S(2)}) collective-permute-start(bf16[512,256]{1,0:T(8,128)(2,1)S(1)} %get-tuple-element.64), channel_id=1, source_target_pairs={{0,3},{1,0},{2,1},{3,2},{4,7},{5,4},{6,5},{7,6},{8,11},{9,8},{10,9... | collective-permute-start | bytes 786440 | tf_op jit(solution)/shard_map/ppermute | solution.py:434
  88.5 8.1 %collective-permute-start.9 = (bf16[512,256]{1,0:T(8,128)(2,1)S(1)}, bf16[512,256]{1,0:T(8,128)(2,1)S(1)}, u32[]{:S(2)}, u32[]{:S(2)}) collective-permute-start(bf16[512,256]{1,0:T(8,128)(2,1)S(1)} %get-tuple-element.59), channel_id=1, source_target_pairs={{0,1},{1,2},{2,3},{3,0},{4,5},{5,6},{6,7},{7,4},{8,9},{9,10},{10,1... | collective-permute-start | bytes 786440 | tf_op jit(solution)/shard_map/ppermute | solution.py:434
  88.6 8.0 %collective-permute-start.10 = (bf16[512,256]{1,0:T(8,128)(2,1)S(1)}, bf16[512,256]{1,0:T(8,128)(2,1)S(1)}, u32[]{:S(2)}, u32[]{:S(2)}) collective-permute-start(bf16[512,256]{1,0:T(8,128)(2,1)S(1)} %get-tuple-element.60), channel_id=1, source_target_pairs={{0,3},{1,0},{2,1},{3,2},{4,7},{5,4},{6,5},{7,6},{8,11},{9,8},{10,9... | collective-permute-start | bytes 786440 | tf_op jit(solution)/shard_map/ppermute | solution.py:434
where the time goes:
time: 98.9 us; the launch traced here: 97.8 us
  Pallas kernels  37.8 us (38%)
  waiting for transfers between devices  29.4 us (30%)
  starting transfers between devices  27.2 us (28%)
  other arithmetic  1.7 us (2%)
  local copies, waits for them, and re-layouts  1.51 us (2%)
    pallas_call x8, Pallas kernels, call(): pl.pallas_call(kernel, name=name, in_specs=in_specs, out_specs=[VMEM] * l...  37.8 us
    ppermute x8, waiting for transfers between devices, turn(): return lax.ppermute(x, 'tp', [(i, (i + by) % 4) for i in range(4)])  20.3 us
    ppermute x8, starting transfers between devices, turn(): return lax.ppermute(x, 'tp', [(i, (i + by) % 4) for i in range(4)])  14 us
    ppermute x3, starting transfers between devices, upward(): lax.ppermute(x, 'ctx', [(i, i ^ by) for i in range(32) if i < i ^ by])  8.93 us
    ppermute x4, waiting for transfers between devices, across(): return lax.ppermute(x, 'ctx', [(i, i ^ by) for i in range(32)])  7.08 us
    ppermute x4, starting transfers between devices, across(): return lax.ppermute(x, 'ctx', [(i, i ^ by) for i in range(32)])  4.26 us
    ppermute x3, waiting for transfers between devices, upward(): lax.ppermute(x, 'ctx', [(i, i ^ by) for i in range(32) if i < i ^ by])  2.03 us
  transfers between devices with their start and end apart: 15, of which 11 were waited for; matrix products, arithmetic and copies ran while one was open for 0% of the time, Pallas kernels for 18%

commit v1 on v0

--- a/solution.py
+++ b/solution.py
@@ -86,8 +86,8 @@
 
 
 def project_kernel(
-    meta, docs, decays, tok_hbm, value_hbm, state_hbm, gate_hbm, tok, gate, sp, v, local, pay, w_value, w_state, tail,
-    grow, scaled, sems,
+    docs, decays_hbm, tok_hbm, value_hbm, state_hbm, tok, sp, v, local, pay, w_value, w_state, tail, grow, scaled, decays,
+    sems,
 ):
     heads = decays.shape[0]
     blocks = w_value.shape[1] // BLOCK
@@ -98,22 +98,25 @@
         return pltpu.make_async_copy(tok_hbm.at[at, :], tok.at[at, :], sems.at[i])
 
     def value_copy(k):
-        at = pl.ds(pl.multiple_of(k * BLOCK, BLOCK), BLOCK)
+        at = pl.ds(k * BLOCK, BLOCK)
         return pltpu.make_async_copy(value_hbm.at[:, at], w_value.at[:, at], sems.at[STEPS + k])
 
     state_copy = pltpu.make_async_copy(state_hbm, w_state, sems.at[STEPS + blocks])
-    gate_copy = pltpu.make_async_copy(gate_hbm, gate, sems.at[STEPS + blocks + 1])
+    decay_copy = pltpu.make_async_copy(decays_hbm, decays, sems.at[STEPS + blocks + 1])
+    decay_copy.start()
     token_copy(0).start()
     state_copy.start()
+    value_copy(0).start()
     for i in range(1, STEPS):
         token_copy(i).start()
-    value_copy(0).start()
-
-    stacked = jnp.concatenate([decays[:, i * STRETCH : (i + 1) * STRETCH] for i in range(STEPS)], axis=0)
+    value_copy(1).start()
+
+    decay_copy.wait()
+    stacked = jnp.concatenate([decays[:, pl.ds(i * STRETCH, STRETCH)] for i in range(STEPS)], axis=0)
     cum = running_sums(stacked)
     total = lanes(cum[:, STRETCH - 1 :])
     rest = jnp.exp(twice(total) - cum)
-    first = meta[0] * STEPS
+    first = lax.axis_index("ctx") * STEPS
     whole = jnp.zeros((heads, STATE), F32)
     for i in range(STEPS):
         rows = slice(i * heads, (i + 1) * heads)
@@ -123,42 +126,23 @@
         whole = whole + total[rows]
     store_total(pay, heads * HEAD, whole)
 
-    state_copy.wait()
-    for i in range(STEPS):
-        token_copy(i).wait()
-        at = pl.ds(i * STRETCH, STRETCH)
-        sp[at, :] = dot(tok[at, :], w_state[...]).astype(BF16)
-
-    @pl.loop(0, blocks)
-    def _(k):
-        value_copy(k).wait()
-
-        @pl.when(k + 1 < blocks)
-        def _():
-            value_copy(k + 1).start()
-
-        @pl.when(k == 1)
-        def _():
-            gate_copy.start()
-
-        at = pl.ds(pl.multiple_of(k * BLOCK, BLOCK), BLOCK)
-        v[at, :] = jnp.transpose(dot(tok[...], w_value[:, at]).astype(BF16))
+    def states(k):
+        at = pl.ds(k * BLOCK, BLOCK)
         for h in range(per_block):
-            rows = pl.ds(pl.multiple_of(k * BLOCK + h * HEAD, HEAD), HEAD)
-            scaled[pl.ds(h * HEAD, HEAD), :] = (
-                v[rows, :].astype(F32) * tail[pl.ds(k * per_block + h, 1), :]
-            ).astype(BF16)
+            rows = pl.ds(k * BLOCK + h * HEAD, HEAD)
+            row = k * per_block + h
+            scaled[rows, :] = (v[rows, :].astype(F32) * tail[row : row + 1, :]).astype(BF16)
         run = None
         for i in range(STEPS):
             here = pl.ds(i * STRETCH, STRETCH)
-            state = dot(scaled[:, here], sp[here, :STATE])
+            state = dot(scaled[at, here], sp[here, :STATE])
             if i == 0:
                 run = state
                 local[0, at, :] = state.astype(BF16)
                 continue
             factor = jnp.concatenate(
                 [
-                    jnp.broadcast_to(grow[i, pl.ds(k * per_block + h, 1), :], (HEAD, STATE))
+                    jnp.broadcast_to(grow[i, k * per_block + h : k * per_block + h + 1, :], (HEAD, STATE))
                     for h in range(per_block)
                 ],
                 axis=0,
@@ -170,37 +154,57 @@
                 local[2, at, :] = state.astype(BF16)
         pay[at, :] = run.astype(BF16)
 
-    gate_copy.wait()
-
-
-def project(meta, docs, decays, tokens, w_value, w_state, w_gate):
+    for k in range(blocks):
+        at = pl.ds(k * BLOCK, BLOCK)
+        if k:
+            value_copy(k).wait()
+            v[at, :] = jnp.transpose(dot(tok[...], w_value[:, at]).astype(BF16))
+            states(k - 1)
+        else:
+            for i in range(STEPS):
+                here = pl.ds(i * STRETCH, STRETCH)
+                token_copy(i).wait()
+                if i == 0:
+                    state_copy.wait()
+                sp[here, :] = dot(tok[here, :], w_state[...]).astype(BF16)
+                if i == 0:
+                    value_copy(0).wait()
+                if i == 1:
+                    value_copy(2).start()
+                if i == 2:
+                    value_copy(3).start()
+                v[at, here] = jnp.transpose(dot(tok[here, :], w_value[:, at]).astype(BF16))
+    states(blocks - 1)
+
+
+def project(docs, decays, tokens, w_value, w_state):
     rows, depth = tokens.shape
     heads = decays.shape[0]
     width = w_value.shape[1]
     return call(
         project_kernel,
         "project",
-        [SMEM, SMEM, VMEM, FAR, FAR, FAR, FAR],
+        [SMEM, FAR, FAR, FAR, FAR],
         [
             ((rows, depth), BF16),
-            ((depth, width), BF16),
             ((rows, 2 * STATE), BF16),
             ((width, rows), BF16),
             ((3, width, STATE), BF16),
             ((width + 3 * heads, STATE), BF16),
         ],
-        (meta, docs, decays, *(far(x) for x in (tokens, w_value, w_state, w_gate))),
+        (docs, *(far(x) for x in (decays, tokens, w_value, w_state))),
         [
             pltpu.VMEM((depth, width), BF16),
             pltpu.VMEM((depth, 2 * STATE), BF16),
             pltpu.VMEM((heads, rows), F32),
             pltpu.VMEM((STEPS, heads, STATE), F32),
-            pltpu.VMEM((BLOCK, rows), BF16),
+            pltpu.VMEM((width, rows), BF16),
+            pltpu.VMEM((heads, rows), F32),
             pltpu.SemaphoreType.DMA((STEPS + width // BLOCK + 2,)),
         ],
         mib=16,
         flops=2 * rows * depth * (width + 2 * STATE),
-        moved=2 * (rows * depth + 2 * depth * width),
+        moved=2 * (rows * depth + depth * width),
     )
 
 
@@ -208,31 +212,37 @@
     return (docs[last_first] == docs[last_second]).astype(F32)
 
 
-def near_kernel(meta, docs, own, peer, pay, earlier):
+def half_rows(core, *factors):
+    half = factors[0].shape[0] // 2
+    return [jnp.where(core == 0, x[:half], x[half:]) for x in factors]
+
+
+def near_kernel(docs, own, peer, pay, earlier):
     heads = earlier.shape[0]
-    top = heads * HEAD
-    ctx = meta[0]
-    second = (ctx & 1) == 1
-    pair = ctx >> 1
-    total_own, total_peer = load_total(own, top, heads), load_total(peer, top, heads)
+    half = heads // 2
+    ctx = lax.axis_index("ctx")
+    core, pair = ctx & 1, ctx >> 1
+    second = core == 1
+    total_own, total_peer = load_total(own, heads * HEAD, heads), load_total(peer, heads * HEAD, heads)
     keep = joined(docs, pair * 2 * STEPS + STEPS - 1, pair * 2 * STEPS + 2 * STEPS - 1)
     factor = jnp.exp(jnp.where(second, total_own, total_peer)) * keep
-    own_by = jnp.where(second, 1.0, factor)
-    peer_by = jnp.where(second, factor, 1.0)
-    for h in range(heads):
-        at = pl.ds(h * HEAD, HEAD)
-        pay[at, :] = (own[at, :].astype(F32) * own_by[h : h + 1] + peer[at, :].astype(F32) * peer_by[h : h + 1]).astype(
-            BF16
-        )
-    store_total(pay, top, total_own + total_peer)
+    own_by, peer_by = half_rows(core, jnp.where(second, 1.0, factor), jnp.where(second, factor, 1.0))
+    for h in range(half):
+        at = pl.ds(pl.multiple_of(core * (half * HEAD) + h * HEAD, HEAD), HEAD)
+        row = slice(h, h + 1)
+        pay[pl.ds(h * HEAD, HEAD), :] = (
+            own[at, :].astype(F32) * own_by[row] + peer[at, :].astype(F32) * peer_by[row]
+        ).astype(BF16)
+    store_total(pay, half * HEAD, total_own + total_peer)
     earlier[...] = jnp.where(second, total_peer, 0.0)
 
 
-def middle_kernel(meta, docs, own, one, two, three, before, pay, left, earlier):
+def middle_kernel(docs, own, one, two, three, before, after, pay, left, earlier):
     heads = before.shape[0]
-    top = heads * HEAD
-    ctx = meta[0]
-    chip = ctx >> 1
+    half = heads // 2
+    top = half * HEAD
+    ctx = lax.axis_index("ctx")
+    core, chip = ctx & 1, ctx >> 1
     odd, high = (chip & 1) == 1, (chip & 2) == 2
     t_own, t_one, t_two, t_three = (load_total(x, top, heads) for x in (own, one, two, three))
     last = lambda at: (at + 1) * 2 * STEPS - 1
@@ -242,16 +252,23 @@
     keep_all = joined(docs, last(base + 1), last(base + 3))
     by_mine = jnp.exp(jnp.where(odd, t_own, t_one)) * keep_mine
     by_theirs = jnp.exp(jnp.where(odd, t_two, t_three)) * keep_theirs
-    own_by, one_by = jnp.where(odd, 1.0, by_mine), jnp.where(odd, by_mine, 1.0)
-    two_by, three_by = jnp.where(odd, 1.0, by_theirs), jnp.where(odd, by_theirs, 1.0)
     by_all = jnp.exp(jnp.where(high, t_own + t_one, t_two + t_three)) * keep_all
-    mine_by, theirs_by = jnp.where(high, 1.0, by_all), jnp.where(high, by_all, 1.0)
-    for h in range(heads):
+    own_by, one_by, two_by, three_by, mine_by, theirs_by = half_rows(
+        core,
+        jnp.where(odd, 1.0, by_mine),
+        jnp.where(odd, by_mine, 1.0),
+        jnp.where(odd, 1.0, by_theirs),
+        jnp.where(odd, by_theirs, 1.0),
+        jnp.where(high, 1.0, by_all),
+        jnp.where(high, by_all, 1.0),
+    )
+    for h in range(half):
         at = pl.ds(h * HEAD, HEAD)
         row = slice(h, h + 1)
         here = own[at, :].astype(F32) * own_by[row] + one[at, :].astype(F32) * one_by[row]
         there = two[at, :].astype(F32) * two_by[row] + three[at, :].astype(F32) * three_by[row]
-        left[at, :] = there.astype(BF16)
+        left[at, :] = one[at, :]
+        left[pl.ds(top + h * HEAD, HEAD), :] = there.astype(BF16)
         pay[at, :] = (here * mine_by[row] + there * theirs_by[row]).astype(BF16)
     store_total(pay, top, (t_own + t_one) + (t_two + t_three))
     second = before[...] + jnp.where(odd, t_one, 0.0)
@@ -259,27 +276,46 @@
     earlier[pl.ds(heads, heads), :] = second + jnp.where(high, t_two + t_three, 0.0)
 
 
-def far_kernel(meta, docs, one, two, three, before, left, earlier):
+def far_kernel(docs, one, two, three, before, after, left, earlier):
     heads = earlier.shape[0]
-    top = heads * HEAD
-    row_of = meta[0] >> 3
+    half = heads // 2
+    top = half * HEAD
+    ctx = lax.axis_index("ctx")
+    row_of = ctx >> 3
     odd = (row_of & 1) == 1
     t_one, t_two, t_three = (load_total(x, top, heads) for x in (one, two, three))
     theirs = ((row_of >> 1) ^ 1) << 1
     last = lambda at: (at + 1) * 8 * STEPS - 1
     factor = jnp.exp(jnp.where(odd, t_two, t_three)) * joined(docs, last(theirs), last(theirs + 1))
-    two_by, three_by = jnp.where(odd, 1.0, factor), jnp.where(odd, factor, 1.0)
-    for h in range(heads):
+    two_by, three_by = half_rows(ctx & 1, jnp.where(odd, 1.0, factor), jnp.where(odd, factor, 1.0))
+    for h in range(half):
         at = pl.ds(h * HEAD, HEAD)
-        left[at, :] = (
-            two[at, :].astype(F32) * two_by[h : h + 1] + three[at, :].astype(F32) * three_by[h : h + 1]
+        row = slice(h, h + 1)
+        left[at, :] = one[at, :]
+        left[pl.ds(top + h * HEAD, HEAD), :] = (
+            two[at, :].astype(F32) * two_by[row] + three[at, :].astype(F32) * three_by[row]
         ).astype(BF16)
     earlier[...] = before[pl.ds(heads, heads), :] + jnp.where(odd, t_one, 0.0)
 
 
-def gate_kernel(tok, gate, w_level, out_hbm, gates, weight, w_out, sem):
-    copy = pltpu.make_async_copy(out_hbm, w_out, sem)
-    copy.start()
+def assemble(core, own, peer, full):
+    half = own.shape[0] // 2
+    for level in range(2):
+        source = pl.ds(level * half, half)
+        full[level, pl.ds(pl.multiple_of(core * half, half), half), :] = own[source, :]
+        full[level, pl.ds(pl.multiple_of((1 - core) * half, half), half), :] = peer[source, :]
+
+
+def gate_kernel(tok, w_level, gate_hbm, out_hbm, gates, weight, w_out, w_gate, sems):
+    blocks = w_gate.shape[1] // BLOCK
+
+    def gate_copy(k):
+        at = pl.ds(pl.multiple_of(k * BLOCK, BLOCK), BLOCK)
+        return pltpu.make_async_copy(gate_hbm.at[:, at], w_gate.at[:, at], sems.at[k])
+
+    out_copy = pltpu.make_async_copy(out_hbm, w_out, sems.at[blocks])
+    gate_copy(0).start()
+    gate_copy(1).start()
     cols = w_level.shape[1]
     heads = cols // LEVELS
     to_row, from_col = iota((cols, cols), 0), iota((cols, cols), 1)
@@ -287,17 +323,39 @@
     turned = dot_nt(pick, dot(tok[...], w_level[...]).astype(BF16))
     weight[...] = jnp.maximum(turned, 0.0) + jnp.log1p(jnp.exp(-jnp.abs(turned)))
 
-    @pl.loop(0, gate.shape[1] // BLOCK)
+    @pl.loop(0, blocks)
     def _(k):
+        gate_copy(k).wait()
+
+        @pl.when(k + 2 < blocks)
+        def _():
+            gate_copy(k + 2).start()
+
+        @pl.when(k == 1)
+        def _():
+            out_copy.start()
+
         at = pl.ds(pl.multiple_of(k * BLOCK, BLOCK), BLOCK)
-        gates[at, :] = jnp.transpose(dot(tok[...], gate[:, at]).astype(BF16))
-
-    copy.wait()
-
-
-def intra_kernel(meta, docs, skip, weight, decays, v, sp, local, ho, scaled_weight):
+        gates[at, :] = jnp.transpose(dot(tok[...], w_gate[:, at]).astype(BF16))
+
+    out_copy.wait()
+
+
+def remote_term(docs, ctx, bit, stretch_doc, weight, here, gone, source, c_out):
+    heads = weight.shape[0] // LEVELS
+    base = (ctx >> (bit + 1)) << (bit + 1)
+    last_left = docs[(base + (1 << bit)) * STEPS - 1]
+    live = ((((ctx >> bit) & 1) == 1) & (last_left == stretch_doc)).astype(F32)
+    rows = weight[pl.ds((bit + 3) * heads, heads), here] * live
+    if gone is not None:
+        rows = rows * twice(jnp.exp(gone))
+    return dot_nt(source[pl.ds(0, heads * HEAD), :], c_out), rows
+
+
+def intra_kernel(docs, skip, weight, decays, v, sp, local, r0, ho, scaled_weight):
     heads = decays.shape[0]
-    first = meta[0] * STEPS
+    ctx = lax.axis_index("ctx")
+    first = ctx * STEPS
     causal = iota((128, 128), 0) <= iota((128, 128), 1)
     lower = (iota((STRETCH, STRETCH), 0) >= iota((STRETCH, STRETCH), 1)).astype(F32)
     begin = jnp.zeros((heads, STATE), F32)
@@ -324,6 +382,8 @@
             factor = grown * jnp.exp(twice(previous)) if index == 3 else grown
             terms.append((1, weight[pl.ds(2 * heads, heads), here] * factor * keep))
         crosses = [(dot_nt(local[slot], c_out), row) for slot, row in terms]
+        stretch_doc = docs[first + index]
+        crosses.append(remote_term(docs, ctx, 0, stretch_doc, scaled_weight, here, None, r0, c_out))
         own_weight = weight[pl.ds(0, heads), here]
         for h in range(heads):
             at = slice(h * HEAD, (h + 1) * HEAD)
@@ -349,27 +409,41 @@
         previous = total
 
 
+def late_kernel(docs, sp, ho, weight, e1, e23, own, peer, out, full):
+    heads = e1.shape[0]
+    ctx = lax.axis_index("ctx")
+    assemble(ctx & 1, own, peer, full)
+    for index in range(STEPS):
+        here = pl.ds(index * STRETCH, STRETCH)
+        c_out = sp[here, STATE:]
+        stretch_doc = docs[ctx * STEPS + index]
+        terms = [
+            remote_term(docs, ctx, bit, stretch_doc, weight, here, gone, full.at[bit - 1], c_out)
+            for bit, gone in ((1, e1[...]), (2, e23[pl.ds(0, heads), :]))
+        ]
+        for h in range(heads):
+            at = pl.ds(h * HEAD, HEAD)
+            total = ho[at, here]
+            for cross, rows in terms:
+                total = total + rows[h : h + 1, :] * cross[h * HEAD : (h + 1) * HEAD]
+            out[at, here] = total
+
+
 def finish_kernel(
-    start, count, meta, docs, gain, w_out, sp, gates, ho, weight, e1, e23, e4, *refs
+    start, count, docs, gain, w_out, sp, gates, ho, weight, e23, e4, *refs
 ):
-    sources = refs[:5]
-    plus, minus, keep, own, acc, normed = refs[5:]
-    ctx, tp = meta[0], meta[1]
-    heads = e1.shape[0]
+    far_own, far_peer, plus, minus, keep, own, acc, normed, full = refs
+    ctx, tp = lax.axis_index("ctx"), lax.axis_index("tp")
+    heads = e4.shape[0]
+    assemble(ctx & 1, far_own, far_peer, full)
     for j in range(count):
         here = pl.ds((start + j) * STRETCH, STRETCH)
+        c_out = sp[here, STATE:]
         stretch_doc = docs[ctx * STEPS + start + j]
-        c_out = sp[here, STATE:]
-        terms = []
-        for bit in range(5):
-            base = (ctx >> (bit + 1)) << (bit + 1)
-            last_left = docs[(base + (1 << bit)) * STEPS - 1]
-            live = ((((ctx >> bit) & 1) == 1) & (last_left == stretch_doc)).astype(F32)
-            rows = weight[pl.ds((bit + 3) * heads, heads), here] * live
-            if bit:
-                gone = (None, e1[...], e23[pl.ds(0, heads), :], e23[pl.ds(heads, heads), :], e4[...])[bit]
-                rows = rows * twice(jnp.exp(gone))
-            terms.append((dot_nt(sources[bit][pl.ds(0, heads * HEAD), :], c_out), rows))
+        terms = [
+            remote_term(docs, ctx, bit, stretch_doc, weight, here, gone, full.at[bit - 3], c_out)
+            for bit, gone in ((3, e23[pl.ds(heads, heads), :]), (4, e4[...]))
+        ]
         for h in range(heads):
             at = pl.ds(h * HEAD, HEAD)
             total = ho[at, here]
@@ -397,17 +471,21 @@
     own[:, second] = piece(0, 1)
 
 
-def finish(start, stop, meta, docs, gain, w_out, *operands):
+def finish(start, stop, docs, gain, w_out, *operands):
     count = stop - start
     width, depth = w_out.shape
     rows = count * STRETCH
     return call(
         functools.partial(finish_kernel, start, count),
         f"finish{start}",
-        [SMEM] * 2 + [VMEM] * (2 + len(operands)),
+        [SMEM] + [VMEM] * (2 + len(operands)),
         [((rows, depth // 4), BF16)] * 4,
-        (meta, docs, gain, w_out, *operands),
-        [pltpu.VMEM((width, STRETCH), F32), pltpu.VMEM((rows, width), BF16)],
+        (docs, gain, w_out, *operands),
+        [
+            pltpu.VMEM((width, STRETCH), F32),
+            pltpu.VMEM((rows, width), BF16),
+            pltpu.VMEM((2, width, STATE), BF16),
+        ],
         mib=16,
         flops=4 * rows * depth * width,
         moved=2 * width * depth + 8 * rows * width,
@@ -418,70 +496,80 @@
     rows, depth = tokens.shape
     width = w_value.shape[1]
     heads = log_decay.shape[1]
-    ctx, tp = lax.axis_index("ctx"), lax.axis_index("tp")
-    meta = jnp.where(jnp.arange(2, dtype=jnp.int32) == 0, ctx, tp)
+    docs = far(doc_ids)
     decays = jnp.transpose(log_decay)
-    payload = ((width + 3 * heads, STATE), BF16)
+    part = ((width // 2 + 3 * heads, STATE), BF16)
     tail = ((width, STATE), BF16)
+    gone = ((heads, STATE), F32)
 
     def across(x, by):
         return lax.ppermute(x, "ctx", [(i, i ^ by) for i in range(32)])
 
-    def upward(x, by):
-        return lax.ppermute(x, "ctx", [(i, i ^ by) for i in range(32) if i < i ^ by])
-
     def turn(x, by):
         return lax.ppermute(x, "tp", [(i, (i + by) % 4) for i in range(4)])
 
-    tok, gate, sp, v, local, pay0 = project(meta, doc_ids, decays, tokens, w_value, w_state, w_gate)
+    tok, sp, v, local, pay0 = project(docs, decays, tokens, w_value, w_state)
     peer = across(pay0, 1)
     pay1, e1 = call(
-        near_kernel, "near", [SMEM] * 2 + [VMEM] * 2, [payload, ((heads, STATE), F32)], (meta, doc_ids, pay0, peer)
+        near_kernel, "near", [SMEM] + [VMEM] * 2, [part, gone], (docs, pay0, peer)
     )
     ys = [across(pay1, by) for by in (4, 2, 6)]
     gates, weight, w_out_near = call(
         gate_kernel,
         "gate",
-        [VMEM] * 3 + [FAR],
+        [VMEM] * 2 + [FAR] * 2,
         [((width, rows), BF16), ((heads * LEVELS, rows), F32), (w_out.shape, BF16)],
-        (tok, gate, w_level, far(w_out)),
-        [pltpu.SemaphoreType.DMA(())],
-        mib=12,
+        (tok, w_level, far(w_gate), far(w_out)),
+        [pltpu.VMEM(w_gate.shape, BF16), pltpu.SemaphoreType.DMA((width // BLOCK + 1,))],
+        mib=16,
         flops=2 * rows * depth * (width + STATE),
         moved=2 * (rows * depth + depth * width),
     )
     y2, y1, y3 = ys
-    pay2, left2, e23 = call(
+    pay2, mid_own, e23 = call(
         middle_kernel,
         "middle",
-        [SMEM] * 2 + [VMEM] * 5,
-        [payload, tail, ((2 * heads, STATE), F32)],
-        (meta, doc_ids, pay1, y1, y2, y3, e1),
-    )
-    x2, x1, x3 = (upward(pay2, by) for by in (16, 8, 24))
+        [SMEM] + [VMEM] * 6,
+        [part, tail, ((2 * heads, STATE), F32)],
+        (docs, pay1, y1, y2, y3, e1, weight),
+    )
+    x2, x1, x3 = (across(pay2, by) for by in (16, 8, 24))
+    mid_peer = across(mid_own, 1)
     ho, scaled_weight = call(
         intra_kernel,
         "intra",
-        [SMEM] * 3 + [VMEM] * 5,
+        [SMEM] * 2 + [VMEM] * 6,
         [((width, rows), F32), ((heads * LEVELS, rows), F32)],
-        (meta, doc_ids, skip_weight, weight, decays, v, sp, local),
+        (docs, skip_weight, weight, decays, v, sp, local, peer),
         mib=12,
         flops=6 << 30,
         moved=8 << 20,
     )
-    left4, e4 = call(
+    far_own, e4 = call(
         far_kernel,
         "far",
-        [SMEM] * 2 + [VMEM] * 4,
-        [tail, ((heads, STATE), F32)],
-        (meta, doc_ids, x1, x2, x3, e23),
+        [SMEM] + [VMEM] * 5,
+        [tail, gone],
+        (docs, x1, x2, x3, e23, scaled_weight),
+    )
+    far_peer = across(far_own, 1)
+    (ho,) = call(
+        late_kernel,
+        "late",
+        [SMEM] + [VMEM] * 7,
+        [((width, rows), F32)],
+        (docs, sp, ho, scaled_weight, e1, e23, mid_own, mid_peer),
+        [pltpu.VMEM((2, width, STATE), BF16)],
+        mib=8,
+        flops=2 << 30,
+        moved=4 << 20,
     )
     gain = norm_gain.reshape(1, -1)
     results = []
     half = w_out.shape[1] // 8
     for lo, hi in CHUNKS:
         plus, minus, keep, own = finish(
-            lo, hi, meta, doc_ids, gain, w_out_near, sp, gates, ho, scaled_weight, e1, e23, e4, peer, y1, left2, x1, left4
+            lo, hi, docs, gain, w_out_near, sp, gates, ho, scaled_weight, e23, e4, far_own, far_peer
         )
         from_below, from_above = turn(plus, 1), turn(minus, 3)
         on_plus = (keep[:, :half].astype(F32) + from_below[:, :half].astype(F32)).astype(BF16)

time: 98.9 us -> 91.1 us (0.921)
  waiting for transfers between devices: 29.4 us -> 23.9 us
  starting transfers between devices: 27.2 us -> 24.6 us
  Pallas kernels: 37.8 us -> 39.6 us
  local copies, waits for them, and re-layouts: 1.51 us -> 0.02 us
    ppermute x3 -> x0, starting transfers between devices: 8.93 us -> none  [upward(): lax.ppermute(x, 'ctx', [(i, i ^ by) for i in range(32) if i < i ^ by])]
    ppermute x4 -> x9, starting transfers between devices: 4.26 us -> 9.73 us  [across(): return lax.ppermute(x, 'ctx', [(i, i ^ by) for i in range(32)])]
    ppermute x4 -> x9, waiting for transfers between devices: 7.08 us -> 4.54 us  [across(): return lax.ppermute(x, 'ctx', [(i, i ^ by) for i in range(32)])]
    ppermute x3 -> x0, waiting for transfers between devices: 2.03 us -> none  [upward(): lax.ppermute(x, 'ctx', [(i, i ^ by) for i in range(32) if i < i ^ by])]
    pallas_call x8 -> x9, Pallas kernels: 37.8 us -> 39.6 us  [call(): pl.pallas_call(kernel, name=name, in_specs=in_specs, out_specs=[VMEM] * l...]
    unnamed x14 -> x8, local copies, waits for them, and re-layouts: 1.51 us -> 0.02 us
  transfers between devices with their start and end apart: 15 -> 17, of which waited for: 11 -> 7; matrix products, arithmetic and copies ran while one was open for 0% -> 1% of each run, Pallas kernels for 18% -> 23%
where the time goes in v1:
time: 91.1 us; the launch traced here: 90.1 us
  Pallas kernels  39.6 us (43%)
  starting transfers between devices  24.6 us (27%)
  waiting for transfers between devices  23.9 us (26%)
  other arithmetic  1.76 us (2%)
    pallas_call x9, Pallas kernels, call(): pl.pallas_call(kernel, name=name, in_specs=in_specs, out_specs=[VMEM] * l...  39.6 us
    ppermute x8, waiting for transfers between devices, turn(): return lax.ppermute(x, 'tp', [(i, (i + by) % 4) for i in range(4)])  19.4 us
    ppermute x8, starting transfers between devices, turn(): return lax.ppermute(x, 'tp', [(i, (i + by) % 4) for i in range(4)])  14.9 us
    ppermute x9, starting transfers between devices, across(): return lax.ppermute(x, 'ctx', [(i, i ^ by) for i in range(32)])  9.73 us
    ppermute x9, waiting for transfers between devices, across(): return lax.ppermute(x, 'ctx', [(i, i ^ by) for i in range(32)])  4.54 us
  transfers between devices with their start and end apart: 17, of which 7 were waited for; matrix products, arithmetic and copies ran while one was open for 1% of the time, Pallas kernels for 23%

profile of v1, /device:TPU:0, one launch (start us, length us, event | category | flops | bytes accessed | tf_op | source)
XLA Modules:
  0.0 90.1 jit_solution(1490931792827668557)
XLA Ops:
  0.0 12.8 %project.1 = (bf16[1024,2048]{1,0:T(8,128)(2,1)S(1)}, bf16[1024,256]{1,0:T(8,128)(2,1)S(1)}, bf16[1024,1024]{1,0:T(8,128)(2,1)S(1)}, bf16[3,1024,128]{2,1,0:T(8,128)(2,1)S(1)}, bf16[1072,128]{1,0:T(8,128)(2,1)S(1)}) custom-call(s32[128]{0:T(128)} %docs.15, f32[16,1024]{1,0:T(8,128)} %bitcast.2, bf16[1024,2048]{1,0:T(8,128)(2,1)} %tok_hbm.1, ...), custom_call_target="tpu_custom_call" | custom-call | flops 5368709120 | bytes 8388608 | tf_op jit(solution)/shard_map/project/pallas_call | solution.py:76
  12.9 1.5 %collective-permute-done.r0.peer = bf16[1072,128]{1,0:T(8,128)(2,1)S(1)} collective-permute-done((bf16[1072,128]{1,0:T(8,128)(2,1)S(1)}, bf16[1072,128]{1,0:T(8,128)(2,1)S(1)}, u32[]{:S(2)}, u32[]{:S(2)}) %collective-permute-start) | collective-permute-done | bytes 274464 | tf_op jit(solution)/shard_map/ppermute | solution.py:506
  15.2 1.7 %collective-permute-start.1 = (bf16[560,128]{1,0:T(8,128)(2,1)S(1)}, bf16[560,128]{1,0:T(8,128)(2,1)S(1)}, u32[]{:S(2)}, u32[]{:S(2)}) collective-permute-start(bf16[560,128]{1,0:T(8,128)(2,1)S(1)} %get-tuple-element.41.own), channel_id=1, source_target_pairs={{0,8},{4,12},{8,0},{12,4},{16,24},{20,28},{24,16},{28,20},{32,40},... | collective-permute-start | bytes 430088 | tf_op jit(solution)/shard_map/ppermute | solution.py:506
  16.9 2.9 %collective-permute-start.2 = (bf16[560,128]{1,0:T(8,128)(2,1)S(1)}, bf16[560,128]{1,0:T(8,128)(2,1)S(1)}, u32[]{:S(2)}, u32[]{:S(2)}) collective-permute-start(bf16[560,128]{1,0:T(8,128)(2,1)S(1)} %get-tuple-element.41.own), channel_id=1, source_target_pairs={{0,16},{4,20},{8,24},{12,28},{16,0},{20,4},{24,8},{28,12},{32,48},... | collective-permute-start | bytes 430088 | tf_op jit(solution)/shard_map/ppermute | solution.py:506
  20.0 6.9 %gate.1 = (bf16[1024,1024]{1,0:T(8,128)(2,1)S(1)}, f32[128,1024]{1,0:T(8,128)S(1)}, bf16[1024,2048]{1,0:T(8,128)(2,1)S(1)}) custom-call(bf16[1024,2048]{1,0:T(8,128)(2,1)S(1)} %get-tuple-element.30.tok, bf16[2048,128]{1,0:T(8,128)(2,1)S(1)} %copy-done, bf16[2048,1024]{1,0:T(8,128)(2,1)} %gate_hbm.1, bf16[1024,2048]{1,0:T(8,128)(2,1)} %out_hbm.1), custom_call_target="tpu_custom_call" | custom-call | flops 4831838208 | bytes 8388608 | tf_op jit(solution)/shard_map/gate/pallas_call | solution.py:76
  26.9 2.2 %collective-permute-done.3.three = bf16[560,128]{1,0:T(8,128)(2,1)S(1)} collective-permute-done((bf16[560,128]{1,0:T(8,128)(2,1)S(1)}, bf16[560,128]{1,0:T(8,128)(2,1)S(1)}, u32[]{:S(2)}, u32[]{:S(2)}) %collective-permute-start.3) | collective-permute-done | bytes 143392 | tf_op jit(solution)/shard_map/ppermute | solution.py:506
  30.0 1.6 %collective-permute-start.5 = (bf16[560,128]{1,0:T(8,128)(2,1)S(1)}, bf16[560,128]{1,0:T(8,128)(2,1)S(1)}, u32[]{:S(2)}, u32[]{:S(2)}) collective-permute-start(bf16[560,128]{1,0:T(8,128)(2,1)S(1)} %get-tuple-element.44), channel_id=1, source_target_pairs={{0,32},{4,36},{8,40},{12,44},{16,48},{20,52},{24,56},{28,60},{32,0... | collective-permute-start | bytes 430088 | tf_op jit(solution)/shard_map/ppermute | solution.py:506
  31.6 2.7 %collective-permute-start.6 = (bf16[560,128]{1,0:T(8,128)(2,1)S(1)}, bf16[560,128]{1,0:T(8,128)(2,1)S(1)}, u32[]{:S(2)}, u32[]{:S(2)}) collective-permute-start(bf16[560,128]{1,0:T(8,128)(2,1)S(1)} %get-tuple-element.44), channel_id=1, source_target_pairs={{0,64},{4,68},{8,72},{12,76},{16,80},{20,84},{24,88},{28,92},{32,9... | collective-permute-start | bytes 430088 | tf_op jit(solution)/shard_map/ppermute | solution.py:506
  34.8 6.8 %intra.1 = (f32[1024,1024]{1,0:T(8,128)S(1)}, f32[128,1024]{1,0:T(8,128)S(1)}) custom-call(s32[128]{0:T(128)} %docs.15, f32[16]{0:T(128)S(1)} %copy-done.3, f32[128,1024]{1,0:T(8,128)S(1)} %get-tuple-element.34.weight.after, f32[16,1024]{1,0:T(8,128)S(1)} %bitcast.3, bf16[1024,1024]{1,0:T(8,128)(2,1)S(1)} %get-tuple-element.35.v, ...), custom_call_target="tpu_custom_call" | custom-call | flops 6442450944 | bytes 8388608 | tf_op jit(solution)/shard_map/intra/pallas_call | solution.py:76
  43.3 2.1 %late.1.ho = f32[1024,1024]{1,0:T(8,128)S(1)} custom-call(s32[128]{0:T(128)} %docs.15, bf16[1024,256]{1,0:T(8,128)(2,1)S(1)} %get-tuple-element.32.sp, f32[1024,1024]{1,0:T(8,128)S(1)} %get-tuple-element.38.ho, f32[128,1024]{1,0:T(8,128)S(1)} %get-tuple-element.39.weight.after, f32[16,128]{1,0:T(8,128)S(1)} %get-tuple-element.40.before.e1, ...), custom_call_target="tpu_custom_call" | custom-call | flops 2147483648 | bytes 4194304 | tf_op jit(solution)/shard_map/late/pallas_call | solution.py:76
  45.4 4.3 %finish2.1 = (bf16[512,512]{1,0:T(8,128)(2,1)S(1)}, bf16[512,512]{1,0:T(8,128)(2,1)S(1)}, bf16[512,512]{1,0:T(8,128)(2,1)S(1)}, bf16[512,512]{1,0:T(8,128)(2,1)S(1)}) custom-call(s32[128]{0:T(128)} %docs.15, f32[1,1024]{1,0:T(1,128)S(1)} %bitcast.4, bf16[1024,2048]{1,0:T(8,128)(2,1)S(1)} %get-tuple-element.31.w_out, ...), custom_call_target="tpu_custom_call" | custom-call | flops 4294967296 | bytes 8388608 | tf_op jit(solution)/shard_map/finish2/pallas_call | solution.py:76
  49.7 2.0 %collective-permute-start.14 = (bf16[512,512]{1,0:T(8,128)(2,1)S(1)}, bf16[512,512]{1,0:T(8,128)(2,1)S(1)}, u32[]{:S(2)}, u32[]{:S(2)}) collective-permute-start(bf16[512,512]{1,0:T(8,128)(2,1)S(1)} %get-tuple-element.54), channel_id=1, source_target_pairs={{0,1},{1,2},{2,3},{3,0},{4,5},{5,6},{6,7},{7,4},{8,9},{9,10},{10,1... | collective-permute-start | bytes 1572872 | tf_op jit(solution)/shard_map/ppermute | solution.py:509
  51.7 2.4 %collective-permute-start.13 = (bf16[512,512]{1,0:T(8,128)(2,1)S(1)}, bf16[512,512]{1,0:T(8,128)(2,1)S(1)}, u32[]{:S(2)}, u32[]{:S(2)}) collective-permute-start(bf16[512,512]{1,0:T(8,128)(2,1)S(1)} %get-tuple-element.52), channel_id=1, source_target_pairs={{0,3},{1,0},{2,1},{3,2},{4,7},{5,4},{6,5},{7,6},{8,11},{9,8},{10,9... | collective-permute-start | bytes 1572872 | tf_op jit(solution)/shard_map/ppermute | solution.py:509
  54.1 4.3 %finish0.1 = (bf16[512,512]{1,0:T(8,128)(2,1)S(1)}, bf16[512,512]{1,0:T(8,128)(2,1)S(1)}, bf16[512,512]{1,0:T(8,128)(2,1)S(1)}, bf16[512,512]{1,0:T(8,128)(2,1)S(1)}) custom-call(s32[128]{0:T(128)} %docs.15, f32[1,1024]{1,0:T(1,128)S(1)} %bitcast.5, bf16[1024,2048]{1,0:T(8,128)(2,1)S(1)} %get-tuple-element.31.w_out, ...), custom_call_target="tpu_custom_call" | custom-call | flops 4294967296 | bytes 8388608 | tf_op jit(solution)/shard_map/finish0/pallas_call | solution.py:76
  58.5 3.2 %collective-permute-start.9 = (bf16[512,512]{1,0:T(8,128)(2,1)S(1)}, bf16[512,512]{1,0:T(8,128)(2,1)S(1)}, u32[]{:S(2)}, u32[]{:S(2)}) collective-permute-start(bf16[512,512]{1,0:T(8,128)(2,1)S(1)} %get-tuple-element.48), channel_id=1, source_target_pairs={{0,3},{1,0},{2,1},{3,2},{4,7},{5,4},{6,5},{7,6},{8,11},{9,8},{10,9... | collective-permute-start | bytes 1572872 | tf_op jit(solution)/shard_map/ppermute | solution.py:509
  61.7 4.8 %collective-permute-done.14 = bf16[512,512]{1,0:T(8,128)(2,1)S(1)} collective-permute-done((bf16[512,512]{1,0:T(8,128)(2,1)S(1)}, bf16[512,512]{1,0:T(8,128)(2,1)S(1)}, u32[]{:S(2)}, u32[]{:S(2)}) %collective-permute-start.14) | collective-permute-done | bytes 524320 | tf_op jit(solution)/shard_map/ppermute | solution.py:509
  66.7 1.9 %collective-permute-start.15 = (bf16[512,256]{1,0:T(8,128)(2,1)S(1)}, bf16[512,256]{1,0:T(8,128)(2,1)S(1)}, u32[]{:S(2)}, u32[]{:S(2)}) collective-permute-start(bf16[512,256]{1,0:T(8,128)(2,1)S(1)} %get-tuple-element.61), channel_id=1, source_target_pairs={{0,1},{1,2},{2,3},{3,0},{4,5},{5,6},{6,7},{7,4},{8,9},{9,10},{10,1... | collective-permute-start | bytes 786440 | tf_op jit(solution)/shard_map/ppermute | solution.py:509
  68.6 1.7 %collective-permute-start.16 = (bf16[512,256]{1,0:T(8,128)(2,1)S(1)}, bf16[512,256]{1,0:T(8,128)(2,1)S(1)}, u32[]{:S(2)}, u32[]{:S(2)}) collective-permute-start(bf16[512,256]{1,0:T(8,128)(2,1)S(1)} %get-tuple-element.62), channel_id=1, source_target_pairs={{0,3},{1,0},{2,1},{3,2},{4,7},{5,4},{6,5},{7,6},{8,11},{9,8},{10,9... | collective-permute-start | bytes 786440 | tf_op jit(solution)/shard_map/ppermute | solution.py:509
  70.3 7.5 %collective-permute-done.10 = bf16[512,512]{1,0:T(8,128)(2,1)S(1)} collective-permute-done((bf16[512,512]{1,0:T(8,128)(2,1)S(1)}, bf16[512,512]{1,0:T(8,128)(2,1)S(1)}, u32[]{:S(2)}, u32[]{:S(2)}) %collective-permute-start.10) | collective-permute-done | bytes 524320 | tf_op jit(solution)/shard_map/ppermute | solution.py:509
  77.9 1.9 %collective-permute-start.11 = (bf16[512,256]{1,0:T(8,128)(2,1)S(1)}, bf16[512,256]{1,0:T(8,128)(2,1)S(1)}, u32[]{:S(2)}, u32[]{:S(2)}) collective-permute-start(bf16[512,256]{1,0:T(8,128)(2,1)S(1)} %get-tuple-element.57), channel_id=1, source_target_pairs={{0,1},{1,2},{2,3},{3,0},{4,5},{5,6},{6,7},{7,4},{8,9},{9,10},{10,1... | collective-permute-start | bytes 786440 | tf_op jit(solution)/shard_map/ppermute | solution.py:509
  79.8 1.7 %collective-permute-start.12 = (bf16[512,256]{1,0:T(8,128)(2,1)S(1)}, bf16[512,256]{1,0:T(8,128)(2,1)S(1)}, u32[]{:S(2)}, u32[]{:S(2)}) collective-permute-start(bf16[512,256]{1,0:T(8,128)(2,1)S(1)} %get-tuple-element.58), channel_id=1, source_target_pairs={{0,3},{1,0},{2,1},{3,2},{4,7},{5,4},{6,5},{7,6},{8,11},{9,8},{10,9... | collective-permute-start | bytes 786440 | tf_op jit(solution)/shard_map/ppermute | solution.py:509
  81.5 1.9 %collective-permute-done.15 = bf16[512,256]{1,0:T(8,128)(2,1)S(1)} collective-permute-done((bf16[512,256]{1,0:T(8,128)(2,1)S(1)}, bf16[512,256]{1,0:T(8,128)(2,1)S(1)}, u32[]{:S(2)}, u32[]{:S(2)}) %collective-permute-start.15) | collective-permute-done | bytes 262176 | tf_op jit(solution)/shard_map/ppermute | solution.py:509
  83.7 5.2 %collective-permute-done.11 = bf16[512,256]{1,0:T(8,128)(2,1)S(1)} collective-permute-done((bf16[512,256]{1,0:T(8,128)(2,1)S(1)}, bf16[512,256]{1,0:T(8,128)(2,1)S(1)}, u32[]{:S(2)}, u32[]{:S(2)}) %collective-permute-start.11) | collective-permute-done | bytes 262176 | tf_op jit(solution)/shard_map/ppermute | solution.py:509
  89.0 1.1 %maximum_maximum_fusion = bf16[1024,512]{1,0:T(8,128)(2,1)} fusion(bf16[512,256]{1,0:T(8,128)(2,1)S(1)} %get-tuple-element.60, bf16[512,256]{1,0:T(8,128)(2,1)S(1)} %get-tuple-element.59, bf16[512,256]{1,0:T(8,128)(2,1)S(1)} %get-tuple-element.56, bf16[512,256]{1,0:T(8,128)(2,1)S(1)} %get-tuple-element.55), kind=kLoop, calls=%fused_computation | loop fusion | flops 4194304 | bytes 2097152 | tf_op jit(solution)/shard_map/concatenate | solution.py:581
  (32 shorter events, 4.7 us)
Async XLA Ops:
  0.0 20.0 %copy-start = (bf16[2048,128]{1,0:T(8,128)(2,1)S(1)}, bf16[2048,128]{1,0:T(8,128)(2,1)}, u32[]{:S(2)}) copy-start(bf16[2048,128]{1,0:T(8,128)(2,1)} %w_level.1) | copy-start | bytes 1572868
  12.8 1.6 %collective-permute-start = (bf16[1072,128]{1,0:T(8,128)(2,1)S(1)}, bf16[1072,128]{1,0:T(8,128)(2,1)S(1)}, u32[]{:S(2)}, u32[]{:S(2)}) collective-permute-start(bf16[1072,128]{1,0:T(8,128)(2,1)S(1)} %get-tuple-element.37.own), channel_id=1, source_target_pairs={{0,4},{4,0},{8,12},{12,8},{16,20},{20,16},{24,28},{28,24},{32,36},... | collective-permute-start | bytes 823304 | tf_op jit(solution)/shard_map/ppermute | solution.py:506
  15.2 11.7 %collective-permute-start.1 = (bf16[560,128]{1,0:T(8,128)(2,1)S(1)}, bf16[560,128]{1,0:T(8,128)(2,1)S(1)}, u32[]{:S(2)}, u32[]{:S(2)}) collective-permute-start(bf16[560,128]{1,0:T(8,128)(2,1)S(1)} %get-tuple-element.41.own), channel_id=1, source_target_pairs={{0,8},{4,12},{8,0},{12,4},{16,24},{20,28},{24,16},{28,20},{32,40},... | collective-permute-start | bytes 430088 | tf_op jit(solution)/shard_map/ppermute | solution.py:506
  16.9 10.0 %collective-permute-start.2 = (bf16[560,128]{1,0:T(8,128)(2,1)S(1)}, bf16[560,128]{1,0:T(8,128)(2,1)S(1)}, u32[]{:S(2)}, u32[]{:S(2)}) collective-permute-start(bf16[560,128]{1,0:T(8,128)(2,1)S(1)} %get-tuple-element.41.own), channel_id=1, source_target_pairs={{0,16},{4,20},{8,24},{12,28},{16,0},{20,4},{24,8},{28,12},{32,48},... | collective-permute-start | bytes 430088 | tf_op jit(solution)/shard_map/ppermute | solution.py:506
  19.8 9.3 %collective-permute-start.3 = (bf16[560,128]{1,0:T(8,128)(2,1)S(1)}, bf16[560,128]{1,0:T(8,128)(2,1)S(1)}, u32[]{:S(2)}, u32[]{:S(2)}) collective-permute-start(bf16[560,128]{1,0:T(8,128)(2,1)S(1)} %get-tuple-element.41.own), channel_id=1, source_target_pairs={{0,24},{4,28},{8,16},{12,20},{16,8},{20,12},{24,0},{28,4},{32,56},... | collective-permute-start | bytes 430088 | tf_op jit(solution)/shard_map/ppermute | solution.py:506
  20.0 14.8 %copy-start.1 = (f32[1024,16]{0,1:T(8,128)S(1)}, f32[1024,16]{0,1:T(8,128)}, u32[]{:S(2)}) copy-start(f32[1024,16]{0,1:T(8,128)} %param.15) | copy-start | bytes 196612
  20.0 14.8 %copy-start.3 = (f32[16]{0:T(128)S(1)}, f32[16]{0:T(128)}, u32[]{:S(2)}) copy-start(f32[16]{0:T(128)} %skip.1) | copy-start | bytes 196
  30.0 11.6 %collective-permute-start.5 = (bf16[560,128]{1,0:T(8,128)(2,1)S(1)}, bf16[560,128]{1,0:T(8,128)(2,1)S(1)}, u32[]{:S(2)}, u32[]{:S(2)}) collective-permute-start(bf16[560,128]{1,0:T(8,128)(2,1)S(1)} %get-tuple-element.44), channel_id=1, source_target_pairs={{0,32},{4,36},{8,40},{12,44},{16,48},{20,52},{24,56},{28,60},{32,0... | collective-permute-start | bytes 430088 | tf_op jit(solution)/shard_map/ppermute | solution.py:506
  31.6 10.1 %collective-permute-start.6 = (bf16[560,128]{1,0:T(8,128)(2,1)S(1)}, bf16[560,128]{1,0:T(8,128)(2,1)S(1)}, u32[]{:S(2)}, u32[]{:S(2)}) collective-permute-start(bf16[560,128]{1,0:T(8,128)(2,1)S(1)} %get-tuple-element.44), channel_id=1, source_target_pairs={{0,64},{4,68},{8,72},{12,76},{16,80},{20,84},{24,88},{28,92},{32,9... | collective-permute-start | bytes 430088 | tf_op jit(solution)/shard_map/ppermute | solution.py:506
  34.3 8.1 %collective-permute-start.7 = (bf16[560,128]{1,0:T(8,128)(2,1)S(1)}, bf16[560,128]{1,0:T(8,128)(2,1)S(1)}, u32[]{:S(2)}, u32[]{:S(2)}) collective-permute-start(bf16[560,128]{1,0:T(8,128)(2,1)S(1)} %get-tuple-element.44), channel_id=1, source_target_pairs={{0,96},{4,100},{8,104},{12,108},{16,112},{20,116},{24,120},{28,124... | collective-permute-start | bytes 430088 | tf_op jit(solution)/shard_map/ppermute | solution.py:506
  34.8 8.5 %collective-permute-start.4 = (bf16[1024,128]{1,0:T(8,128)(2,1)S(1)}, bf16[1024,128]{1,0:T(8,128)(2,1)S(1)}, u32[]{:S(2)}, u32[]{:S(2)}) collective-permute-start(bf16[1024,128]{1,0:T(8,128)(2,1)S(1)} %get-tuple-element.43.own), channel_id=1, source_target_pairs={{0,4},{4,0},{8,12},{12,8},{16,20},{20,16},{24,28},{28,24},{32,36},... | collective-permute-start | bytes 786440 | tf_op jit(solution)/shard_map/ppermute | solution.py:506
  43.2 2.2 %collective-permute-start.8 = (bf16[1024,128]{1,0:T(8,128)(2,1)S(1)}, bf16[1024,128]{1,0:T(8,128)(2,1)S(1)}, u32[]{:S(2)}, u32[]{:S(2)}) collective-permute-start(bf16[1024,128]{1,0:T(8,128)(2,1)S(1)} %get-tuple-element.46.refs_0_), channel_id=1, source_target_pairs={{0,4},{4,0},{8,12},{12,8},{16,20},{20,16},{24,28},{28,24},{32,36},... | collective-permute-start | bytes 786440 | tf_op jit(solution)/shard_map/ppermute | solution.py:506
  43.3 2.1 %copy-start.2 = (f32[1024]{0:T(1024)S(1)}, f32[1024]{0:T(1024)}, u32[]{:S(2)}) copy-start(f32[1024]{0:T(1024)} %param.17) | copy-start | bytes 12292
  49.7 16.9 %collective-permute-start.14 = (bf16[512,512]{1,0:T(8,128)(2,1)S(1)}, bf16[512,512]{1,0:T(8,128)(2,1)S(1)}, u32[]{:S(2)}, u32[]{:S(2)}) collective-permute-start(bf16[512,512]{1,0:T(8,128)(2,1)S(1)} %get-tuple-element.54), channel_id=1, source_target_pairs={{0,1},{1,2},{2,3},{3,0},{4,5},{5,6},{6,7},{7,4},{8,9},{9,10},{10,1... | collective-permute-start | bytes 1572872 | tf_op jit(solution)/shard_map/ppermute | solution.py:509
  51.7 14.9 %collective-permute-start.13 = (bf16[512,512]{1,0:T(8,128)(2,1)S(1)}, bf16[512,512]{1,0:T(8,128)(2,1)S(1)}, u32[]{:S(2)}, u32[]{:S(2)}) collective-permute-start(bf16[512,512]{1,0:T(8,128)(2,1)S(1)} %get-tuple-element.52), channel_id=1, source_target_pairs={{0,3},{1,0},{2,1},{3,2},{4,7},{5,4},{6,5},{7,6},{8,11},{9,8},{10,9... | collective-permute-start | bytes 1572872 | tf_op jit(solution)/shard_map/ppermute | solution.py:509
  58.4 19.4 %collective-permute-start.10 = (bf16[512,512]{1,0:T(8,128)(2,1)S(1)}, bf16[512,512]{1,0:T(8,128)(2,1)S(1)}, u32[]{:S(2)}, u32[]{:S(2)}) collective-permute-start(bf16[512,512]{1,0:T(8,128)(2,1)S(1)} %get-tuple-element.50), channel_id=1, source_target_pairs={{0,1},{1,2},{2,3},{3,0},{4,5},{5,6},{6,7},{7,4},{8,9},{9,10},{10,1... | collective-permute-start | bytes 1572872 | tf_op jit(solution)/shard_map/ppermute | solution.py:509
  58.5 19.3 %collective-permute-start.9 = (bf16[512,512]{1,0:T(8,128)(2,1)S(1)}, bf16[512,512]{1,0:T(8,128)(2,1)S(1)}, u32[]{:S(2)}, u32[]{:S(2)}) collective-permute-start(bf16[512,512]{1,0:T(8,128)(2,1)S(1)} %get-tuple-element.48), channel_id=1, source_target_pairs={{0,3},{1,0},{2,1},{3,2},{4,7},{5,4},{6,5},{7,6},{8,11},{9,8},{10,9... | collective-permute-start | bytes 1572872 | tf_op jit(solution)/shard_map/ppermute | solution.py:509
  66.7 16.7 %collective-permute-start.15 = (bf16[512,256]{1,0:T(8,128)(2,1)S(1)}, bf16[512,256]{1,0:T(8,128)(2,1)S(1)}, u32[]{:S(2)}, u32[]{:S(2)}) collective-permute-start(bf16[512,256]{1,0:T(8,128)(2,1)S(1)} %get-tuple-element.61), channel_id=1, source_target_pairs={{0,1},{1,2},{2,3},{3,0},{4,5},{5,6},{6,7},{7,4},{8,9},{9,10},{10,1... | collective-permute-start | bytes 786440 | tf_op jit(solution)/shard_map/ppermute | solution.py:509
  68.6 14.8 %collective-permute-start.16 = (bf16[512,256]{1,0:T(8,128)(2,1)S(1)}, bf16[512,256]{1,0:T(8,128)(2,1)S(1)}, u32[]{:S(2)}, u32[]{:S(2)}) collective-permute-start(bf16[512,256]{1,0:T(8,128)(2,1)S(1)} %get-tuple-element.62), channel_id=1, source_target_pairs={{0,3},{1,0},{2,1},{3,2},{4,7},{5,4},{6,5},{7,6},{8,11},{9,8},{10,9... | collective-permute-start | bytes 786440 | tf_op jit(solution)/shard_map/ppermute | solution.py:509
  77.9 10.9 %collective-permute-start.11 = (bf16[512,256]{1,0:T(8,128)(2,1)S(1)}, bf16[512,256]{1,0:T(8,128)(2,1)S(1)}, u32[]{:S(2)}, u32[]{:S(2)}) collective-permute-start(bf16[512,256]{1,0:T(8,128)(2,1)S(1)} %get-tuple-element.57), channel_id=1, source_target_pairs={{0,1},{1,2},{2,3},{3,0},{4,5},{5,6},{6,7},{7,4},{8,9},{9,10},{10,1... | collective-permute-start | bytes 786440 | tf_op jit(solution)/shard_map/ppermute | solution.py:509
  79.8 9.0 %collective-permute-start.12 = (bf16[512,256]{1,0:T(8,128)(2,1)S(1)}, bf16[512,256]{1,0:T(8,128)(2,1)S(1)}, u32[]{:S(2)}, u32[]{:S(2)}) collective-permute-start(bf16[512,256]{1,0:T(8,128)(2,1)S(1)} %get-tuple-element.58), channel_id=1, source_target_pairs={{0,3},{1,0},{2,1},{3,2},{4,7},{5,4},{6,5},{7,6},{8,11},{9,8},{10,9... | collective-permute-start | bytes 786440 | tf_op jit(solution)/shard_map/ppermute | solution.py:509

commit v2 on v1

--- a/solution.py
+++ b/solution.py
@@ -13,9 +13,9 @@
 STATE = 128
 LEVELS = 8
 BLOCK = 256
+GATE_BLOCK = 512
 F32 = jnp.float32
 BF16 = jnp.bfloat16
-HIGHEST = lax.Precision.HIGHEST
 NT = (((1,), (1,)), ((), ()))
 CHUNKS = ((0, 2), (2, 4))
 SMEM = pl.BlockSpec(memory_space=pltpu.SMEM)
@@ -43,13 +43,19 @@
     return jnp.concatenate([x, x], axis=1)
 
 
-def upper_ones():
+def split(x):
+    high = x.astype(BF16)
+    rest = x - high.astype(F32)
+    middle = rest.astype(BF16)
+    low = (rest - middle.astype(F32)).astype(BF16)
+    return jnp.concatenate([high, middle, low], axis=0)
+
+
+def running_sums(decays):
+    rows = decays.shape[0]
     shape = (STRETCH, STRETCH)
-    return (iota(shape, 0) <= iota(shape, 1)).astype(F32)
-
-
-def running_sums(decays):
-    return jnp.dot(decays, upper_ones(), precision=HIGHEST, preferred_element_type=F32)
+    parts = dot(split(decays), (iota(shape, 0) <= iota(shape, 1)).astype(BF16))
+    return (parts[:rows] + parts[rows : 2 * rows]) + parts[2 * rows :]
 
 
 def lanes(column):
@@ -158,7 +164,9 @@
         at = pl.ds(k * BLOCK, BLOCK)
         if k:
             value_copy(k).wait()
-            v[at, :] = jnp.transpose(dot(tok[...], w_value[:, at]).astype(BF16))
+            for i in range(STEPS):
+                here = pl.ds(i * STRETCH, STRETCH)
+                v[at, here] = jnp.transpose(dot(tok[here, :], w_value[:, at]).astype(BF16))
             states(k - 1)
         else:
             for i in range(STEPS):
@@ -306,39 +314,40 @@
         full[level, pl.ds(pl.multiple_of((1 - core) * half, half), half), :] = peer[source, :]
 
 
+SEND_ORDER = ((2, 0), (1, 1), (2, 1), (3, 0), (1, 0), (3, 1), (0, 0), (0, 1))
+
+
 def gate_kernel(tok, w_level, gate_hbm, out_hbm, gates, weight, w_out, w_gate, sems):
-    blocks = w_gate.shape[1] // BLOCK
+    blocks = w_gate.shape[1] // GATE_BLOCK
+    tp = lax.axis_index("tp")
+    eighth = w_out.shape[1] // len(SEND_ORDER)
 
     def gate_copy(k):
-        at = pl.ds(pl.multiple_of(k * BLOCK, BLOCK), BLOCK)
+        at = pl.ds(k * GATE_BLOCK, GATE_BLOCK)
         return pltpu.make_async_copy(gate_hbm.at[:, at], w_gate.at[:, at], sems.at[k])
 
-    out_copy = pltpu.make_async_copy(out_hbm, w_out, sems.at[blocks])
-    gate_copy(0).start()
-    gate_copy(1).start()
+    def out_copy(j):
+        shift, side = SEND_ORDER[j]
+        source = pl.ds(pl.multiple_of((((tp + shift) & 3) * 2 + side) * eighth, eighth), eighth)
+        return pltpu.make_async_copy(out_hbm.at[:, source], w_out.at[:, pl.ds(j * eighth, eighth)], sems.at[blocks + j])
+
+    for k in range(blocks):
+        gate_copy(k).start()
     cols = w_level.shape[1]
     heads = cols // LEVELS
     to_row, from_col = iota((cols, cols), 0), iota((cols, cols), 1)
     pick = ((to_row % heads) * LEVELS + to_row // heads == from_col).astype(BF16)
     turned = dot_nt(pick, dot(tok[...], w_level[...]).astype(BF16))
     weight[...] = jnp.maximum(turned, 0.0) + jnp.log1p(jnp.exp(-jnp.abs(turned)))
-
-    @pl.loop(0, blocks)
-    def _(k):
+    for k in range(blocks):
         gate_copy(k).wait()
-
-        @pl.when(k + 2 < blocks)
-        def _():
-            gate_copy(k + 2).start()
-
-        @pl.when(k == 1)
-        def _():
-            out_copy.start()
-
-        at = pl.ds(pl.multiple_of(k * BLOCK, BLOCK), BLOCK)
+        if k == 0:
+            for j in range(len(SEND_ORDER)):
+                out_copy(j).start()
+        at = pl.ds(k * GATE_BLOCK, GATE_BLOCK)
         gates[at, :] = jnp.transpose(dot(tok[...], w_gate[:, at]).astype(BF16))
-
-    out_copy.wait()
+    for j in range(len(SEND_ORDER)):
+        out_copy(j).wait()
 
 
 def remote_term(docs, ctx, bit, stretch_doc, weight, here, gone, source, c_out):
@@ -357,14 +366,15 @@
     ctx = lax.axis_index("ctx")
     first = ctx * STEPS
     causal = iota((128, 128), 0) <= iota((128, 128), 1)
-    lower = (iota((STRETCH, STRETCH), 0) >= iota((STRETCH, STRETCH), 1)).astype(F32)
+    lower = (iota((STRETCH, STRETCH), 0) >= iota((STRETCH, STRETCH), 1)).astype(BF16)
     begin = jnp.zeros((heads, STATE), F32)
     previous = begin
     for index in range(STEPS):
         here = pl.ds(index * STRETCH, STRETCH)
         now = decays[:, here]
         cum = running_sums(now)
-        cum_col = lax.dot_general(lower, now, NT, precision=HIGHEST, preferred_element_type=F32)
+        parts = dot_nt(lower, split(now))
+        cum_col = (parts[:, :heads] + parts[:, heads : 2 * heads]) + parts[:, 2 * heads :]
         total = lanes(cum[:, STRETCH - 1 :])
         grown = jnp.exp(cum)
         from_device = jnp.exp(cum + twice(begin))
@@ -433,7 +443,7 @@
     start, count, docs, gain, w_out, sp, gates, ho, weight, e23, e4, *refs
 ):
     far_own, far_peer, plus, minus, keep, own, acc, normed, full = refs
-    ctx, tp = lax.axis_index("ctx"), lax.axis_index("tp")
+    ctx = lax.axis_index("ctx")
     heads = e4.shape[0]
     assemble(ctx & 1, far_own, far_peer, full)
     for j in range(count):
@@ -454,21 +464,9 @@
             power = jnp.sum(gated * gated, axis=0, keepdims=True) * (1.0 / HEAD)
             acc[at, :] = gated * lax.rsqrt(power + 1e-5)
         normed[pl.ds(j * STRETCH, STRETCH), :] = (jnp.transpose(acc[...]) * gain[...]).astype(BF16)
-    quarter = w_out.shape[1] // 8
-
-    def piece(shift, side):
-        col = pl.multiple_of((((tp + shift) & 3) * 2 + side) * quarter, quarter)
-        return dot(normed[...], w_out[:, pl.ds(col, quarter)]).astype(BF16)
-
-    first, second = pl.ds(0, quarter), pl.ds(quarter, quarter)
-    plus[:, first] = piece(2, 0)
-    plus[:, second] = piece(1, 1)
-    minus[:, first] = piece(2, 1)
-    minus[:, second] = piece(3, 0)
-    keep[:, first] = piece(1, 0)
-    keep[:, second] = piece(3, 1)
-    own[:, first] = piece(0, 0)
-    own[:, second] = piece(0, 1)
+    quarter = w_out.shape[1] // 4
+    for j, out in enumerate((plus, minus, keep, own)):
+        out[...] = dot(normed[...], w_out[:, pl.ds(j * quarter, quarter)]).astype(BF16)
 
 
 def finish(start, stop, docs, gain, w_out, *operands):
@@ -520,7 +518,7 @@
         [VMEM] * 2 + [FAR] * 2,
         [((width, rows), BF16), ((heads * LEVELS, rows), F32), (w_out.shape, BF16)],
         (tok, w_level, far(w_gate), far(w_out)),
-        [pltpu.VMEM(w_gate.shape, BF16), pltpu.SemaphoreType.DMA((width // BLOCK + 1,))],
+        [pltpu.VMEM(w_gate.shape, BF16), pltpu.SemaphoreType.DMA((width // GATE_BLOCK + len(SEND_ORDER),))],
         mib=16,
         flops=2 * rows * depth * (width + STATE),
         moved=2 * (rows * depth + depth * width),

time: 91.1 us -> 89.1 us (0.978)
  Pallas kernels: 39.6 us -> 36 us
  waiting for transfers between devices: 23.9 us -> 26 us
    pallas_call x9, Pallas kernels: 39.6 us -> 36 us  [call(): pl.pallas_call(kernel, name=name, in_specs=in_specs, out_specs=[VMEM] * l...]
    ppermute x9, waiting for transfers between devices: 4.54 us -> 5.88 us  [across(): return lax.ppermute(x, 'ctx', [(i, i ^ by) for i in range(32)])]
  transfers between devices with their start and end apart: 17 -> 17, of which waited for: 7 -> 8; matrix products, arithmetic and copies ran while one was open for 1% -> 1% of each run, Pallas kernels for 23% -> 22%
where the time goes in v2:
time: 89.1 us; the launch traced here: 88.1 us
  Pallas kernels  36 us (40%)
  waiting for transfers between devices  26 us (29%)
  starting transfers between devices  24.2 us (27%)
  other arithmetic  1.76 us (2%)
    pallas_call x9, Pallas kernels, call(): pl.pallas_call(kernel, name=name, in_specs=in_specs, out_specs=[VMEM] * l...  36 us
    ppermute x8, waiting for transfers between devices, turn(): return lax.ppermute(x, 'tp', [(i, (i + by) % 4) for i in range(4)])  20.1 us
    ppermute x8, starting transfers between devices, turn(): return lax.ppermute(x, 'tp', [(i, (i + by) % 4) for i in range(4)])  14.2 us
    ppermute x9, starting transfers between devices, across(): return lax.ppermute(x, 'ctx', [(i, i ^ by) for i in range(32)])  9.95 us
    ppermute x9, waiting for transfers between devices, across(): return lax.ppermute(x, 'ctx', [(i, i ^ by) for i in range(32)])  5.88 us
  transfers between devices with their start and end apart: 17, of which 8 were waited for; matrix products, arithmetic and copies ran while one was open for 1% of the time, Pallas kernels for 22%

profile of v2, /device:TPU:0, one launch (start us, length us, event | category | flops | bytes accessed | tf_op | source)
XLA Modules:
  0.0 88.1 jit_solution(590027935172826443)
XLA Ops:
  0.0 10.6 %project.1 = (bf16[1024,2048]{1,0:T(8,128)(2,1)S(1)}, bf16[1024,256]{1,0:T(8,128)(2,1)S(1)}, bf16[1024,1024]{1,0:T(8,128)(2,1)S(1)}, bf16[3,1024,128]{2,1,0:T(8,128)(2,1)S(1)}, bf16[1072,128]{1,0:T(8,128)(2,1)S(1)}) custom-call(s32[128]{0:T(128)} %docs.15, f32[16,1024]{1,0:T(8,128)} %bitcast.2, bf16[1024,2048]{1,0:T(8,128)(2,1)} %tok_hbm.1, ...), custom_call_target="tpu_custom_call" | custom-call | flops 5368709120 | bytes 8388608 | tf_op jit(solution)/shard_map/project/pallas_call | solution.py:82
  10.7 1.5 %collective-permute-done.r0.peer = bf16[1072,128]{1,0:T(8,128)(2,1)S(1)} collective-permute-done((bf16[1072,128]{1,0:T(8,128)(2,1)S(1)}, bf16[1072,128]{1,0:T(8,128)(2,1)S(1)}, u32[]{:S(2)}, u32[]{:S(2)}) %collective-permute-start) | collective-permute-done | bytes 274464 | tf_op jit(solution)/shard_map/ppermute | solution.py:504
  13.0 1.7 %collective-permute-start.1 = (bf16[560,128]{1,0:T(8,128)(2,1)S(1)}, bf16[560,128]{1,0:T(8,128)(2,1)S(1)}, u32[]{:S(2)}, u32[]{:S(2)}) collective-permute-start(bf16[560,128]{1,0:T(8,128)(2,1)S(1)} %get-tuple-element.41.own), channel_id=1, source_target_pairs={{0,8},{4,12},{8,0},{12,4},{16,24},{20,28},{24,16},{28,20},{32,40},... | collective-permute-start | bytes 430088 | tf_op jit(solution)/shard_map/ppermute | solution.py:504
  14.7 2.9 %collective-permute-start.2 = (bf16[560,128]{1,0:T(8,128)(2,1)S(1)}, bf16[560,128]{1,0:T(8,128)(2,1)S(1)}, u32[]{:S(2)}, u32[]{:S(2)}) collective-permute-start(bf16[560,128]{1,0:T(8,128)(2,1)S(1)} %get-tuple-element.41.own), channel_id=1, source_target_pairs={{0,16},{4,20},{8,24},{12,28},{16,0},{20,4},{24,8},{28,12},{32,48},... | collective-permute-start | bytes 430088 | tf_op jit(solution)/shard_map/ppermute | solution.py:504
  17.8 6.5 %gate.1 = (bf16[1024,1024]{1,0:T(8,128)(2,1)S(1)}, f32[128,1024]{1,0:T(8,128)S(1)}, bf16[1024,2048]{1,0:T(8,128)(2,1)S(1)}) custom-call(bf16[1024,2048]{1,0:T(8,128)(2,1)S(1)} %get-tuple-element.30.tok, bf16[2048,128]{1,0:T(8,128)(2,1)S(1)} %copy-done, bf16[2048,1024]{1,0:T(8,128)(2,1)} %gate_hbm.1, bf16[1024,2048]{1,0:T(8,128)(2,1)} %out_hbm.1), custom_call_target="tpu_custom_call" | custom-call | flops 4831838208 | bytes 8388608 | tf_op jit(solution)/shard_map/gate/pallas_call | solution.py:82
  24.6 2.4 %collective-permute-done.3.three = bf16[560,128]{1,0:T(8,128)(2,1)S(1)} collective-permute-done((bf16[560,128]{1,0:T(8,128)(2,1)S(1)}, bf16[560,128]{1,0:T(8,128)(2,1)S(1)}, u32[]{:S(2)}, u32[]{:S(2)}) %collective-permute-start.3) | collective-permute-done | bytes 143392 | tf_op jit(solution)/shard_map/ppermute | solution.py:504
  27.8 1.6 %collective-permute-start.5 = (bf16[560,128]{1,0:T(8,128)(2,1)S(1)}, bf16[560,128]{1,0:T(8,128)(2,1)S(1)}, u32[]{:S(2)}, u32[]{:S(2)}) collective-permute-start(bf16[560,128]{1,0:T(8,128)(2,1)S(1)} %get-tuple-element.44), channel_id=1, source_target_pairs={{0,32},{4,36},{8,40},{12,44},{16,48},{20,52},{24,56},{28,60},{32,0... | collective-permute-start | bytes 430088 | tf_op jit(solution)/shard_map/ppermute | solution.py:504
  29.4 2.7 %collective-permute-start.6 = (bf16[560,128]{1,0:T(8,128)(2,1)S(1)}, bf16[560,128]{1,0:T(8,128)(2,1)S(1)}, u32[]{:S(2)}, u32[]{:S(2)}) collective-permute-start(bf16[560,128]{1,0:T(8,128)(2,1)S(1)} %get-tuple-element.44), channel_id=1, source_target_pairs={{0,64},{4,68},{8,72},{12,76},{16,80},{20,84},{24,88},{28,92},{32,9... | collective-permute-start | bytes 430088 | tf_op jit(solution)/shard_map/ppermute | solution.py:504
  32.6 5.9 %intra.1 = (f32[1024,1024]{1,0:T(8,128)S(1)}, f32[128,1024]{1,0:T(8,128)S(1)}) custom-call(s32[128]{0:T(128)} %docs.15, f32[16]{0:T(128)S(1)} %copy-done.3, f32[128,1024]{1,0:T(8,128)S(1)} %get-tuple-element.34.weight.after, f32[16,1024]{1,0:T(8,128)S(1)} %bitcast.3, bf16[1024,1024]{1,0:T(8,128)(2,1)S(1)} %get-tuple-element.35.v, ...), custom_call_target="tpu_custom_call" | custom-call | flops 6442450944 | bytes 8388608 | tf_op jit(solution)/shard_map/intra/pallas_call | solution.py:82
  38.5 1.7 %collective-permute-done.7.three = bf16[560,128]{1,0:T(8,128)(2,1)S(1)} collective-permute-done((bf16[560,128]{1,0:T(8,128)(2,1)S(1)}, bf16[560,128]{1,0:T(8,128)(2,1)S(1)}, u32[]{:S(2)}, u32[]{:S(2)}) %collective-permute-start.7) | collective-permute-done | bytes 143392 | tf_op jit(solution)/shard_map/ppermute | solution.py:504
  41.3 2.1 %late.1.ho = f32[1024,1024]{1,0:T(8,128)S(1)} custom-call(s32[128]{0:T(128)} %docs.15, bf16[1024,256]{1,0:T(8,128)(2,1)S(1)} %get-tuple-element.32.sp, f32[1024,1024]{1,0:T(8,128)S(1)} %get-tuple-element.38.ho, f32[128,1024]{1,0:T(8,128)S(1)} %get-tuple-element.39.weight.after, f32[16,128]{1,0:T(8,128)S(1)} %get-tuple-element.40.before.e1, ...), custom_call_target="tpu_custom_call" | custom-call | flops 2147483648 | bytes 4194304 | tf_op jit(solution)/shard_map/late/pallas_call | solution.py:82
  43.4 4.3 %finish2.1 = (bf16[512,512]{1,0:T(8,128)(2,1)S(1)}, bf16[512,512]{1,0:T(8,128)(2,1)S(1)}, bf16[512,512]{1,0:T(8,128)(2,1)S(1)}, bf16[512,512]{1,0:T(8,128)(2,1)S(1)}) custom-call(s32[128]{0:T(128)} %docs.15, f32[1,1024]{1,0:T(1,128)S(1)} %bitcast.4, bf16[1024,2048]{1,0:T(8,128)(2,1)S(1)} %get-tuple-element.31.w_out, ...), custom_call_target="tpu_custom_call" | custom-call | flops 4294967296 | bytes 8388608 | tf_op jit(solution)/shard_map/finish2/pallas_call | solution.py:82
  47.7 2.0 %collective-permute-start.14 = (bf16[512,512]{1,0:T(8,128)(2,1)S(1)}, bf16[512,512]{1,0:T(8,128)(2,1)S(1)}, u32[]{:S(2)}, u32[]{:S(2)}) collective-permute-start(bf16[512,512]{1,0:T(8,128)(2,1)S(1)} %get-tuple-element.54), channel_id=1, source_target_pairs={{0,1},{1,2},{2,3},{3,0},{4,5},{5,6},{6,7},{7,4},{8,9},{9,10},{10,1... | collective-permute-start | bytes 1572872 | tf_op jit(solution)/shard_map/ppermute | solution.py:507
  49.7 2.2 %collective-permute-start.13 = (bf16[512,512]{1,0:T(8,128)(2,1)S(1)}, bf16[512,512]{1,0:T(8,128)(2,1)S(1)}, u32[]{:S(2)}, u32[]{:S(2)}) collective-permute-start(bf16[512,512]{1,0:T(8,128)(2,1)S(1)} %get-tuple-element.52), channel_id=1, source_target_pairs={{0,3},{1,0},{2,1},{3,2},{4,7},{5,4},{6,5},{7,6},{8,11},{9,8},{10,9... | collective-permute-start | bytes 1572872 | tf_op jit(solution)/shard_map/ppermute | solution.py:507
  51.9 4.3 %finish0.1 = (bf16[512,512]{1,0:T(8,128)(2,1)S(1)}, bf16[512,512]{1,0:T(8,128)(2,1)S(1)}, bf16[512,512]{1,0:T(8,128)(2,1)S(1)}, bf16[512,512]{1,0:T(8,128)(2,1)S(1)}) custom-call(s32[128]{0:T(128)} %docs.15, f32[1,1024]{1,0:T(1,128)S(1)} %bitcast.5, bf16[1024,2048]{1,0:T(8,128)(2,1)S(1)} %get-tuple-element.31.w_out, ...), custom_call_target="tpu_custom_call" | custom-call | flops 4294967296 | bytes 8388608 | tf_op jit(solution)/shard_map/finish0/pallas_call | solution.py:82
  56.3 3.2 %collective-permute-start.9 = (bf16[512,512]{1,0:T(8,128)(2,1)S(1)}, bf16[512,512]{1,0:T(8,128)(2,1)S(1)}, u32[]{:S(2)}, u32[]{:S(2)}) collective-permute-start(bf16[512,512]{1,0:T(8,128)(2,1)S(1)} %get-tuple-element.48), channel_id=1, source_target_pairs={{0,3},{1,0},{2,1},{3,2},{4,7},{5,4},{6,5},{7,6},{8,11},{9,8},{10,9... | collective-permute-start | bytes 1572872 | tf_op jit(solution)/shard_map/ppermute | solution.py:507
  59.5 5.1 %collective-permute-done.14 = bf16[512,512]{1,0:T(8,128)(2,1)S(1)} collective-permute-done((bf16[512,512]{1,0:T(8,128)(2,1)S(1)}, bf16[512,512]{1,0:T(8,128)(2,1)S(1)}, u32[]{:S(2)}, u32[]{:S(2)}) %collective-permute-start.14) | collective-permute-done | bytes 524320 | tf_op jit(solution)/shard_map/ppermute | solution.py:507
  64.7 1.9 %collective-permute-start.15 = (bf16[512,256]{1,0:T(8,128)(2,1)S(1)}, bf16[512,256]{1,0:T(8,128)(2,1)S(1)}, u32[]{:S(2)}, u32[]{:S(2)}) collective-permute-start(bf16[512,256]{1,0:T(8,128)(2,1)S(1)} %get-tuple-element.61), channel_id=1, source_target_pairs={{0,1},{1,2},{2,3},{3,0},{4,5},{5,6},{6,7},{7,4},{8,9},{9,10},{10,1... | collective-permute-start | bytes 786440 | tf_op jit(solution)/shard_map/ppermute | solution.py:507
  66.6 1.5 %collective-permute-start.16 = (bf16[512,256]{1,0:T(8,128)(2,1)S(1)}, bf16[512,256]{1,0:T(8,128)(2,1)S(1)}, u32[]{:S(2)}, u32[]{:S(2)}) collective-permute-start(bf16[512,256]{1,0:T(8,128)(2,1)S(1)} %get-tuple-element.62), channel_id=1, source_target_pairs={{0,3},{1,0},{2,1},{3,2},{4,7},{5,4},{6,5},{7,6},{8,11},{9,8},{10,9... | collective-permute-start | bytes 786440 | tf_op jit(solution)/shard_map/ppermute | solution.py:507
  68.1 7.7 %collective-permute-done.10 = bf16[512,512]{1,0:T(8,128)(2,1)S(1)} collective-permute-done((bf16[512,512]{1,0:T(8,128)(2,1)S(1)}, bf16[512,512]{1,0:T(8,128)(2,1)S(1)}, u32[]{:S(2)}, u32[]{:S(2)}) %collective-permute-start.10) | collective-permute-done | bytes 524320 | tf_op jit(solution)/shard_map/ppermute | solution.py:507
  75.9 1.9 %collective-permute-start.11 = (bf16[512,256]{1,0:T(8,128)(2,1)S(1)}, bf16[512,256]{1,0:T(8,128)(2,1)S(1)}, u32[]{:S(2)}, u32[]{:S(2)}) collective-permute-start(bf16[512,256]{1,0:T(8,128)(2,1)S(1)} %get-tuple-element.57), channel_id=1, source_target_pairs={{0,1},{1,2},{2,3},{3,0},{4,5},{5,6},{6,7},{7,4},{8,9},{9,10},{10,1... | collective-permute-start | bytes 786440 | tf_op jit(solution)/shard_map/ppermute | solution.py:507
  77.8 1.5 %collective-permute-start.12 = (bf16[512,256]{1,0:T(8,128)(2,1)S(1)}, bf16[512,256]{1,0:T(8,128)(2,1)S(1)}, u32[]{:S(2)}, u32[]{:S(2)}) collective-permute-start(bf16[512,256]{1,0:T(8,128)(2,1)S(1)} %get-tuple-element.58), channel_id=1, source_target_pairs={{0,3},{1,0},{2,1},{3,2},{4,7},{5,4},{6,5},{7,6},{8,11},{9,8},{10,9... | collective-permute-start | bytes 786440 | tf_op jit(solution)/shard_map/ppermute | solution.py:507
  79.3 2.1 %collective-permute-done.15 = bf16[512,256]{1,0:T(8,128)(2,1)S(1)} collective-permute-done((bf16[512,256]{1,0:T(8,128)(2,1)S(1)}, bf16[512,256]{1,0:T(8,128)(2,1)S(1)}, u32[]{:S(2)}, u32[]{:S(2)}) %collective-permute-start.15) | collective-permute-done | bytes 262176 | tf_op jit(solution)/shard_map/ppermute | solution.py:507
  81.6 5.2 %collective-permute-done.11 = bf16[512,256]{1,0:T(8,128)(2,1)S(1)} collective-permute-done((bf16[512,256]{1,0:T(8,128)(2,1)S(1)}, bf16[512,256]{1,0:T(8,128)(2,1)S(1)}, u32[]{:S(2)}, u32[]{:S(2)}) %collective-permute-start.11) | collective-permute-done | bytes 262176 | tf_op jit(solution)/shard_map/ppermute | solution.py:507
  (32 shorter events, 5.4 us)
Async XLA Ops:
  0.0 17.8 %copy-start = (bf16[2048,128]{1,0:T(8,128)(2,1)S(1)}, bf16[2048,128]{1,0:T(8,128)(2,1)}, u32[]{:S(2)}) copy-start(bf16[2048,128]{1,0:T(8,128)(2,1)} %w_level.1) | copy-start | bytes 1572868
  10.6 1.6 %collective-permute-start = (bf16[1072,128]{1,0:T(8,128)(2,1)S(1)}, bf16[1072,128]{1,0:T(8,128)(2,1)S(1)}, u32[]{:S(2)}, u32[]{:S(2)}) collective-permute-start(bf16[1072,128]{1,0:T(8,128)(2,1)S(1)} %get-tuple-element.37.own), channel_id=1, source_target_pairs={{0,4},{4,0},{8,12},{12,8},{16,20},{20,16},{24,28},{28,24},{32,36},... | collective-permute-start | bytes 823304 | tf_op jit(solution)/shard_map/ppermute | solution.py:504
  13.0 11.3 %collective-permute-start.1 = (bf16[560,128]{1,0:T(8,128)(2,1)S(1)}, bf16[560,128]{1,0:T(8,128)(2,1)S(1)}, u32[]{:S(2)}, u32[]{:S(2)}) collective-permute-start(bf16[560,128]{1,0:T(8,128)(2,1)S(1)} %get-tuple-element.41.own), channel_id=1, source_target_pairs={{0,8},{4,12},{8,0},{12,4},{16,24},{20,28},{24,16},{28,20},{32,40},... | collective-permute-start | bytes 430088 | tf_op jit(solution)/shard_map/ppermute | solution.py:504
  14.7 9.9 %collective-permute-start.2 = (bf16[560,128]{1,0:T(8,128)(2,1)S(1)}, bf16[560,128]{1,0:T(8,128)(2,1)S(1)}, u32[]{:S(2)}, u32[]{:S(2)}) collective-permute-start(bf16[560,128]{1,0:T(8,128)(2,1)S(1)} %get-tuple-element.41.own), channel_id=1, source_target_pairs={{0,16},{4,20},{8,24},{12,28},{16,0},{20,4},{24,8},{28,12},{32,48},... | collective-permute-start | bytes 430088 | tf_op jit(solution)/shard_map/ppermute | solution.py:504
  17.6 9.3 %collective-permute-start.3 = (bf16[560,128]{1,0:T(8,128)(2,1)S(1)}, bf16[560,128]{1,0:T(8,128)(2,1)S(1)}, u32[]{:S(2)}, u32[]{:S(2)}) collective-permute-start(bf16[560,128]{1,0:T(8,128)(2,1)S(1)} %get-tuple-element.41.own), channel_id=1, source_target_pairs={{0,24},{4,28},{8,16},{12,20},{16,8},{20,12},{24,0},{28,4},{32,56},... | collective-permute-start | bytes 430088 | tf_op jit(solution)/shard_map/ppermute | solution.py:504
  17.8 14.8 %copy-start.1 = (f32[1024,16]{0,1:T(8,128)S(1)}, f32[1024,16]{0,1:T(8,128)}, u32[]{:S(2)}) copy-start(f32[1024,16]{0,1:T(8,128)} %param.15) | copy-start | bytes 196612
  17.8 14.8 %copy-start.3 = (f32[16]{0:T(128)S(1)}, f32[16]{0:T(128)}, u32[]{:S(2)}) copy-start(f32[16]{0:T(128)} %skip.1) | copy-start | bytes 196
  27.8 10.7 %collective-permute-start.5 = (bf16[560,128]{1,0:T(8,128)(2,1)S(1)}, bf16[560,128]{1,0:T(8,128)(2,1)S(1)}, u32[]{:S(2)}, u32[]{:S(2)}) collective-permute-start(bf16[560,128]{1,0:T(8,128)(2,1)S(1)} %get-tuple-element.44), channel_id=1, source_target_pairs={{0,32},{4,36},{8,40},{12,44},{16,48},{20,52},{24,56},{28,60},{32,0... | collective-permute-start | bytes 430088 | tf_op jit(solution)/shard_map/ppermute | solution.py:504
  29.4 9.1 %collective-permute-start.6 = (bf16[560,128]{1,0:T(8,128)(2,1)S(1)}, bf16[560,128]{1,0:T(8,128)(2,1)S(1)}, u32[]{:S(2)}, u32[]{:S(2)}) collective-permute-start(bf16[560,128]{1,0:T(8,128)(2,1)S(1)} %get-tuple-element.44), channel_id=1, source_target_pairs={{0,64},{4,68},{8,72},{12,76},{16,80},{20,84},{24,88},{28,92},{32,9... | collective-permute-start | bytes 430088 | tf_op jit(solution)/shard_map/ppermute | solution.py:504
  32.1 8.1 %collective-permute-start.7 = (bf16[560,128]{1,0:T(8,128)(2,1)S(1)}, bf16[560,128]{1,0:T(8,128)(2,1)S(1)}, u32[]{:S(2)}, u32[]{:S(2)}) collective-permute-start(bf16[560,128]{1,0:T(8,128)(2,1)S(1)} %get-tuple-element.44), channel_id=1, source_target_pairs={{0,96},{4,100},{8,104},{12,108},{16,112},{20,116},{24,120},{28,124... | collective-permute-start | bytes 430088 | tf_op jit(solution)/shard_map/ppermute | solution.py:504
  32.6 8.7 %collective-permute-start.4 = (bf16[1024,128]{1,0:T(8,128)(2,1)S(1)}, bf16[1024,128]{1,0:T(8,128)(2,1)S(1)}, u32[]{:S(2)}, u32[]{:S(2)}) collective-permute-start(bf16[1024,128]{1,0:T(8,128)(2,1)S(1)} %get-tuple-element.43.own), channel_id=1, source_target_pairs={{0,4},{4,0},{8,12},{12,8},{16,20},{20,16},{24,28},{28,24},{32,36},... | collective-permute-start | bytes 786440 | tf_op jit(solution)/shard_map/ppermute | solution.py:504
  40.9 2.4 %collective-permute-start.8 = (bf16[1024,128]{1,0:T(8,128)(2,1)S(1)}, bf16[1024,128]{1,0:T(8,128)(2,1)S(1)}, u32[]{:S(2)}, u32[]{:S(2)}) collective-permute-start(bf16[1024,128]{1,0:T(8,128)(2,1)S(1)} %get-tuple-element.46.refs_0_), channel_id=1, source_target_pairs={{0,4},{4,0},{8,12},{12,8},{16,20},{20,16},{24,28},{28,24},{32,36},... | collective-permute-start | bytes 786440 | tf_op jit(solution)/shard_map/ppermute | solution.py:504
  41.3 2.1 %copy-start.2 = (f32[1024]{0:T(1024)S(1)}, f32[1024]{0:T(1024)}, u32[]{:S(2)}) copy-start(f32[1024]{0:T(1024)} %param.17) | copy-start | bytes 12292
  47.7 16.9 %collective-permute-start.14 = (bf16[512,512]{1,0:T(8,128)(2,1)S(1)}, bf16[512,512]{1,0:T(8,128)(2,1)S(1)}, u32[]{:S(2)}, u32[]{:S(2)}) collective-permute-start(bf16[512,512]{1,0:T(8,128)(2,1)S(1)} %get-tuple-element.54), channel_id=1, source_target_pairs={{0,1},{1,2},{2,3},{3,0},{4,5},{5,6},{6,7},{7,4},{8,9},{9,10},{10,1... | collective-permute-start | bytes 1572872 | tf_op jit(solution)/shard_map/ppermute | solution.py:507
  49.7 14.9 %collective-permute-start.13 = (bf16[512,512]{1,0:T(8,128)(2,1)S(1)}, bf16[512,512]{1,0:T(8,128)(2,1)S(1)}, u32[]{:S(2)}, u32[]{:S(2)}) collective-permute-start(bf16[512,512]{1,0:T(8,128)(2,1)S(1)} %get-tuple-element.52), channel_id=1, source_target_pairs={{0,3},{1,0},{2,1},{3,2},{4,7},{5,4},{6,5},{7,6},{8,11},{9,8},{10,9... | collective-permute-start | bytes 1572872 | tf_op jit(solution)/shard_map/ppermute | solution.py:507
  56.2 19.6 %collective-permute-start.10 = (bf16[512,512]{1,0:T(8,128)(2,1)S(1)}, bf16[512,512]{1,0:T(8,128)(2,1)S(1)}, u32[]{:S(2)}, u32[]{:S(2)}) collective-permute-start(bf16[512,512]{1,0:T(8,128)(2,1)S(1)} %get-tuple-element.50), channel_id=1, source_target_pairs={{0,1},{1,2},{2,3},{3,0},{4,5},{5,6},{6,7},{7,4},{8,9},{9,10},{10,1... | collective-permute-start | bytes 1572872 | tf_op jit(solution)/shard_map/ppermute | solution.py:507
  56.3 19.5 %collective-permute-start.9 = (bf16[512,512]{1,0:T(8,128)(2,1)S(1)}, bf16[512,512]{1,0:T(8,128)(2,1)S(1)}, u32[]{:S(2)}, u32[]{:S(2)}) collective-permute-start(bf16[512,512]{1,0:T(8,128)(2,1)S(1)} %get-tuple-element.48), channel_id=1, source_target_pairs={{0,3},{1,0},{2,1},{3,2},{4,7},{5,4},{6,5},{7,6},{8,11},{9,8},{10,9... | collective-permute-start | bytes 1572872 | tf_op jit(solution)/shard_map/ppermute | solution.py:507
  64.7 16.7 %collective-permute-start.15 = (bf16[512,256]{1,0:T(8,128)(2,1)S(1)}, bf16[512,256]{1,0:T(8,128)(2,1)S(1)}, u32[]{:S(2)}, u32[]{:S(2)}) collective-permute-start(bf16[512,256]{1,0:T(8,128)(2,1)S(1)} %get-tuple-element.61), channel_id=1, source_target_pairs={{0,1},{1,2},{2,3},{3,0},{4,5},{5,6},{6,7},{7,4},{8,9},{9,10},{10,1... | collective-permute-start | bytes 786440 | tf_op jit(solution)/shard_map/ppermute | solution.py:507
  66.6 14.8 %collective-permute-start.16 = (bf16[512,256]{1,0:T(8,128)(2,1)S(1)}, bf16[512,256]{1,0:T(8,128)(2,1)S(1)}, u32[]{:S(2)}, u32[]{:S(2)}) collective-permute-start(bf16[512,256]{1,0:T(8,128)(2,1)S(1)} %get-tuple-element.62), channel_id=1, source_target_pairs={{0,3},{1,0},{2,1},{3,2},{4,7},{5,4},{6,5},{7,6},{8,11},{9,8},{10,9... | collective-permute-start | bytes 786440 | tf_op jit(solution)/shard_map/ppermute | solution.py:507
  75.9 10.9 %collective-permute-start.11 = (bf16[512,256]{1,0:T(8,128)(2,1)S(1)}, bf16[512,256]{1,0:T(8,128)(2,1)S(1)}, u32[]{:S(2)}, u32[]{:S(2)}) collective-permute-start(bf16[512,256]{1,0:T(8,128)(2,1)S(1)} %get-tuple-element.57), channel_id=1, source_target_pairs={{0,1},{1,2},{2,3},{3,0},{4,5},{5,6},{6,7},{7,4},{8,9},{9,10},{10,1... | collective-permute-start | bytes 786440 | tf_op jit(solution)/shard_map/ppermute | solution.py:507
  77.8 9.0 %collective-permute-start.12 = (bf16[512,256]{1,0:T(8,128)(2,1)S(1)}, bf16[512,256]{1,0:T(8,128)(2,1)S(1)}, u32[]{:S(2)}, u32[]{:S(2)}) collective-permute-start(bf16[512,256]{1,0:T(8,128)(2,1)S(1)} %get-tuple-element.58), channel_id=1, source_target_pairs={{0,3},{1,0},{2,1},{3,2},{4,7},{5,4},{6,5},{7,6},{8,11},{9,8},{10,9... | collective-permute-start | bytes 786440 | tf_op jit(solution)/shard_map/ppermute | solution.py:507

commit v3 on v2

--- a/solution.py
+++ b/solution.py
@@ -17,7 +17,7 @@
 F32 = jnp.float32
 BF16 = jnp.bfloat16
 NT = (((1,), (1,)), ((), ()))
-CHUNKS = ((0, 2), (2, 4))
+CHUNKS = ((0, 2), (2, 3), (3, 4))
 SMEM = pl.BlockSpec(memory_space=pltpu.SMEM)
 VMEM = pl.BlockSpec(memory_space=pltpu.VMEM)
 FAR = pl.BlockSpec(memory_space=pltpu.HBM)
@@ -442,7 +442,7 @@
 def finish_kernel(
     start, count, docs, gain, w_out, sp, gates, ho, weight, e23, e4, *refs
 ):
-    far_own, far_peer, plus, minus, keep, own, acc, normed, full = refs
+    far_own, far_peer, plus, minus, normed, acc, full = refs
     ctx = lax.axis_index("ctx")
     heads = e4.shape[0]
     assemble(ctx & 1, far_own, far_peer, full)
@@ -465,8 +465,29 @@
             acc[at, :] = gated * lax.rsqrt(power + 1e-5)
         normed[pl.ds(j * STRETCH, STRETCH), :] = (jnp.transpose(acc[...]) * gain[...]).astype(BF16)
     quarter = w_out.shape[1] // 4
-    for j, out in enumerate((plus, minus, keep, own)):
+    for j, out in enumerate((plus, minus)):
         out[...] = dot(normed[...], w_out[:, pl.ds(j * quarter, quarter)]).astype(BF16)
+
+
+def stay_kernel(normed, w_out, keep, own):
+    quarter = w_out.shape[1] // 4
+    for j, out in enumerate((keep, own)):
+        out[...] = dot(normed[...], w_out[:, pl.ds((j + 2) * quarter, quarter)]).astype(BF16)
+
+
+def stay(start, normed, w_out):
+    rows, width = normed.shape
+    depth = w_out.shape[1]
+    return call(
+        stay_kernel,
+        f"stay{start}",
+        [VMEM] * 2,
+        [((rows, depth // 4), BF16)] * 2,
+        (normed, w_out),
+        mib=8,
+        flops=rows * depth * width,
+        moved=1 << 20,
+    )
 
 
 def finish(start, stop, docs, gain, w_out, *operands):
@@ -477,15 +498,14 @@
         functools.partial(finish_kernel, start, count),
         f"finish{start}",
         [SMEM] + [VMEM] * (2 + len(operands)),
-        [((rows, depth // 4), BF16)] * 4,
+        [((rows, depth // 4), BF16)] * 2 + [((rows, width), BF16)],
         (docs, gain, w_out, *operands),
         [
             pltpu.VMEM((width, STRETCH), F32),
-            pltpu.VMEM((rows, width), BF16),
             pltpu.VMEM((2, width, STATE), BF16),
         ],
         mib=16,
-        flops=4 * rows * depth * width,
+        flops=2 * rows * depth * width,
         moved=2 * width * depth + 8 * rows * width,
     )
 
@@ -566,10 +586,11 @@
     results = []
     half = w_out.shape[1] // 8
     for lo, hi in CHUNKS:
-        plus, minus, keep, own = finish(
+        plus, minus, normed = finish(
             lo, hi, docs, gain, w_out_near, sp, gates, ho, scaled_weight, e23, e4, far_own, far_peer
         )
         from_below, from_above = turn(plus, 1), turn(minus, 3)
+        keep, own = stay(lo, normed, w_out_near)
         on_plus = (keep[:, :half].astype(F32) + from_below[:, :half].astype(F32)).astype(BF16)
         on_minus = (keep[:, half:].astype(F32) + from_above[:, :half].astype(F32)).astype(BF16)
         last_below, last_above = turn(on_plus, 1), turn(on_minus, 3)

time: 89.1 us -> 86.9 us (0.975)
  waiting for transfers between devices: 26 us -> 18.7 us
  starting transfers between devices: 24.2 us -> 28.7 us
  Pallas kernels: 36 us -> 37.3 us
    ppermute x8 -> x12, waiting for transfers between devices: 20.1 us -> 12.8 us  [turn(): return lax.ppermute(x, 'tp', [(i, (i + by) % 4) for i in range(4)])]
    ppermute x8 -> x12, starting transfers between devices: 14.2 us -> 18.7 us  [turn(): return lax.ppermute(x, 'tp', [(i, (i + by) % 4) for i in range(4)])]
    pallas_call x9 -> x13, Pallas kernels: 36 us -> 37.3 us  [call(): pl.pallas_call(kernel, name=name, in_specs=in_specs, out_specs=[VMEM] * l...]
  transfers between devices with their start and end apart: 17 -> 21, of which waited for: 8 -> 10; matrix products, arithmetic and copies ran while one was open for 1% -> 1% of each run, Pallas kernels for 22% -> 27%
where the time goes in v3:
time: 86.9 us; the launch traced here: 86.7 us
  Pallas kernels  37.3 us (43%)
  starting transfers between devices  28.7 us (33%)
  waiting for transfers between devices  18.7 us (22%)
  other arithmetic  1.7 us (2%)
    pallas_call x13, Pallas kernels, call(): pl.pallas_call(kernel, name=name, in_specs=in_specs, out_specs=[VMEM] * l...  37.3 us
    ppermute x12, starting transfers between devices, turn(): return lax.ppermute(x, 'tp', [(i, (i + by) % 4) for i in range(4)])  18.7 us
    ppermute x12, waiting for transfers between devices, turn(): return lax.ppermute(x, 'tp', [(i, (i + by) % 4) for i in range(4)])  12.8 us
    ppermute x9, starting transfers between devices, across(): return lax.ppermute(x, 'ctx', [(i, i ^ by) for i in range(32)])  9.95 us
    ppermute x9, waiting for transfers between devices, across(): return lax.ppermute(x, 'ctx', [(i, i ^ by) for i in range(32)])  5.9 us
  transfers between devices with their start and end apart: 21, of which 10 were waited for; matrix products, arithmetic and copies ran while one was open for 1% of the time, Pallas kernels for 27%

profile of v3, /device:TPU:0, one launch (start us, length us, event | category | flops | bytes accessed | tf_op | source)
XLA Modules:
  0.0 86.7 jit_solution(4923033795748654709)
XLA Ops:
  0.0 10.6 %project.1 = (bf16[1024,2048]{1,0:T(8,128)(2,1)S(1)}, bf16[1024,256]{1,0:T(8,128)(2,1)S(1)}, bf16[1024,1024]{1,0:T(8,128)(2,1)S(1)}, bf16[3,1024,128]{2,1,0:T(8,128)(2,1)S(1)}, bf16[1072,128]{1,0:T(8,128)(2,1)S(1)}) custom-call(s32[128]{0:T(128)} %docs.17, f32[16,1024]{1,0:T(8,128)} %bitcast.5, bf16[1024,2048]{1,0:T(8,128)(2,1)} %tok_hbm.1, ...), custom_call_target="tpu_custom_call" | custom-call | flops 5368709120 | bytes 8388608 | tf_op jit(solution)/shard_map/project/pallas_call | solution.py:82
  10.7 1.5 %collective-permute-done.r0.peer = bf16[1072,128]{1,0:T(8,128)(2,1)S(1)} collective-permute-done((bf16[1072,128]{1,0:T(8,128)(2,1)S(1)}, bf16[1072,128]{1,0:T(8,128)(2,1)S(1)}, u32[]{:S(2)}, u32[]{:S(2)}) %collective-permute-start) | collective-permute-done | bytes 274464 | tf_op jit(solution)/shard_map/ppermute | solution.py:524
  13.0 1.7 %collective-permute-start.1 = (bf16[560,128]{1,0:T(8,128)(2,1)S(1)}, bf16[560,128]{1,0:T(8,128)(2,1)S(1)}, u32[]{:S(2)}, u32[]{:S(2)}) collective-permute-start(bf16[560,128]{1,0:T(8,128)(2,1)S(1)} %get-tuple-element.48.own), channel_id=1, source_target_pairs={{0,8},{4,12},{8,0},{12,4},{16,24},{20,28},{24,16},{28,20},{32,40},... | collective-permute-start | bytes 430088 | tf_op jit(solution)/shard_map/ppermute | solution.py:524
  14.7 2.9 %collective-permute-start.2 = (bf16[560,128]{1,0:T(8,128)(2,1)S(1)}, bf16[560,128]{1,0:T(8,128)(2,1)S(1)}, u32[]{:S(2)}, u32[]{:S(2)}) collective-permute-start(bf16[560,128]{1,0:T(8,128)(2,1)S(1)} %get-tuple-element.48.own), channel_id=1, source_target_pairs={{0,16},{4,20},{8,24},{12,28},{16,0},{20,4},{24,8},{28,12},{32,48},... | collective-permute-start | bytes 430088 | tf_op jit(solution)/shard_map/ppermute | solution.py:524
  17.7 6.5 %gate.1 = (bf16[1024,1024]{1,0:T(8,128)(2,1)S(1)}, f32[128,1024]{1,0:T(8,128)S(1)}, bf16[1024,2048]{1,0:T(8,128)(2,1)S(1)}) custom-call(bf16[1024,2048]{1,0:T(8,128)(2,1)S(1)} %get-tuple-element.37.tok, bf16[2048,128]{1,0:T(8,128)(2,1)S(1)} %copy-done.1, bf16[2048,1024]{1,0:T(8,128)(2,1)} %gate_hbm.1, bf16[1024,2048]{1,0:T(8,128)(2,1)} %out_hbm.1), custom_call_target="tpu_custom_call" | custom-call | flops 4831838208 | bytes 8388608 | tf_op jit(solution)/shard_map/gate/pallas_call | solution.py:82
  24.6 2.4 %collective-permute-done.3.three = bf16[560,128]{1,0:T(8,128)(2,1)S(1)} collective-permute-done((bf16[560,128]{1,0:T(8,128)(2,1)S(1)}, bf16[560,128]{1,0:T(8,128)(2,1)S(1)}, u32[]{:S(2)}, u32[]{:S(2)}) %collective-permute-start.3) | collective-permute-done | bytes 143392 | tf_op jit(solution)/shard_map/ppermute | solution.py:524
  27.8 1.6 %collective-permute-start.5 = (bf16[560,128]{1,0:T(8,128)(2,1)S(1)}, bf16[560,128]{1,0:T(8,128)(2,1)S(1)}, u32[]{:S(2)}, u32[]{:S(2)}) collective-permute-start(bf16[560,128]{1,0:T(8,128)(2,1)S(1)} %get-tuple-element.51), channel_id=1, source_target_pairs={{0,32},{4,36},{8,40},{12,44},{16,48},{20,52},{24,56},{28,60},{32,0... | collective-permute-start | bytes 430088 | tf_op jit(solution)/shard_map/ppermute | solution.py:524
  29.3 2.7 %collective-permute-start.6 = (bf16[560,128]{1,0:T(8,128)(2,1)S(1)}, bf16[560,128]{1,0:T(8,128)(2,1)S(1)}, u32[]{:S(2)}, u32[]{:S(2)}) collective-permute-start(bf16[560,128]{1,0:T(8,128)(2,1)S(1)} %get-tuple-element.51), channel_id=1, source_target_pairs={{0,64},{4,68},{8,72},{12,76},{16,80},{20,84},{24,88},{28,92},{32,9... | collective-permute-start | bytes 430088 | tf_op jit(solution)/shard_map/ppermute | solution.py:524
  32.6 5.9 %intra.1 = (f32[1024,1024]{1,0:T(8,128)S(1)}, f32[128,1024]{1,0:T(8,128)S(1)}) custom-call(s32[128]{0:T(128)} %docs.17, f32[16]{0:T(128)S(1)} %copy-done.3, f32[128,1024]{1,0:T(8,128)S(1)} %get-tuple-element.41.weight.after, f32[16,1024]{1,0:T(8,128)S(1)} %bitcast.6, bf16[1024,1024]{1,0:T(8,128)(2,1)S(1)} %get-tuple-element.42.v, ...), custom_call_target="tpu_custom_call" | custom-call | flops 6442450944 | bytes 8388608 | tf_op jit(solution)/shard_map/intra/pallas_call | solution.py:82
  38.4 1.7 %collective-permute-done.7.three = bf16[560,128]{1,0:T(8,128)(2,1)S(1)} collective-permute-done((bf16[560,128]{1,0:T(8,128)(2,1)S(1)}, bf16[560,128]{1,0:T(8,128)(2,1)S(1)}, u32[]{:S(2)}, u32[]{:S(2)}) %collective-permute-start.7) | collective-permute-done | bytes 143392 | tf_op jit(solution)/shard_map/ppermute | solution.py:524
  41.3 2.1 %late.1.ho = f32[1024,1024]{1,0:T(8,128)S(1)} custom-call(s32[128]{0:T(128)} %docs.17, bf16[1024,256]{1,0:T(8,128)(2,1)S(1)} %get-tuple-element.39.sp, f32[1024,1024]{1,0:T(8,128)S(1)} %get-tuple-element.45.ho, f32[128,1024]{1,0:T(8,128)S(1)} %get-tuple-element.46.weight.after, f32[16,128]{1,0:T(8,128)S(1)} %get-tuple-element.47.before.e1, ...), custom_call_target="tpu_custom_call" | custom-call | flops 2147483648 | bytes 4194304 | tf_op jit(solution)/shard_map/late/pallas_call | solution.py:82
  43.4 2.1 %finish3.1 = (bf16[256,512]{1,0:T(8,128)(2,1)S(1)}, bf16[256,512]{1,0:T(8,128)(2,1)S(1)}, bf16[256,1024]{1,0:T(8,128)(2,1)S(1)}) custom-call(s32[128]{0:T(128)} %docs.17, f32[1,1024]{1,0:T(1,128)S(1)} %bitcast.2, bf16[1024,2048]{1,0:T(8,128)(2,1)S(1)} %get-tuple-element.38.w_out, bf16[1024,256]{1,0:T(8,128)(2,1)S(1)} %get-tuple-element.39.sp, ...), custom_call_target="tpu_custom_call" | custom-call | flops 1073741824 | bytes 6291456 | tf_op jit(solution)/shard_map/finish3/pallas_call | solution.py:82
  45.4 2.0 %collective-permute-start.18 = (bf16[256,512]{1,0:T(8,128)(2,1)S(1)}, bf16[256,512]{1,0:T(8,128)(2,1)S(1)}, u32[]{:S(2)}, u32[]{:S(2)}) collective-permute-start(bf16[256,512]{1,0:T(8,128)(2,1)S(1)} %get-tuple-element.68), channel_id=1, source_target_pairs={{0,1},{1,2},{2,3},{3,0},{4,5},{5,6},{6,7},{7,4},{8,9},{9,10},{10,1... | collective-permute-start | bytes 786440 | tf_op jit(solution)/shard_map/ppermute | solution.py:527
  47.4 2.2 %collective-permute-start.17 = (bf16[256,512]{1,0:T(8,128)(2,1)S(1)}, bf16[256,512]{1,0:T(8,128)(2,1)S(1)}, u32[]{:S(2)}, u32[]{:S(2)}) collective-permute-start(bf16[256,512]{1,0:T(8,128)(2,1)S(1)} %get-tuple-element.66), channel_id=1, source_target_pairs={{0,3},{1,0},{2,1},{3,2},{4,7},{5,4},{6,5},{7,6},{8,11},{9,8},{10,9... | collective-permute-start | bytes 786440 | tf_op jit(solution)/shard_map/ppermute | solution.py:527
  49.6 2.1 %finish2.1 = (bf16[256,512]{1,0:T(8,128)(2,1)S(1)}, bf16[256,512]{1,0:T(8,128)(2,1)S(1)}, bf16[256,1024]{1,0:T(8,128)(2,1)S(1)}) custom-call(s32[128]{0:T(128)} %docs.17, f32[1,1024]{1,0:T(1,128)S(1)} %bitcast.3, bf16[1024,2048]{1,0:T(8,128)(2,1)S(1)} %get-tuple-element.38.w_out, bf16[1024,256]{1,0:T(8,128)(2,1)S(1)} %get-tuple-element.39.sp, ...), custom_call_target="tpu_custom_call" | custom-call | flops 1073741824 | bytes 6291456 | tf_op jit(solution)/shard_map/finish2/pallas_call | solution.py:82
  51.8 3.2 %collective-permute-start.13 = (bf16[256,512]{1,0:T(8,128)(2,1)S(1)}, bf16[256,512]{1,0:T(8,128)(2,1)S(1)}, u32[]{:S(2)}, u32[]{:S(2)}) collective-permute-start(bf16[256,512]{1,0:T(8,128)(2,1)S(1)} %get-tuple-element.61), channel_id=1, source_target_pairs={{0,3},{1,0},{2,1},{3,2},{4,7},{5,4},{6,5},{7,6},{8,11},{9,8},{10,9... | collective-permute-start | bytes 786440 | tf_op jit(solution)/shard_map/ppermute | solution.py:527
  55.0 3.1 %finish0.1 = (bf16[512,512]{1,0:T(8,128)(2,1)S(1)}, bf16[512,512]{1,0:T(8,128)(2,1)S(1)}, bf16[512,1024]{1,0:T(8,128)(2,1)S(1)}) custom-call(s32[128]{0:T(128)} %docs.17, f32[1,1024]{1,0:T(1,128)S(1)} %bitcast.4, bf16[1024,2048]{1,0:T(8,128)(2,1)S(1)} %get-tuple-element.38.w_out, bf16[1024,256]{1,0:T(8,128)(2,1)S(1)} %get-tuple-element.39.sp, ...), custom_call_target="tpu_custom_call" | custom-call | flops 2147483648 | bytes 8388608 | tf_op jit(solution)/shard_map/finish0/pallas_call | solution.py:82
  58.9 1.2 %stay0.1 = (bf16[512,512]{1,0:T(8,128)(2,1)S(1)}, bf16[512,512]{1,0:T(8,128)(2,1)S(1)}) custom-call(bf16[512,1024]{1,0:T(8,128)(2,1)S(1)} %get-tuple-element.54.normed, bf16[1024,2048]{1,0:T(8,128)(2,1)S(1)} %get-tuple-element.38.w_out), custom_call_target="tpu_custom_call" | custom-call | flops 1073741824 | bytes 1048576 | tf_op jit(solution)/shard_map/stay0/pallas_call | solution.py:82
  60.2 3.3 %collective-permute-start.9 = (bf16[512,512]{1,0:T(8,128)(2,1)S(1)}, bf16[512,512]{1,0:T(8,128)(2,1)S(1)}, u32[]{:S(2)}, u32[]{:S(2)}) collective-permute-start(bf16[512,512]{1,0:T(8,128)(2,1)S(1)} %get-tuple-element.56), channel_id=1, source_target_pairs={{0,3},{1,0},{2,1},{3,2},{4,7},{5,4},{6,5},{7,6},{8,11},{9,8},{10,9... | collective-permute-start | bytes 1572872 | tf_op jit(solution)/shard_map/ppermute | solution.py:527
  64.4 3.2 %collective-permute-start.20 = (bf16[256,256]{1,0:T(8,128)(2,1)S(1)}, bf16[256,256]{1,0:T(8,128)(2,1)S(1)}, u32[]{:S(2)}, u32[]{:S(2)}) collective-permute-start(bf16[256,256]{1,0:T(8,128)(2,1)S(1)} %get-tuple-element.80), channel_id=1, source_target_pairs={{0,3},{1,0},{2,1},{3,2},{4,7},{5,4},{6,5},{7,6},{8,11},{9,8},{10,9... | collective-permute-start | bytes 393224 | tf_op jit(solution)/shard_map/ppermute | solution.py:527
  67.8 6.5 %collective-permute-done.10 = bf16[512,512]{1,0:T(8,128)(2,1)S(1)} collective-permute-done((bf16[512,512]{1,0:T(8,128)(2,1)S(1)}, bf16[512,512]{1,0:T(8,128)(2,1)S(1)}, u32[]{:S(2)}, u32[]{:S(2)}) %collective-permute-start.10) | collective-permute-done | bytes 524320 | tf_op jit(solution)/shard_map/ppermute | solution.py:527
  77.1 2.8 %collective-permute-start.12 = (bf16[512,256]{1,0:T(8,128)(2,1)S(1)}, bf16[512,256]{1,0:T(8,128)(2,1)S(1)}, u32[]{:S(2)}, u32[]{:S(2)}) collective-permute-start(bf16[512,256]{1,0:T(8,128)(2,1)S(1)} %get-tuple-element.72), channel_id=1, source_target_pairs={{0,3},{1,0},{2,1},{3,2},{4,7},{5,4},{6,5},{7,6},{8,11},{9,8},{10,9... | collective-permute-start | bytes 786440 | tf_op jit(solution)/shard_map/ppermute | solution.py:527
  80.0 1.5 %collective-permute-done.16 = bf16[256,256]{1,0:T(8,128)(2,1)S(1)} collective-permute-done((bf16[256,256]{1,0:T(8,128)(2,1)S(1)}, bf16[256,256]{1,0:T(8,128)(2,1)S(1)}, u32[]{:S(2)}, u32[]{:S(2)}) %collective-permute-start.16) | collective-permute-done | bytes 131104 | tf_op jit(solution)/shard_map/ppermute | solution.py:527
  81.6 3.0 %collective-permute-done.11 = bf16[512,256]{1,0:T(8,128)(2,1)S(1)} collective-permute-done((bf16[512,256]{1,0:T(8,128)(2,1)S(1)}, bf16[512,256]{1,0:T(8,128)(2,1)S(1)}, u32[]{:S(2)}, u32[]{:S(2)}) %collective-permute-start.11) | collective-permute-done | bytes 262176 | tf_op jit(solution)/shard_map/ppermute | solution.py:527
  (46 shorter events, 10.6 us)
Async XLA Ops:
  0.0 17.7 %copy-start.1 = (bf16[2048,128]{1,0:T(8,128)(2,1)S(1)}, bf16[2048,128]{1,0:T(8,128)(2,1)}, u32[]{:S(2)}) copy-start(bf16[2048,128]{1,0:T(8,128)(2,1)} %w_level.1) | copy-start | bytes 1572868
  10.6 1.6 %collective-permute-start = (bf16[1072,128]{1,0:T(8,128)(2,1)S(1)}, bf16[1072,128]{1,0:T(8,128)(2,1)S(1)}, u32[]{:S(2)}, u32[]{:S(2)}) collective-permute-start(bf16[1072,128]{1,0:T(8,128)(2,1)S(1)} %get-tuple-element.44.own), channel_id=1, source_target_pairs={{0,4},{4,0},{8,12},{12,8},{16,20},{20,16},{24,28},{28,24},{32,36},... | collective-permute-start | bytes 823304 | tf_op jit(solution)/shard_map/ppermute | solution.py:524
  13.0 11.3 %collective-permute-start.1 = (bf16[560,128]{1,0:T(8,128)(2,1)S(1)}, bf16[560,128]{1,0:T(8,128)(2,1)S(1)}, u32[]{:S(2)}, u32[]{:S(2)}) collective-permute-start(bf16[560,128]{1,0:T(8,128)(2,1)S(1)} %get-tuple-element.48.own), channel_id=1, source_target_pairs={{0,8},{4,12},{8,0},{12,4},{16,24},{20,28},{24,16},{28,20},{32,40},... | collective-permute-start | bytes 430088 | tf_op jit(solution)/shard_map/ppermute | solution.py:524
  14.7 9.9 %collective-permute-start.2 = (bf16[560,128]{1,0:T(8,128)(2,1)S(1)}, bf16[560,128]{1,0:T(8,128)(2,1)S(1)}, u32[]{:S(2)}, u32[]{:S(2)}) collective-permute-start(bf16[560,128]{1,0:T(8,128)(2,1)S(1)} %get-tuple-element.48.own), channel_id=1, source_target_pairs={{0,16},{4,20},{8,24},{12,28},{16,0},{20,4},{24,8},{28,12},{32,48},... | collective-permute-start | bytes 430088 | tf_op jit(solution)/shard_map/ppermute | solution.py:524
  17.6 9.3 %collective-permute-start.3 = (bf16[560,128]{1,0:T(8,128)(2,1)S(1)}, bf16[560,128]{1,0:T(8,128)(2,1)S(1)}, u32[]{:S(2)}, u32[]{:S(2)}) collective-permute-start(bf16[560,128]{1,0:T(8,128)(2,1)S(1)} %get-tuple-element.48.own), channel_id=1, source_target_pairs={{0,24},{4,28},{8,16},{12,20},{16,8},{20,12},{24,0},{28,4},{32,56},... | collective-permute-start | bytes 430088 | tf_op jit(solution)/shard_map/ppermute | solution.py:524
  17.7 14.8 %copy-start.2 = (f32[1024,16]{0,1:T(8,128)S(1)}, f32[1024,16]{0,1:T(8,128)}, u32[]{:S(2)}) copy-start(f32[1024,16]{0,1:T(8,128)} %param.15) | copy-start | bytes 196612
  17.7 14.8 %copy-start.3 = (f32[16]{0:T(128)S(1)}, f32[16]{0:T(128)}, u32[]{:S(2)}) copy-start(f32[16]{0:T(128)} %skip.1) | copy-start | bytes 196
  27.8 10.7 %collective-permute-start.5 = (bf16[560,128]{1,0:T(8,128)(2,1)S(1)}, bf16[560,128]{1,0:T(8,128)(2,1)S(1)}, u32[]{:S(2)}, u32[]{:S(2)}) collective-permute-start(bf16[560,128]{1,0:T(8,128)(2,1)S(1)} %get-tuple-element.51), channel_id=1, source_target_pairs={{0,32},{4,36},{8,40},{12,44},{16,48},{20,52},{24,56},{28,60},{32,0... | collective-permute-start | bytes 430088 | tf_op jit(solution)/shard_map/ppermute | solution.py:524
  29.3 9.1 %collective-permute-start.6 = (bf16[560,128]{1,0:T(8,128)(2,1)S(1)}, bf16[560,128]{1,0:T(8,128)(2,1)S(1)}, u32[]{:S(2)}, u32[]{:S(2)}) collective-permute-start(bf16[560,128]{1,0:T(8,128)(2,1)S(1)} %get-tuple-element.51), channel_id=1, source_target_pairs={{0,64},{4,68},{8,72},{12,76},{16,80},{20,84},{24,88},{28,92},{32,9... | collective-permute-start | bytes 430088 | tf_op jit(solution)/shard_map/ppermute | solution.py:524
  32.1 8.1 %collective-permute-start.7 = (bf16[560,128]{1,0:T(8,128)(2,1)S(1)}, bf16[560,128]{1,0:T(8,128)(2,1)S(1)}, u32[]{:S(2)}, u32[]{:S(2)}) collective-permute-start(bf16[560,128]{1,0:T(8,128)(2,1)S(1)} %get-tuple-element.51), channel_id=1, source_target_pairs={{0,96},{4,100},{8,104},{12,108},{16,112},{20,116},{24,120},{28,124... | collective-permute-start | bytes 430088 | tf_op jit(solution)/shard_map/ppermute | solution.py:524
  32.5 8.7 %collective-permute-start.4 = (bf16[1024,128]{1,0:T(8,128)(2,1)S(1)}, bf16[1024,128]{1,0:T(8,128)(2,1)S(1)}, u32[]{:S(2)}, u32[]{:S(2)}) collective-permute-start(bf16[1024,128]{1,0:T(8,128)(2,1)S(1)} %get-tuple-element.50.own), channel_id=1, source_target_pairs={{0,4},{4,0},{8,12},{12,8},{16,20},{20,16},{24,28},{28,24},{32,36},... | collective-permute-start | bytes 786440 | tf_op jit(solution)/shard_map/ppermute | solution.py:524
  40.9 2.4 %collective-permute-start.8 = (bf16[1024,128]{1,0:T(8,128)(2,1)S(1)}, bf16[1024,128]{1,0:T(8,128)(2,1)S(1)}, u32[]{:S(2)}, u32[]{:S(2)}) collective-permute-start(bf16[1024,128]{1,0:T(8,128)(2,1)S(1)} %get-tuple-element.53.refs_0_), channel_id=1, source_target_pairs={{0,4},{4,0},{8,12},{12,8},{16,20},{20,16},{24,28},{28,24},{32,36},... | collective-permute-start | bytes 786440 | tf_op jit(solution)/shard_map/ppermute | solution.py:524
  45.4 14.8 %collective-permute-start.18 = (bf16[256,512]{1,0:T(8,128)(2,1)S(1)}, bf16[256,512]{1,0:T(8,128)(2,1)S(1)}, u32[]{:S(2)}, u32[]{:S(2)}) collective-permute-start(bf16[256,512]{1,0:T(8,128)(2,1)S(1)} %get-tuple-element.68), channel_id=1, source_target_pairs={{0,1},{1,2},{2,3},{3,0},{4,5},{5,6},{6,7},{7,4},{8,9},{9,10},{10,1... | collective-permute-start | bytes 786440 | tf_op jit(solution)/shard_map/ppermute | solution.py:527
  47.4 16.8 %collective-permute-start.17 = (bf16[256,512]{1,0:T(8,128)(2,1)S(1)}, bf16[256,512]{1,0:T(8,128)(2,1)S(1)}, u32[]{:S(2)}, u32[]{:S(2)}) collective-permute-start(bf16[256,512]{1,0:T(8,128)(2,1)S(1)} %get-tuple-element.66), channel_id=1, source_target_pairs={{0,3},{1,0},{2,1},{3,2},{4,7},{5,4},{6,5},{7,6},{8,11},{9,8},{10,9... | collective-permute-start | bytes 786440 | tf_op jit(solution)/shard_map/ppermute | solution.py:527
  51.7 12.7 %collective-permute-start.14 = (bf16[256,512]{1,0:T(8,128)(2,1)S(1)}, bf16[256,512]{1,0:T(8,128)(2,1)S(1)}, u32[]{:S(2)}, u32[]{:S(2)}) collective-permute-start(bf16[256,512]{1,0:T(8,128)(2,1)S(1)} %get-tuple-element.63), channel_id=1, source_target_pairs={{0,1},{1,2},{2,3},{3,0},{4,5},{5,6},{6,7},{7,4},{8,9},{9,10},{10,1... | collective-permute-start | bytes 786440 | tf_op jit(solution)/shard_map/ppermute | solution.py:527
  51.8 15.8 %collective-permute-start.13 = (bf16[256,512]{1,0:T(8,128)(2,1)S(1)}, bf16[256,512]{1,0:T(8,128)(2,1)S(1)}, u32[]{:S(2)}, u32[]{:S(2)}) collective-permute-start(bf16[256,512]{1,0:T(8,128)(2,1)S(1)} %get-tuple-element.61), channel_id=1, source_target_pairs={{0,3},{1,0},{2,1},{3,2},{4,7},{5,4},{6,5},{7,6},{8,11},{9,8},{10,9... | collective-permute-start | bytes 786440 | tf_op jit(solution)/shard_map/ppermute | solution.py:527
  58.1 16.1 %collective-permute-start.10 = (bf16[512,512]{1,0:T(8,128)(2,1)S(1)}, bf16[512,512]{1,0:T(8,128)(2,1)S(1)}, u32[]{:S(2)}, u32[]{:S(2)}) collective-permute-start(bf16[512,512]{1,0:T(8,128)(2,1)S(1)} %get-tuple-element.58), channel_id=1, source_target_pairs={{0,1},{1,2},{2,3},{3,0},{4,5},{5,6},{6,7},{7,4},{8,9},{9,10},{10,1... | collective-permute-start | bytes 1572872 | tf_op jit(solution)/shard_map/ppermute | solution.py:527
  60.2 15.7 %collective-permute-start.9 = (bf16[512,512]{1,0:T(8,128)(2,1)S(1)}, bf16[512,512]{1,0:T(8,128)(2,1)S(1)}, u32[]{:S(2)}, u32[]{:S(2)}) collective-permute-start(bf16[512,512]{1,0:T(8,128)(2,1)S(1)} %get-tuple-element.56), channel_id=1, source_target_pairs={{0,3},{1,0},{2,1},{3,2},{4,7},{5,4},{6,5},{7,6},{8,11},{9,8},{10,9... | collective-permute-start | bytes 1572872 | tf_op jit(solution)/shard_map/ppermute | solution.py:527
  64.3 12.8 %collective-permute-start.19 = (bf16[256,256]{1,0:T(8,128)(2,1)S(1)}, bf16[256,256]{1,0:T(8,128)(2,1)S(1)}, u32[]{:S(2)}, u32[]{:S(2)}) collective-permute-start(bf16[256,256]{1,0:T(8,128)(2,1)S(1)} %get-tuple-element.79), channel_id=1, source_target_pairs={{0,1},{1,2},{2,3},{3,0},{4,5},{5,6},{6,7},{7,4},{8,9},{9,10},{10,1... | collective-permute-start | bytes 393224 | tf_op jit(solution)/shard_map/ppermute | solution.py:527
  64.4 15.5 %collective-permute-start.20 = (bf16[256,256]{1,0:T(8,128)(2,1)S(1)}, bf16[256,256]{1,0:T(8,128)(2,1)S(1)}, u32[]{:S(2)}, u32[]{:S(2)}) collective-permute-start(bf16[256,256]{1,0:T(8,128)(2,1)S(1)} %get-tuple-element.80), channel_id=1, source_target_pairs={{0,3},{1,0},{2,1},{3,2},{4,7},{5,4},{6,5},{7,6},{8,11},{9,8},{10,9... | collective-permute-start | bytes 393224 | tf_op jit(solution)/shard_map/ppermute | solution.py:527
  67.7 12.3 %collective-permute-start.15 = (bf16[256,256]{1,0:T(8,128)(2,1)S(1)}, bf16[256,256]{1,0:T(8,128)(2,1)S(1)}, u32[]{:S(2)}, u32[]{:S(2)}) collective-permute-start(bf16[256,256]{1,0:T(8,128)(2,1)S(1)} %get-tuple-element.75), channel_id=1, source_target_pairs={{0,1},{1,2},{2,3},{3,0},{4,5},{5,6},{6,7},{7,4},{8,9},{9,10},{10,1... | collective-permute-start | bytes 393224 | tf_op jit(solution)/shard_map/ppermute | solution.py:527
  74.3 7.2 %collective-permute-start.16 = (bf16[256,256]{1,0:T(8,128)(2,1)S(1)}, bf16[256,256]{1,0:T(8,128)(2,1)S(1)}, u32[]{:S(2)}, u32[]{:S(2)}) collective-permute-start(bf16[256,256]{1,0:T(8,128)(2,1)S(1)} %get-tuple-element.76), channel_id=1, source_target_pairs={{0,3},{1,0},{2,1},{3,2},{4,7},{5,4},{6,5},{7,6},{8,11},{9,8},{10,9... | collective-permute-start | bytes 393224 | tf_op jit(solution)/shard_map/ppermute | solution.py:527
  76.0 8.6 %collective-permute-start.11 = (bf16[512,256]{1,0:T(8,128)(2,1)S(1)}, bf16[512,256]{1,0:T(8,128)(2,1)S(1)}, u32[]{:S(2)}, u32[]{:S(2)}) collective-permute-start(bf16[512,256]{1,0:T(8,128)(2,1)S(1)} %get-tuple-element.71), channel_id=1, source_target_pairs={{0,1},{1,2},{2,3},{3,0},{4,5},{5,6},{6,7},{7,4},{8,9},{9,10},{10,1... | collective-permute-start | bytes 786440 | tf_op jit(solution)/shard_map/ppermute | solution.py:527
  77.1 8.3 %collective-permute-start.12 = (bf16[512,256]{1,0:T(8,128)(2,1)S(1)}, bf16[512,256]{1,0:T(8,128)(2,1)S(1)}, u32[]{:S(2)}, u32[]{:S(2)}) collective-permute-start(bf16[512,256]{1,0:T(8,128)(2,1)S(1)} %get-tuple-element.72), channel_id=1, source_target_pairs={{0,3},{1,0},{2,1},{3,2},{4,7},{5,4},{6,5},{7,6},{8,11},{9,8},{10,9... | collective-permute-start | bytes 786440 | tf_op jit(solution)/shard_map/ppermute | solution.py:527
  (1 other events, 2.1 us)

commit v4 on v3

--- a/solution.py
+++ b/solution.py
@@ -12,6 +12,7 @@
 HEAD = 64
 STATE = 128
 LEVELS = 8
+LATE_FROM = 2
 BLOCK = 256
 GATE_BLOCK = 512
 F32 = jnp.float32
@@ -318,6 +319,7 @@
 
 
 def gate_kernel(tok, w_level, gate_hbm, out_hbm, gates, weight, w_out, w_gate, sems):
+    now = pl.ds(STRETCH, tok.shape[0] - STRETCH)
     blocks = w_gate.shape[1] // GATE_BLOCK
     tp = lax.axis_index("tp")
     eighth = w_out.shape[1] // len(SEND_ORDER)
@@ -345,9 +347,15 @@
             for j in range(len(SEND_ORDER)):
                 out_copy(j).start()
         at = pl.ds(k * GATE_BLOCK, GATE_BLOCK)
-        gates[at, :] = jnp.transpose(dot(tok[...], w_gate[:, at]).astype(BF16))
+        gates[at, now] = jnp.transpose(dot(tok[now, :], w_gate[:, at]).astype(BF16))
     for j in range(len(SEND_ORDER)):
         out_copy(j).wait()
+
+
+def first_gate_kernel(tok, w_gate, after, gates):
+    for k in range(w_gate.shape[1] // GATE_BLOCK):
+        at = pl.ds(k * GATE_BLOCK, GATE_BLOCK)
+        gates[at, :] = jnp.transpose(dot(tok[pl.ds(0, STRETCH), :], w_gate[:, at]).astype(BF16))
 
 
 def remote_term(docs, ctx, bit, stretch_doc, weight, here, gone, source, c_out):
@@ -361,7 +369,9 @@
     return dot_nt(source[pl.ds(0, heads * HEAD), :], c_out), rows
 
 
-def intra_kernel(docs, skip, weight, decays, v, sp, local, r0, ho, scaled_weight):
+def intra_kernel(docs, skip, weight, decays, v, sp, local, r0, *refs):
+    late = len(refs) == 3
+    (scaled_weight, _, ho) = refs if late else (refs[1], None, refs[0])
     heads = decays.shape[0]
     ctx = lax.axis_index("ctx")
     first = ctx * STEPS
@@ -369,7 +379,7 @@
     lower = (iota((STRETCH, STRETCH), 0) >= iota((STRETCH, STRETCH), 1)).astype(BF16)
     begin = jnp.zeros((heads, STATE), F32)
     previous = begin
-    for index in range(STEPS):
+    for index in range(1 if late else STEPS):
         here = pl.ds(index * STRETCH, STRETCH)
         now = decays[:, here]
         cum = running_sums(now)
@@ -378,9 +388,13 @@
         total = lanes(cum[:, STRETCH - 1 :])
         grown = jnp.exp(cum)
         from_device = jnp.exp(cum + twice(begin))
-        for level in range(3, LEVELS):
-            rows = pl.ds(level * heads, heads)
-            scaled_weight[rows, here] = weight[rows, here] * from_device
+        if not late:
+            for level in range(3, LEVELS):
+                rows = pl.ds(level * heads, heads)
+                scaled_weight[rows, here] = weight[rows, here] * from_device
+        if not late and index == 0:
+            begin = previous = total
+            continue
         b_in, c_out = sp[here, :STATE], sp[here, STATE:]
         scores = dot_nt(b_in, c_out)
         terms = []
@@ -420,10 +434,11 @@
 
 
 def late_kernel(docs, sp, ho, weight, e1, e23, own, peer, out, full):
+    first = LATE_FROM
     heads = e1.shape[0]
     ctx = lax.axis_index("ctx")
     assemble(ctx & 1, own, peer, full)
-    for index in range(STEPS):
+    for index in range(first, STEPS):
         here = pl.ds(index * STRETCH, STRETCH)
         c_out = sp[here, STATE:]
         stretch_doc = docs[ctx * STEPS + index]
@@ -442,11 +457,16 @@
 def finish_kernel(
     start, count, docs, gain, w_out, sp, gates, ho, weight, e23, e4, *refs
 ):
-    far_own, far_peer, plus, minus, normed, acc, full = refs
+    far_own, far_peer, *before, plus, minus, normed, acc, full = refs[: len(refs) - (1 if len(refs) > 7 else 0)]
+    mid = refs[-1] if before else None
     ctx = lax.axis_index("ctx")
     heads = e4.shape[0]
     assemble(ctx & 1, far_own, far_peer, full)
+    if before:
+        first_gates, first_ho, mid_own, mid_peer, e1 = before
+        assemble(ctx & 1, mid_own, mid_peer, mid)
     for j in range(count):
+        at_first = before and start + j == 0
         here = pl.ds((start + j) * STRETCH, STRETCH)
         c_out = sp[here, STATE:]
         stretch_doc = docs[ctx * STEPS + start + j]
@@ -454,12 +474,17 @@
             remote_term(docs, ctx, bit, stretch_doc, weight, here, gone, full.at[bit - 3], c_out)
             for bit, gone in ((3, e23[pl.ds(heads, heads), :]), (4, e4[...]))
         ]
+        if before:
+            terms += [
+                remote_term(docs, ctx, bit, stretch_doc, weight, here, gone, mid.at[bit - 1], c_out)
+                for bit, gone in ((1, e1[...]), (2, e23[pl.ds(0, heads), :]))
+            ]
         for h in range(heads):
             at = pl.ds(h * HEAD, HEAD)
-            total = ho[at, here]
+            total = first_ho[at, :] if at_first else ho[at, here]
             for cross, rows in terms:
                 total = total + rows[h : h + 1, :] * cross[h * HEAD : (h + 1) * HEAD]
-            g = gates[at, here].astype(F32)
+            g = (first_gates[at, :] if at_first else gates[at, here]).astype(F32)
             gated = total * (g / (1.0 + jnp.exp(-g)))
             power = jnp.sum(gated * gated, axis=0, keepdims=True) * (1.0 / HEAD)
             acc[at, :] = gated * lax.rsqrt(power + 1e-5)
@@ -503,6 +528,7 @@
         [
             pltpu.VMEM((width, STRETCH), F32),
             pltpu.VMEM((2, width, STATE), BF16),
+            *([pltpu.VMEM((2, width, STATE), BF16)] if start < LATE_FROM else []),
         ],
         mib=16,
         flops=2 * rows * depth * width,
@@ -532,13 +558,13 @@
         near_kernel, "near", [SMEM] + [VMEM] * 2, [part, gone], (docs, pay0, peer)
     )
     ys = [across(pay1, by) for by in (4, 2, 6)]
-    gates, weight, w_out_near = call(
+    gates, weight, w_out_near, w_gate_near = call(
         gate_kernel,
         "gate",
         [VMEM] * 2 + [FAR] * 2,
-        [((width, rows), BF16), ((heads * LEVELS, rows), F32), (w_out.shape, BF16)],
+        [((width, rows), BF16), ((heads * LEVELS, rows), F32), (w_out.shape, BF16), (w_gate.shape, BF16)],
         (tok, w_level, far(w_gate), far(w_out)),
-        [pltpu.VMEM(w_gate.shape, BF16), pltpu.SemaphoreType.DMA((width // GATE_BLOCK + len(SEND_ORDER),))],
+        [pltpu.SemaphoreType.DMA((width // GATE_BLOCK + len(SEND_ORDER),))],
         mib=16,
         flops=2 * rows * depth * (width + STATE),
         moved=2 * (rows * depth + depth * width),
@@ -571,7 +597,7 @@
         (docs, x1, x2, x3, e23, scaled_weight),
     )
     far_peer = across(far_own, 1)
-    (ho,) = call(
+    (ho_late,) = call(
         late_kernel,
         "late",
         [SMEM] + [VMEM] * 7,
@@ -583,21 +609,44 @@
         moved=4 << 20,
     )
     gain = norm_gain.reshape(1, -1)
-    results = []
+    results, arrived = {}, None
     half = w_out.shape[1] // 8
-    for lo, hi in CHUNKS:
+    for lo, hi in reversed(CHUNKS):
+        extra = ()
+        if lo < LATE_FROM:
+            (first_gates,) = call(
+                first_gate_kernel,
+                "first_gate",
+                [VMEM] * 3,
+                [((width, STRETCH), BF16)],
+                (tok, w_gate_near, arrived),
+                mib=6,
+                flops=2 * STRETCH * depth * width,
+            )
+            (first_ho,) = call(
+                intra_kernel,
+                "first_intra",
+                [SMEM] * 2 + [VMEM] * 8,
+                [((width, STRETCH), F32)],
+                (docs, skip_weight, weight, decays, v, sp, local, peer, scaled_weight, arrived),
+                mib=8,
+                flops=1 << 30,
+            )
+            extra = (first_gates, first_ho, mid_own, mid_peer, e1)
         plus, minus, normed = finish(
-            lo, hi, docs, gain, w_out_near, sp, gates, ho, scaled_weight, e23, e4, far_own, far_peer
+            lo, hi, docs, gain, w_out_near, sp, gates, ho_late if lo >= LATE_FROM else ho, scaled_weight,
+            e23, e4, far_own, far_peer, *extra,
         )
         from_below, from_above = turn(plus, 1), turn(minus, 3)
+        arrived = from_below if arrived is None else arrived
         keep, own = stay(lo, normed, w_out_near)
         on_plus = (keep[:, :half].astype(F32) + from_below[:, :half].astype(F32)).astype(BF16)
         on_minus = (keep[:, half:].astype(F32) + from_above[:, :half].astype(F32)).astype(BF16)
         last_below, last_above = turn(on_plus, 1), turn(on_minus, 3)
         first = own[:, :half].astype(F32) + from_above[:, half:].astype(F32) + last_below.astype(F32)
         second = own[:, half:].astype(F32) + from_below[:, half:].astype(F32) + last_above.astype(F32)
-        results.append(jnp.concatenate([first, second], axis=1).astype(BF16))
-    return jnp.concatenate(results, axis=0)
+        results[lo] = jnp.concatenate([first, second], axis=1).astype(BF16)
+    return jnp.concatenate([results[lo] for lo, _ in CHUNKS], axis=0)
 
 
 def solution(mesh):

time: 86.9 us -> 90.8 us (1.045)
  Pallas kernels: 37.3 us -> 40.4 us
  waiting for transfers between devices: 18.7 us -> 20.7 us
  starting transfers between devices: 28.7 us -> 27.6 us
    pallas_call x13 -> x15, Pallas kernels: 37.3 us -> 40.4 us  [call(): pl.pallas_call(kernel, name=name, in_specs=in_specs, out_specs=[VMEM] * l...]
    ppermute x12, waiting for transfers between devices: 12.8 us -> 14.3 us  [turn(): return lax.ppermute(x, 'tp', [(i, (i + by) % 4) for i in range(4)])]
    ppermute x12, starting transfers between devices: 18.7 us -> 17.7 us  [turn(): return lax.ppermute(x, 'tp', [(i, (i + by) % 4) for i in range(4)])]
  transfers between devices with their start and end apart: 21 -> 21, of which waited for: 10 -> 10; matrix products, arithmetic and copies ran while one was open for 1% -> 1% of each run, Pallas kernels for 27% -> 29%
where the time goes in v4:
time: 90.8 us; the launch traced here: 90.6 us
  Pallas kernels  40.4 us (44%)
  starting transfers between devices  27.6 us (30%)
  waiting for transfers between devices  20.7 us (23%)
  other arithmetic  1.71 us (2%)
    pallas_call x15, Pallas kernels, call(): pl.pallas_call(kernel, name=name, in_specs=in_specs, out_specs=[VMEM] * l...  40.4 us
    ppermute x12, starting transfers between devices, turn(): return lax.ppermute(x, 'tp', [(i, (i + by) % 4) for i in range(4)])  17.7 us
    ppermute x12, waiting for transfers between devices, turn(): return lax.ppermute(x, 'tp', [(i, (i + by) % 4) for i in range(4)])  14.3 us
    ppermute x9, starting transfers between devices, across(): return lax.ppermute(x, 'ctx', [(i, i ^ by) for i in range(32)])  9.91 us
    ppermute x9, waiting for transfers between devices, across(): return lax.ppermute(x, 'ctx', [(i, i ^ by) for i in range(32)])  6.39 us
  transfers between devices with their start and end apart: 21, of which 10 were waited for; matrix products, arithmetic and copies ran while one was open for 1% of the time, Pallas kernels for 29%

profile of v4, /device:TPU:0, one launch (start us, length us, event | category | flops | bytes accessed | tf_op | source)
XLA Modules:
  0.0 90.6 jit_solution(2003139699456391284)
XLA Ops:
  0.0 10.7 %project.1 = (bf16[1024,2048]{1,0:T(8,128)(2,1)S(1)}, bf16[1024,256]{1,0:T(8,128)(2,1)S(1)}, bf16[1024,1024]{1,0:T(8,128)(2,1)S(1)}, bf16[3,1024,128]{2,1,0:T(8,128)(2,1)S(1)}, bf16[1072,128]{1,0:T(8,128)(2,1)S(1)}) custom-call(s32[128]{0:T(128)} %docs.19, f32[16,1024]{1,0:T(8,128)} %bitcast.2, bf16[1024,2048]{1,0:T(8,128)(2,1)} %tok_hbm.1, ...), custom_call_target="tpu_custom_call" | custom-call | flops 5368709120 | bytes 8388608 | tf_op jit(solution)/shard_map/project/pallas_call | solution.py:83
  10.8 1.5 %collective-permute-done.r0.peer = bf16[1072,128]{1,0:T(8,128)(2,1)S(1)} collective-permute-done((bf16[1072,128]{1,0:T(8,128)(2,1)S(1)}, bf16[1072,128]{1,0:T(8,128)(2,1)S(1)}, u32[]{:S(2)}, u32[]{:S(2)}) %collective-permute-start) | collective-permute-done | bytes 274464 | tf_op jit(solution)/shard_map/ppermute | solution.py:550
  13.1 1.7 %collective-permute-start.1 = (bf16[560,128]{1,0:T(8,128)(2,1)S(1)}, bf16[560,128]{1,0:T(8,128)(2,1)S(1)}, u32[]{:S(2)}, u32[]{:S(2)}) collective-permute-start(bf16[560,128]{1,0:T(8,128)(2,1)S(1)} %get-tuple-element.48.own), channel_id=1, source_target_pairs={{0,8},{4,12},{8,0},{12,4},{16,24},{20,28},{24,16},{28,20},{32,40},... | collective-permute-start | bytes 430088 | tf_op jit(solution)/shard_map/ppermute | solution.py:550
  14.9 2.9 %collective-permute-start.2 = (bf16[560,128]{1,0:T(8,128)(2,1)S(1)}, bf16[560,128]{1,0:T(8,128)(2,1)S(1)}, u32[]{:S(2)}, u32[]{:S(2)}) collective-permute-start(bf16[560,128]{1,0:T(8,128)(2,1)S(1)} %get-tuple-element.48.own), channel_id=1, source_target_pairs={{0,16},{4,20},{8,24},{12,28},{16,0},{20,4},{24,8},{28,12},{32,48},... | collective-permute-start | bytes 430088 | tf_op jit(solution)/shard_map/ppermute | solution.py:550
  17.9 7.3 %gate.1 = (bf16[1024,1024]{1,0:T(8,128)(2,1)S(1)}, f32[128,1024]{1,0:T(8,128)S(1)}, bf16[1024,2048]{1,0:T(8,128)(2,1)S(1)}, bf16[2048,1024]{1,0:T(8,128)(2,1)S(1)}) custom-call(bf16[1024,2048]{1,0:T(8,128)(2,1)S(1)} %get-tuple-element.38.tok, bf16[2048,128]{1,0:T(8,128)(2,1)S(1)} %copy-done.3, bf16[2048,1024]{1,0:T(8,128)(2,1)} %gate_hbm.1, ...), custom_call_target="tpu_custom_call" | custom-call | flops 4831838208 | bytes 8388608 | tf_op jit(solution)/shard_map/gate/pallas_call | solution.py:83
  25.3 1.8 %collective-permute-done.3.three = bf16[560,128]{1,0:T(8,128)(2,1)S(1)} collective-permute-done((bf16[560,128]{1,0:T(8,128)(2,1)S(1)}, bf16[560,128]{1,0:T(8,128)(2,1)S(1)}, u32[]{:S(2)}, u32[]{:S(2)}) %collective-permute-start.3) | collective-permute-done | bytes 143392 | tf_op jit(solution)/shard_map/ppermute | solution.py:550
  27.9 1.8 %collective-permute-start.4 = (bf16[560,128]{1,0:T(8,128)(2,1)S(1)}, bf16[560,128]{1,0:T(8,128)(2,1)S(1)}, u32[]{:S(2)}, u32[]{:S(2)}) collective-permute-start(bf16[560,128]{1,0:T(8,128)(2,1)S(1)} %get-tuple-element.51), channel_id=1, source_target_pairs={{0,32},{4,36},{8,40},{12,44},{16,48},{20,52},{24,56},{28,60},{32,0... | collective-permute-start | bytes 430088 | tf_op jit(solution)/shard_map/ppermute | solution.py:550
  29.7 2.7 %collective-permute-start.5 = (bf16[560,128]{1,0:T(8,128)(2,1)S(1)}, bf16[560,128]{1,0:T(8,128)(2,1)S(1)}, u32[]{:S(2)}, u32[]{:S(2)}) collective-permute-start(bf16[560,128]{1,0:T(8,128)(2,1)S(1)} %get-tuple-element.51), channel_id=1, source_target_pairs={{0,64},{4,68},{8,72},{12,76},{16,80},{20,84},{24,88},{28,92},{32,9... | collective-permute-start | bytes 430088 | tf_op jit(solution)/shard_map/ppermute | solution.py:550
  32.9 4.6 %intra.1 = (f32[1024,1024]{1,0:T(8,128)S(1)}, f32[128,1024]{1,0:T(8,128)S(1)}) custom-call(s32[128]{0:T(128)} %docs.19, f32[16]{0:T(128)S(1)} %copy-done.2, f32[128,1024]{1,0:T(8,128)S(1)} %get-tuple-element.42.weight.after, f32[16,1024]{1,0:T(8,128)S(1)} %bitcast.3, bf16[1024,1024]{1,0:T(8,128)(2,1)S(1)} %get-tuple-element.43.v, ...), custom_call_target="tpu_custom_call" | custom-call | flops 6442450944 | bytes 8388608 | tf_op jit(solution)/shard_map/intra/pallas_call | solution.py:83
  38.6 1.9 %collective-permute-done.6.three = bf16[560,128]{1,0:T(8,128)(2,1)S(1)} collective-permute-done((bf16[560,128]{1,0:T(8,128)(2,1)S(1)}, bf16[560,128]{1,0:T(8,128)(2,1)S(1)}, u32[]{:S(2)}, u32[]{:S(2)}) %collective-permute-start.6) | collective-permute-done | bytes 143392 | tf_op jit(solution)/shard_map/ppermute | solution.py:550
  41.4 1.5 %late.1.ho = f32[1024,1024]{1,0:T(8,128)S(1)} custom-call(s32[128]{0:T(128)} %docs.19, bf16[1024,256]{1,0:T(8,128)(2,1)S(1)} %get-tuple-element.40.sp, f32[1024,1024]{1,0:T(8,128)S(1)} %get-tuple-element.46.ho, f32[128,1024]{1,0:T(8,128)S(1)} %get-tuple-element.47.after.weight.refs_0_, f32[16,128]{1,0:T(8,128)S(1)} %get-tuple-element.49.before.e1.refs_6_, ...), custom_call_target="tpu_custom_call" | custom-call | flops 2147483648 | bytes 4194304 | tf_op jit(solution)/shard_map/late/pallas_call | solution.py:83
  42.9 2.1 %finish3.1 = (bf16[256,512]{1,0:T(8,128)(2,1)S(1)}, bf16[256,512]{1,0:T(8,128)(2,1)S(1)}, bf16[256,1024]{1,0:T(8,128)(2,1)S(1)}) custom-call(s32[128]{0:T(128)} %docs.19, f32[1,1024]{1,0:T(1,128)S(1)} %bitcast.5, bf16[1024,2048]{1,0:T(8,128)(2,1)S(1)} %get-tuple-element.39.w_out, bf16[1024,256]{1,0:T(8,128)(2,1)S(1)} %get-tuple-element.40.sp, ...), custom_call_target="tpu_custom_call" | custom-call | flops 1073741824 | bytes 6291456 | tf_op jit(solution)/shard_map/finish3/pallas_call | solution.py:83
  45.0 2.0 %collective-permute-start.9 = (bf16[256,512]{1,0:T(8,128)(2,1)S(1)}, bf16[256,512]{1,0:T(8,128)(2,1)S(1)}, u32[]{:S(2)}, u32[]{:S(2)}) collective-permute-start(bf16[256,512]{1,0:T(8,128)(2,1)S(1)} %get-tuple-element.56), channel_id=1, source_target_pairs={{0,1},{1,2},{2,3},{3,0},{4,5},{5,6},{6,7},{7,4},{8,9},{9,10},{10,1... | collective-permute-start | bytes 786440 | tf_op jit(solution)/shard_map/ppermute | solution.py:553
  47.0 2.2 %collective-permute-start.18 = (bf16[256,512]{1,0:T(8,128)(2,1)S(1)}, bf16[256,512]{1,0:T(8,128)(2,1)S(1)}, u32[]{:S(2)}, u32[]{:S(2)}) collective-permute-start(bf16[256,512]{1,0:T(8,128)(2,1)S(1)} %get-tuple-element.69), channel_id=1, source_target_pairs={{0,3},{1,0},{2,1},{3,2},{4,7},{5,4},{6,5},{7,6},{8,11},{9,8},{10,9... | collective-permute-start | bytes 786440 | tf_op jit(solution)/shard_map/ppermute | solution.py:553
  49.2 2.1 %finish2.1 = (bf16[256,512]{1,0:T(8,128)(2,1)S(1)}, bf16[256,512]{1,0:T(8,128)(2,1)S(1)}, bf16[256,1024]{1,0:T(8,128)(2,1)S(1)}) custom-call(s32[128]{0:T(128)} %docs.19, f32[1,1024]{1,0:T(1,128)S(1)} %bitcast.6, bf16[1024,2048]{1,0:T(8,128)(2,1)S(1)} %get-tuple-element.39.w_out, bf16[1024,256]{1,0:T(8,128)(2,1)S(1)} %get-tuple-element.40.sp, ...), custom_call_target="tpu_custom_call" | custom-call | flops 1073741824 | bytes 6291456 | tf_op jit(solution)/shard_map/finish2/pallas_call | solution.py:83
  51.4 3.2 %collective-permute-start.14 = (bf16[256,512]{1,0:T(8,128)(2,1)S(1)}, bf16[256,512]{1,0:T(8,128)(2,1)S(1)}, u32[]{:S(2)}, u32[]{:S(2)}) collective-permute-start(bf16[256,512]{1,0:T(8,128)(2,1)S(1)} %get-tuple-element.64), channel_id=1, source_target_pairs={{0,3},{1,0},{2,1},{3,2},{4,7},{5,4},{6,5},{7,6},{8,11},{9,8},{10,9... | collective-permute-start | bytes 786440 | tf_op jit(solution)/shard_map/ppermute | solution.py:553
  56.3 2.0 %first_intra.1.refs_3_ = f32[1024,256]{1,0:T(8,128)S(1)} custom-call(s32[128]{0:T(128)} %docs.19, f32[16]{0:T(128)S(1)} %copy-done.2, f32[128,1024]{1,0:T(8,128)S(1)} %get-tuple-element.42.weight.after, f32[16,1024]{1,0:T(8,128)S(1)} %bitcast.4, bf16[1024,1024]{1,0:T(8,128)(2,1)S(1)} %get-tuple-element.43.v, bf16[1024,256]{1,0:T(8,128)(2,1)S(1)} %get-tuple-element.40.sp, ...), custom_call_target="tpu_custom_call" | custom-call | flops 1073741824 | bytes 1048576 | tf_op jit(solution)/shard_map/first_intra/pallas_call | solution.py:83
  59.6 3.7 %finish0.1 = (bf16[512,512]{1,0:T(8,128)(2,1)S(1)}, bf16[512,512]{1,0:T(8,128)(2,1)S(1)}, bf16[512,1024]{1,0:T(8,128)(2,1)S(1)}) custom-call(s32[128]{0:T(128)} %docs.19, f32[1,1024]{1,0:T(1,128)S(1)} %bitcast.7, bf16[1024,2048]{1,0:T(8,128)(2,1)S(1)} %get-tuple-element.39.w_out, bf16[1024,256]{1,0:T(8,128)(2,1)S(1)} %get-tuple-element.40.sp, ...), custom_call_target="tpu_custom_call" | custom-call | flops 2147483648 | bytes 8388608 | tf_op jit(solution)/shard_map/finish0/pallas_call | solution.py:83
  63.4 3.2 %collective-permute-start.10 = (bf16[512,512]{1,0:T(8,128)(2,1)S(1)}, bf16[512,512]{1,0:T(8,128)(2,1)S(1)}, u32[]{:S(2)}, u32[]{:S(2)}) collective-permute-start(bf16[512,512]{1,0:T(8,128)(2,1)S(1)} %get-tuple-element.59), channel_id=1, source_target_pairs={{0,3},{1,0},{2,1},{3,2},{4,7},{5,4},{6,5},{7,6},{8,11},{9,8},{10,9... | collective-permute-start | bytes 1572872 | tf_op jit(solution)/shard_map/ppermute | solution.py:553
  66.8 3.2 %collective-permute-start.20 = (bf16[256,256]{1,0:T(8,128)(2,1)S(1)}, bf16[256,256]{1,0:T(8,128)(2,1)S(1)}, u32[]{:S(2)}, u32[]{:S(2)}) collective-permute-start(bf16[256,256]{1,0:T(8,128)(2,1)S(1)} %get-tuple-element.82), channel_id=1, source_target_pairs={{0,3},{1,0},{2,1},{3,2},{4,7},{5,4},{6,5},{7,6},{8,11},{9,8},{10,9... | collective-permute-start | bytes 393224 | tf_op jit(solution)/shard_map/ppermute | solution.py:553
  71.4 8.0 %collective-permute-done.11 = bf16[512,512]{1,0:T(8,128)(2,1)S(1)} collective-permute-done((bf16[512,512]{1,0:T(8,128)(2,1)S(1)}, bf16[512,512]{1,0:T(8,128)(2,1)S(1)}, u32[]{:S(2)}, u32[]{:S(2)}) %collective-permute-start.11) | collective-permute-done | bytes 524320 | tf_op jit(solution)/shard_map/ppermute | solution.py:553
  80.4 1.3 %collective-permute-start.12 = (bf16[512,256]{1,0:T(8,128)(2,1)S(1)}, bf16[512,256]{1,0:T(8,128)(2,1)S(1)}, u32[]{:S(2)}, u32[]{:S(2)}) collective-permute-start(bf16[512,256]{1,0:T(8,128)(2,1)S(1)} %get-tuple-element.73), channel_id=1, source_target_pairs={{0,1},{1,2},{2,3},{3,0},{4,5},{5,6},{6,7},{7,4},{8,9},{9,10},{10,1... | collective-permute-start | bytes 786440 | tf_op jit(solution)/shard_map/ppermute | solution.py:553
  82.3 1.4 %collective-permute-start.13 = (bf16[512,256]{1,0:T(8,128)(2,1)S(1)}, bf16[512,256]{1,0:T(8,128)(2,1)S(1)}, u32[]{:S(2)}, u32[]{:S(2)}) collective-permute-start(bf16[512,256]{1,0:T(8,128)(2,1)S(1)} %get-tuple-element.74), channel_id=1, source_target_pairs={{0,3},{1,0},{2,1},{3,2},{4,7},{5,4},{6,5},{7,6},{8,11},{9,8},{10,9... | collective-permute-start | bytes 786440 | tf_op jit(solution)/shard_map/ppermute | solution.py:553
  85.9 3.5 %collective-permute-done.12 = bf16[512,256]{1,0:T(8,128)(2,1)S(1)} collective-permute-done((bf16[512,256]{1,0:T(8,128)(2,1)S(1)}, bf16[512,256]{1,0:T(8,128)(2,1)S(1)}, u32[]{:S(2)}, u32[]{:S(2)}) %collective-permute-start.12) | collective-permute-done | bytes 262176 | tf_op jit(solution)/shard_map/ppermute | solution.py:553
  (48 shorter events, 13.8 us)
Async XLA Ops:
  0.0 17.9 %copy-start.3 = (bf16[2048,128]{1,0:T(8,128)(2,1)S(1)}, bf16[2048,128]{1,0:T(8,128)(2,1)}, u32[]{:S(2)}) copy-start(bf16[2048,128]{1,0:T(8,128)(2,1)} %w_level.1) | copy-start | bytes 1572868
  10.7 1.6 %collective-permute-start = (bf16[1072,128]{1,0:T(8,128)(2,1)S(1)}, bf16[1072,128]{1,0:T(8,128)(2,1)S(1)}, u32[]{:S(2)}, u32[]{:S(2)}) collective-permute-start(bf16[1072,128]{1,0:T(8,128)(2,1)S(1)} %get-tuple-element.45.own), channel_id=1, source_target_pairs={{0,4},{4,0},{8,12},{12,8},{16,20},{20,16},{24,28},{28,24},{32,36},... | collective-permute-start | bytes 823304 | tf_op jit(solution)/shard_map/ppermute | solution.py:550
  13.1 12.1 %collective-permute-start.1 = (bf16[560,128]{1,0:T(8,128)(2,1)S(1)}, bf16[560,128]{1,0:T(8,128)(2,1)S(1)}, u32[]{:S(2)}, u32[]{:S(2)}) collective-permute-start(bf16[560,128]{1,0:T(8,128)(2,1)S(1)} %get-tuple-element.48.own), channel_id=1, source_target_pairs={{0,8},{4,12},{8,0},{12,4},{16,24},{20,28},{24,16},{28,20},{32,40},... | collective-permute-start | bytes 430088 | tf_op jit(solution)/shard_map/ppermute | solution.py:550
  14.9 10.4 %collective-permute-start.2 = (bf16[560,128]{1,0:T(8,128)(2,1)S(1)}, bf16[560,128]{1,0:T(8,128)(2,1)S(1)}, u32[]{:S(2)}, u32[]{:S(2)}) collective-permute-start(bf16[560,128]{1,0:T(8,128)(2,1)S(1)} %get-tuple-element.48.own), channel_id=1, source_target_pairs={{0,16},{4,20},{8,24},{12,28},{16,0},{20,4},{24,8},{28,12},{32,48},... | collective-permute-start | bytes 430088 | tf_op jit(solution)/shard_map/ppermute | solution.py:550
  17.7 9.3 %collective-permute-start.3 = (bf16[560,128]{1,0:T(8,128)(2,1)S(1)}, bf16[560,128]{1,0:T(8,128)(2,1)S(1)}, u32[]{:S(2)}, u32[]{:S(2)}) collective-permute-start(bf16[560,128]{1,0:T(8,128)(2,1)S(1)} %get-tuple-element.48.own), channel_id=1, source_target_pairs={{0,24},{4,28},{8,16},{12,20},{16,8},{20,12},{24,0},{28,4},{32,56},... | collective-permute-start | bytes 430088 | tf_op jit(solution)/shard_map/ppermute | solution.py:550
  17.9 15.0 %copy-start = (f32[1024,16]{0,1:T(8,128)S(1)}, f32[1024,16]{0,1:T(8,128)}, u32[]{:S(2)}) copy-start(f32[1024,16]{0,1:T(8,128)} %param.15) | copy-start | bytes 196612
  17.9 15.0 %copy-start.2 = (f32[16]{0:T(128)S(1)}, f32[16]{0:T(128)}, u32[]{:S(2)}) copy-start(f32[16]{0:T(128)} %skip.3) | copy-start | bytes 196
  27.9 9.5 %collective-permute-start.4 = (bf16[560,128]{1,0:T(8,128)(2,1)S(1)}, bf16[560,128]{1,0:T(8,128)(2,1)S(1)}, u32[]{:S(2)}, u32[]{:S(2)}) collective-permute-start(bf16[560,128]{1,0:T(8,128)(2,1)S(1)} %get-tuple-element.51), channel_id=1, source_target_pairs={{0,32},{4,36},{8,40},{12,44},{16,48},{20,52},{24,56},{28,60},{32,0... | collective-permute-start | bytes 430088 | tf_op jit(solution)/shard_map/ppermute | solution.py:550
  29.7 8.9 %collective-permute-start.5 = (bf16[560,128]{1,0:T(8,128)(2,1)S(1)}, bf16[560,128]{1,0:T(8,128)(2,1)S(1)}, u32[]{:S(2)}, u32[]{:S(2)}) collective-permute-start(bf16[560,128]{1,0:T(8,128)(2,1)S(1)} %get-tuple-element.51), channel_id=1, source_target_pairs={{0,64},{4,68},{8,72},{12,76},{16,80},{20,84},{24,88},{28,92},{32,9... | collective-permute-start | bytes 430088 | tf_op jit(solution)/shard_map/ppermute | solution.py:550
  32.4 8.1 %collective-permute-start.6 = (bf16[560,128]{1,0:T(8,128)(2,1)S(1)}, bf16[560,128]{1,0:T(8,128)(2,1)S(1)}, u32[]{:S(2)}, u32[]{:S(2)}) collective-permute-start(bf16[560,128]{1,0:T(8,128)(2,1)S(1)} %get-tuple-element.51), channel_id=1, source_target_pairs={{0,96},{4,100},{8,104},{12,108},{16,112},{20,116},{24,120},{28,124... | collective-permute-start | bytes 430088 | tf_op jit(solution)/shard_map/ppermute | solution.py:550
  32.9 8.5 %collective-permute-start.8 = (bf16[1024,128]{1,0:T(8,128)(2,1)S(1)}, bf16[1024,128]{1,0:T(8,128)(2,1)S(1)}, u32[]{:S(2)}, u32[]{:S(2)}) collective-permute-start(bf16[1024,128]{1,0:T(8,128)(2,1)S(1)} %get-tuple-element.55.own.refs_4_), channel_id=1, source_target_pairs={{0,4},{4,0},{8,12},{12,8},{16,20},{20,16},{24,28},{28,24},{32,36},... | collective-permute-start | bytes 786440 | tf_op jit(solution)/shard_map/ppermute | solution.py:550
  41.2 1.6 %collective-permute-start.7 = (bf16[1024,128]{1,0:T(8,128)(2,1)S(1)}, bf16[1024,128]{1,0:T(8,128)(2,1)S(1)}, u32[]{:S(2)}, u32[]{:S(2)}) collective-permute-start(bf16[1024,128]{1,0:T(8,128)(2,1)S(1)} %get-tuple-element.53.refs_0_), channel_id=1, source_target_pairs={{0,4},{4,0},{8,12},{12,8},{16,20},{20,16},{24,28},{28,24},{32,36},... | collective-permute-start | bytes 786440 | tf_op jit(solution)/shard_map/ppermute | solution.py:550
  45.0 11.3 %collective-permute-start.9 = (bf16[256,512]{1,0:T(8,128)(2,1)S(1)}, bf16[256,512]{1,0:T(8,128)(2,1)S(1)}, u32[]{:S(2)}, u32[]{:S(2)}) collective-permute-start(bf16[256,512]{1,0:T(8,128)(2,1)S(1)} %get-tuple-element.56), channel_id=1, source_target_pairs={{0,1},{1,2},{2,3},{3,0},{4,5},{5,6},{6,7},{7,4},{8,9},{9,10},{10,1... | collective-permute-start | bytes 786440 | tf_op jit(solution)/shard_map/ppermute | solution.py:553
  47.0 19.6 %collective-permute-start.18 = (bf16[256,512]{1,0:T(8,128)(2,1)S(1)}, bf16[256,512]{1,0:T(8,128)(2,1)S(1)}, u32[]{:S(2)}, u32[]{:S(2)}) collective-permute-start(bf16[256,512]{1,0:T(8,128)(2,1)S(1)} %get-tuple-element.69), channel_id=1, source_target_pairs={{0,3},{1,0},{2,1},{3,2},{4,7},{5,4},{6,5},{7,6},{8,11},{9,8},{10,9... | collective-permute-start | bytes 786440 | tf_op jit(solution)/shard_map/ppermute | solution.py:553
  51.3 15.5 %collective-permute-start.15 = (bf16[256,512]{1,0:T(8,128)(2,1)S(1)}, bf16[256,512]{1,0:T(8,128)(2,1)S(1)}, u32[]{:S(2)}, u32[]{:S(2)}) collective-permute-start(bf16[256,512]{1,0:T(8,128)(2,1)S(1)} %get-tuple-element.66), channel_id=1, source_target_pairs={{0,1},{1,2},{2,3},{3,0},{4,5},{5,6},{6,7},{7,4},{8,9},{9,10},{10,1... | collective-permute-start | bytes 786440 | tf_op jit(solution)/shard_map/ppermute | solution.py:553
  51.4 18.6 %collective-permute-start.14 = (bf16[256,512]{1,0:T(8,128)(2,1)S(1)}, bf16[256,512]{1,0:T(8,128)(2,1)S(1)}, u32[]{:S(2)}, u32[]{:S(2)}) collective-permute-start(bf16[256,512]{1,0:T(8,128)(2,1)S(1)} %get-tuple-element.64), channel_id=1, source_target_pairs={{0,3},{1,0},{2,1},{3,2},{4,7},{5,4},{6,5},{7,6},{8,11},{9,8},{10,9... | collective-permute-start | bytes 786440 | tf_op jit(solution)/shard_map/ppermute | solution.py:553
  63.3 16.1 %collective-permute-start.11 = (bf16[512,512]{1,0:T(8,128)(2,1)S(1)}, bf16[512,512]{1,0:T(8,128)(2,1)S(1)}, u32[]{:S(2)}, u32[]{:S(2)}) collective-permute-start(bf16[512,512]{1,0:T(8,128)(2,1)S(1)} %get-tuple-element.61), channel_id=1, source_target_pairs={{0,1},{1,2},{2,3},{3,0},{4,5},{5,6},{6,7},{7,4},{8,9},{9,10},{10,1... | collective-permute-start | bytes 1572872 | tf_op jit(solution)/shard_map/ppermute | solution.py:553
  63.4 16.8 %collective-permute-start.10 = (bf16[512,512]{1,0:T(8,128)(2,1)S(1)}, bf16[512,512]{1,0:T(8,128)(2,1)S(1)}, u32[]{:S(2)}, u32[]{:S(2)}) collective-permute-start(bf16[512,512]{1,0:T(8,128)(2,1)S(1)} %get-tuple-element.59), channel_id=1, source_target_pairs={{0,3},{1,0},{2,1},{3,2},{4,7},{5,4},{6,5},{7,6},{8,11},{9,8},{10,9... | collective-permute-start | bytes 1572872 | tf_op jit(solution)/shard_map/ppermute | solution.py:553
  66.7 15.5 %collective-permute-start.19 = (bf16[256,256]{1,0:T(8,128)(2,1)S(1)}, bf16[256,256]{1,0:T(8,128)(2,1)S(1)}, u32[]{:S(2)}, u32[]{:S(2)}) collective-permute-start(bf16[256,256]{1,0:T(8,128)(2,1)S(1)} %get-tuple-element.81), channel_id=1, source_target_pairs={{0,1},{1,2},{2,3},{3,0},{4,5},{5,6},{6,7},{7,4},{8,9},{9,10},{10,1... | collective-permute-start | bytes 393224 | tf_op jit(solution)/shard_map/ppermute | solution.py:553
  66.8 16.9 %collective-permute-start.20 = (bf16[256,256]{1,0:T(8,128)(2,1)S(1)}, bf16[256,256]{1,0:T(8,128)(2,1)S(1)}, u32[]{:S(2)}, u32[]{:S(2)}) collective-permute-start(bf16[256,256]{1,0:T(8,128)(2,1)S(1)} %get-tuple-element.82), channel_id=1, source_target_pairs={{0,3},{1,0},{2,1},{3,2},{4,7},{5,4},{6,5},{7,6},{8,11},{9,8},{10,9... | collective-permute-start | bytes 393224 | tf_op jit(solution)/shard_map/ppermute | solution.py:553
  70.1 15.0 %collective-permute-start.16 = (bf16[256,256]{1,0:T(8,128)(2,1)S(1)}, bf16[256,256]{1,0:T(8,128)(2,1)S(1)}, u32[]{:S(2)}, u32[]{:S(2)}) collective-permute-start(bf16[256,256]{1,0:T(8,128)(2,1)S(1)} %get-tuple-element.77), channel_id=1, source_target_pairs={{0,1},{1,2},{2,3},{3,0},{4,5},{5,6},{6,7},{7,4},{8,9},{9,10},{10,1... | collective-permute-start | bytes 393224 | tf_op jit(solution)/shard_map/ppermute | solution.py:553
  79.5 6.3 %collective-permute-start.17 = (bf16[256,256]{1,0:T(8,128)(2,1)S(1)}, bf16[256,256]{1,0:T(8,128)(2,1)S(1)}, u32[]{:S(2)}, u32[]{:S(2)}) collective-permute-start(bf16[256,256]{1,0:T(8,128)(2,1)S(1)} %get-tuple-element.78), channel_id=1, source_target_pairs={{0,3},{1,0},{2,1},{3,2},{4,7},{5,4},{6,5},{7,6},{8,11},{9,8},{10,9... | collective-permute-start | bytes 393224 | tf_op jit(solution)/shard_map/ppermute | solution.py:553
  80.4 9.0 %collective-permute-start.12 = (bf16[512,256]{1,0:T(8,128)(2,1)S(1)}, bf16[512,256]{1,0:T(8,128)(2,1)S(1)}, u32[]{:S(2)}, u32[]{:S(2)}) collective-permute-start(bf16[512,256]{1,0:T(8,128)(2,1)S(1)} %get-tuple-element.73), channel_id=1, source_target_pairs={{0,1},{1,2},{2,3},{3,0},{4,5},{5,6},{6,7},{7,4},{8,9},{9,10},{10,1... | collective-permute-start | bytes 786440 | tf_op jit(solution)/shard_map/ppermute | solution.py:553
  82.3 7.1 %collective-permute-start.13 = (bf16[512,256]{1,0:T(8,128)(2,1)S(1)}, bf16[512,256]{1,0:T(8,128)(2,1)S(1)}, u32[]{:S(2)}, u32[]{:S(2)}) collective-permute-start(bf16[512,256]{1,0:T(8,128)(2,1)S(1)} %get-tuple-element.74), channel_id=1, source_target_pairs={{0,3},{1,0},{2,1},{3,2},{4,7},{5,4},{6,5},{7,6},{8,11},{9,8},{10,9... | collective-permute-start | bytes 786440 | tf_op jit(solution)/shard_map/ppermute | solution.py:553
  (1 other events, 1.5 us)

commit v5 on v3

--- a/solution.py
+++ b/solution.py
@@ -14,6 +14,7 @@
 LEVELS = 8
 BLOCK = 256
 GATE_BLOCK = 512
+LOG2_E = 1.4426950408889634
 F32 = jnp.float32
 BF16 = jnp.bfloat16
 NT = (((1,), (1,)), ((), ()))
@@ -395,13 +396,14 @@
         stretch_doc = docs[first + index]
         crosses.append(remote_term(docs, ctx, 0, stretch_doc, scaled_weight, here, None, r0, c_out))
         own_weight = weight[pl.ds(0, heads), here]
+        cum2, cum_col2 = cum * LOG2_E, cum_col * LOG2_E
         for h in range(heads):
             at = slice(h * HEAD, (h + 1) * HEAD)
-            col = cum_col[:, h : h + 1]
-            row = cum[h : h + 1, :]
+            col = cum_col2[:, h : h + 1]
+            row = cum2[h : h + 1, :]
 
             def block(s, t, masked):
-                decay = jnp.exp(
+                decay = jnp.exp2(
                     jnp.broadcast_to(row[:, t * 128 : t * 128 + 128], (128, 128)) - col[s * 128 : s * 128 + 128, :]
                 )
                 if masked:

time: 86.9 us -> 86.9 us (level)
  no operation moved by 1% of the time
where the time goes in v5:
time: 86.9 us; the launch traced here: 86.7 us
  Pallas kernels  37.3 us (43%)
  starting transfers between devices  28.7 us (33%)
  waiting for transfers between devices  18.7 us (22%)
  other arithmetic  1.7 us (2%)
    pallas_call x13, Pallas kernels, call(): pl.pallas_call(kernel, name=name, in_specs=in_specs, out_specs=[VMEM] * l...  37.3 us
    ppermute x12, starting transfers between devices, turn(): return lax.ppermute(x, 'tp', [(i, (i + by) % 4) for i in range(4)])  18.7 us
    ppermute x12, waiting for transfers between devices, turn(): return lax.ppermute(x, 'tp', [(i, (i + by) % 4) for i in range(4)])  12.8 us
    ppermute x9, starting transfers between devices, across(): return lax.ppermute(x, 'ctx', [(i, i ^ by) for i in range(32)])  9.95 us
    ppermute x9, waiting for transfers between devices, across(): return lax.ppermute(x, 'ctx', [(i, i ^ by) for i in range(32)])  5.89 us
  transfers between devices with their start and end apart: 21, of which 10 were waited for; matrix products, arithmetic and copies ran while one was open for 1% of the time, Pallas kernels for 27%

profile of v5, /device:TPU:0, one launch (start us, length us, event | category | flops | bytes accessed | tf_op | source)
XLA Modules:
  0.0 86.7 jit_solution(12499591159454686116)
XLA Ops:
  0.0 10.6 %project.1 = (bf16[1024,2048]{1,0:T(8,128)(2,1)S(1)}, bf16[1024,256]{1,0:T(8,128)(2,1)S(1)}, bf16[1024,1024]{1,0:T(8,128)(2,1)S(1)}, bf16[3,1024,128]{2,1,0:T(8,128)(2,1)S(1)}, bf16[1072,128]{1,0:T(8,128)(2,1)S(1)}) custom-call(s32[128]{0:T(128)} %docs.17, f32[16,1024]{1,0:T(8,128)} %bitcast.5, bf16[1024,2048]{1,0:T(8,128)(2,1)} %tok_hbm.1, ...), custom_call_target="tpu_custom_call" | custom-call | flops 5368709120 | bytes 8388608 | tf_op jit(solution)/shard_map/project/pallas_call | solution.py:83
  10.7 1.5 %collective-permute-done.r0.peer = bf16[1072,128]{1,0:T(8,128)(2,1)S(1)} collective-permute-done((bf16[1072,128]{1,0:T(8,128)(2,1)S(1)}, bf16[1072,128]{1,0:T(8,128)(2,1)S(1)}, u32[]{:S(2)}, u32[]{:S(2)}) %collective-permute-start) | collective-permute-done | bytes 274464 | tf_op jit(solution)/shard_map/ppermute | solution.py:526
  13.0 1.7 %collective-permute-start.1 = (bf16[560,128]{1,0:T(8,128)(2,1)S(1)}, bf16[560,128]{1,0:T(8,128)(2,1)S(1)}, u32[]{:S(2)}, u32[]{:S(2)}) collective-permute-start(bf16[560,128]{1,0:T(8,128)(2,1)S(1)} %get-tuple-element.48.own), channel_id=1, source_target_pairs={{0,8},{4,12},{8,0},{12,4},{16,24},{20,28},{24,16},{28,20},{32,40},... | collective-permute-start | bytes 430088 | tf_op jit(solution)/shard_map/ppermute | solution.py:526
  14.7 2.9 %collective-permute-start.2 = (bf16[560,128]{1,0:T(8,128)(2,1)S(1)}, bf16[560,128]{1,0:T(8,128)(2,1)S(1)}, u32[]{:S(2)}, u32[]{:S(2)}) collective-permute-start(bf16[560,128]{1,0:T(8,128)(2,1)S(1)} %get-tuple-element.48.own), channel_id=1, source_target_pairs={{0,16},{4,20},{8,24},{12,28},{16,0},{20,4},{24,8},{28,12},{32,48},... | collective-permute-start | bytes 430088 | tf_op jit(solution)/shard_map/ppermute | solution.py:526
  17.7 6.5 %gate.1 = (bf16[1024,1024]{1,0:T(8,128)(2,1)S(1)}, f32[128,1024]{1,0:T(8,128)S(1)}, bf16[1024,2048]{1,0:T(8,128)(2,1)S(1)}) custom-call(bf16[1024,2048]{1,0:T(8,128)(2,1)S(1)} %get-tuple-element.37.tok, bf16[2048,128]{1,0:T(8,128)(2,1)S(1)} %copy-done.1, bf16[2048,1024]{1,0:T(8,128)(2,1)} %gate_hbm.1, bf16[1024,2048]{1,0:T(8,128)(2,1)} %out_hbm.1), custom_call_target="tpu_custom_call" | custom-call | flops 4831838208 | bytes 8388608 | tf_op jit(solution)/shard_map/gate/pallas_call | solution.py:83
  24.6 2.4 %collective-permute-done.3.three = bf16[560,128]{1,0:T(8,128)(2,1)S(1)} collective-permute-done((bf16[560,128]{1,0:T(8,128)(2,1)S(1)}, bf16[560,128]{1,0:T(8,128)(2,1)S(1)}, u32[]{:S(2)}, u32[]{:S(2)}) %collective-permute-start.3) | collective-permute-done | bytes 143392 | tf_op jit(solution)/shard_map/ppermute | solution.py:526
  27.8 1.6 %collective-permute-start.5 = (bf16[560,128]{1,0:T(8,128)(2,1)S(1)}, bf16[560,128]{1,0:T(8,128)(2,1)S(1)}, u32[]{:S(2)}, u32[]{:S(2)}) collective-permute-start(bf16[560,128]{1,0:T(8,128)(2,1)S(1)} %get-tuple-element.51), channel_id=1, source_target_pairs={{0,32},{4,36},{8,40},{12,44},{16,48},{20,52},{24,56},{28,60},{32,0... | collective-permute-start | bytes 430088 | tf_op jit(solution)/shard_map/ppermute | solution.py:526
  29.3 2.7 %collective-permute-start.6 = (bf16[560,128]{1,0:T(8,128)(2,1)S(1)}, bf16[560,128]{1,0:T(8,128)(2,1)S(1)}, u32[]{:S(2)}, u32[]{:S(2)}) collective-permute-start(bf16[560,128]{1,0:T(8,128)(2,1)S(1)} %get-tuple-element.51), channel_id=1, source_target_pairs={{0,64},{4,68},{8,72},{12,76},{16,80},{20,84},{24,88},{28,92},{32,9... | collective-permute-start | bytes 430088 | tf_op jit(solution)/shard_map/ppermute | solution.py:526
  32.6 5.9 %intra.1 = (f32[1024,1024]{1,0:T(8,128)S(1)}, f32[128,1024]{1,0:T(8,128)S(1)}) custom-call(s32[128]{0:T(128)} %docs.17, f32[16]{0:T(128)S(1)} %copy-done.3, f32[128,1024]{1,0:T(8,128)S(1)} %get-tuple-element.41.weight.after, f32[16,1024]{1,0:T(8,128)S(1)} %bitcast.6, bf16[1024,1024]{1,0:T(8,128)(2,1)S(1)} %get-tuple-element.42.v, ...), custom_call_target="tpu_custom_call" | custom-call | flops 6442450944 | bytes 8388608 | tf_op jit(solution)/shard_map/intra/pallas_call | solution.py:83
  38.5 1.7 %collective-permute-done.7.three = bf16[560,128]{1,0:T(8,128)(2,1)S(1)} collective-permute-done((bf16[560,128]{1,0:T(8,128)(2,1)S(1)}, bf16[560,128]{1,0:T(8,128)(2,1)S(1)}, u32[]{:S(2)}, u32[]{:S(2)}) %collective-permute-start.7) | collective-permute-done | bytes 143392 | tf_op jit(solution)/shard_map/ppermute | solution.py:526
  41.3 2.1 %late.1.ho = f32[1024,1024]{1,0:T(8,128)S(1)} custom-call(s32[128]{0:T(128)} %docs.17, bf16[1024,256]{1,0:T(8,128)(2,1)S(1)} %get-tuple-element.39.sp, f32[1024,1024]{1,0:T(8,128)S(1)} %get-tuple-element.45.ho, f32[128,1024]{1,0:T(8,128)S(1)} %get-tuple-element.46.weight.after, f32[16,128]{1,0:T(8,128)S(1)} %get-tuple-element.47.before.e1, ...), custom_call_target="tpu_custom_call" | custom-call | flops 2147483648 | bytes 4194304 | tf_op jit(solution)/shard_map/late/pallas_call | solution.py:83
  43.4 2.1 %finish3.1 = (bf16[256,512]{1,0:T(8,128)(2,1)S(1)}, bf16[256,512]{1,0:T(8,128)(2,1)S(1)}, bf16[256,1024]{1,0:T(8,128)(2,1)S(1)}) custom-call(s32[128]{0:T(128)} %docs.17, f32[1,1024]{1,0:T(1,128)S(1)} %bitcast.2, bf16[1024,2048]{1,0:T(8,128)(2,1)S(1)} %get-tuple-element.38.w_out, bf16[1024,256]{1,0:T(8,128)(2,1)S(1)} %get-tuple-element.39.sp, ...), custom_call_target="tpu_custom_call" | custom-call | flops 1073741824 | bytes 6291456 | tf_op jit(solution)/shard_map/finish3/pallas_call | solution.py:83
  45.4 2.0 %collective-permute-start.18 = (bf16[256,512]{1,0:T(8,128)(2,1)S(1)}, bf16[256,512]{1,0:T(8,128)(2,1)S(1)}, u32[]{:S(2)}, u32[]{:S(2)}) collective-permute-start(bf16[256,512]{1,0:T(8,128)(2,1)S(1)} %get-tuple-element.68), channel_id=1, source_target_pairs={{0,1},{1,2},{2,3},{3,0},{4,5},{5,6},{6,7},{7,4},{8,9},{9,10},{10,1... | collective-permute-start | bytes 786440 | tf_op jit(solution)/shard_map/ppermute | solution.py:529
  47.4 2.2 %collective-permute-start.17 = (bf16[256,512]{1,0:T(8,128)(2,1)S(1)}, bf16[256,512]{1,0:T(8,128)(2,1)S(1)}, u32[]{:S(2)}, u32[]{:S(2)}) collective-permute-start(bf16[256,512]{1,0:T(8,128)(2,1)S(1)} %get-tuple-element.66), channel_id=1, source_target_pairs={{0,3},{1,0},{2,1},{3,2},{4,7},{5,4},{6,5},{7,6},{8,11},{9,8},{10,9... | collective-permute-start | bytes 786440 | tf_op jit(solution)/shard_map/ppermute | solution.py:529
  49.6 2.1 %finish2.1 = (bf16[256,512]{1,0:T(8,128)(2,1)S(1)}, bf16[256,512]{1,0:T(8,128)(2,1)S(1)}, bf16[256,1024]{1,0:T(8,128)(2,1)S(1)}) custom-call(s32[128]{0:T(128)} %docs.17, f32[1,1024]{1,0:T(1,128)S(1)} %bitcast.3, bf16[1024,2048]{1,0:T(8,128)(2,1)S(1)} %get-tuple-element.38.w_out, bf16[1024,256]{1,0:T(8,128)(2,1)S(1)} %get-tuple-element.39.sp, ...), custom_call_target="tpu_custom_call" | custom-call | flops 1073741824 | bytes 6291456 | tf_op jit(solution)/shard_map/finish2/pallas_call | solution.py:83
  51.8 3.2 %collective-permute-start.13 = (bf16[256,512]{1,0:T(8,128)(2,1)S(1)}, bf16[256,512]{1,0:T(8,128)(2,1)S(1)}, u32[]{:S(2)}, u32[]{:S(2)}) collective-permute-start(bf16[256,512]{1,0:T(8,128)(2,1)S(1)} %get-tuple-element.61), channel_id=1, source_target_pairs={{0,3},{1,0},{2,1},{3,2},{4,7},{5,4},{6,5},{7,6},{8,11},{9,8},{10,9... | collective-permute-start | bytes 786440 | tf_op jit(solution)/shard_map/ppermute | solution.py:529
  55.0 3.1 %finish0.1 = (bf16[512,512]{1,0:T(8,128)(2,1)S(1)}, bf16[512,512]{1,0:T(8,128)(2,1)S(1)}, bf16[512,1024]{1,0:T(8,128)(2,1)S(1)}) custom-call(s32[128]{0:T(128)} %docs.17, f32[1,1024]{1,0:T(1,128)S(1)} %bitcast.4, bf16[1024,2048]{1,0:T(8,128)(2,1)S(1)} %get-tuple-element.38.w_out, bf16[1024,256]{1,0:T(8,128)(2,1)S(1)} %get-tuple-element.39.sp, ...), custom_call_target="tpu_custom_call" | custom-call | flops 2147483648 | bytes 8388608 | tf_op jit(solution)/shard_map/finish0/pallas_call | solution.py:83
  58.9 1.2 %stay0.1 = (bf16[512,512]{1,0:T(8,128)(2,1)S(1)}, bf16[512,512]{1,0:T(8,128)(2,1)S(1)}) custom-call(bf16[512,1024]{1,0:T(8,128)(2,1)S(1)} %get-tuple-element.54.normed, bf16[1024,2048]{1,0:T(8,128)(2,1)S(1)} %get-tuple-element.38.w_out), custom_call_target="tpu_custom_call" | custom-call | flops 1073741824 | bytes 1048576 | tf_op jit(solution)/shard_map/stay0/pallas_call | solution.py:83
  60.2 3.3 %collective-permute-start.9 = (bf16[512,512]{1,0:T(8,128)(2,1)S(1)}, bf16[512,512]{1,0:T(8,128)(2,1)S(1)}, u32[]{:S(2)}, u32[]{:S(2)}) collective-permute-start(bf16[512,512]{1,0:T(8,128)(2,1)S(1)} %get-tuple-element.56), channel_id=1, source_target_pairs={{0,3},{1,0},{2,1},{3,2},{4,7},{5,4},{6,5},{7,6},{8,11},{9,8},{10,9... | collective-permute-start | bytes 1572872 | tf_op jit(solution)/shard_map/ppermute | solution.py:529
  64.4 3.2 %collective-permute-start.20 = (bf16[256,256]{1,0:T(8,128)(2,1)S(1)}, bf16[256,256]{1,0:T(8,128)(2,1)S(1)}, u32[]{:S(2)}, u32[]{:S(2)}) collective-permute-start(bf16[256,256]{1,0:T(8,128)(2,1)S(1)} %get-tuple-element.80), channel_id=1, source_target_pairs={{0,3},{1,0},{2,1},{3,2},{4,7},{5,4},{6,5},{7,6},{8,11},{9,8},{10,9... | collective-permute-start | bytes 393224 | tf_op jit(solution)/shard_map/ppermute | solution.py:529
  67.8 6.5 %collective-permute-done.10 = bf16[512,512]{1,0:T(8,128)(2,1)S(1)} collective-permute-done((bf16[512,512]{1,0:T(8,128)(2,1)S(1)}, bf16[512,512]{1,0:T(8,128)(2,1)S(1)}, u32[]{:S(2)}, u32[]{:S(2)}) %collective-permute-start.10) | collective-permute-done | bytes 524320 | tf_op jit(solution)/shard_map/ppermute | solution.py:529
  77.1 2.8 %collective-permute-start.12 = (bf16[512,256]{1,0:T(8,128)(2,1)S(1)}, bf16[512,256]{1,0:T(8,128)(2,1)S(1)}, u32[]{:S(2)}, u32[]{:S(2)}) collective-permute-start(bf16[512,256]{1,0:T(8,128)(2,1)S(1)} %get-tuple-element.72), channel_id=1, source_target_pairs={{0,3},{1,0},{2,1},{3,2},{4,7},{5,4},{6,5},{7,6},{8,11},{9,8},{10,9... | collective-permute-start | bytes 786440 | tf_op jit(solution)/shard_map/ppermute | solution.py:529
  80.0 1.5 %collective-permute-done.16 = bf16[256,256]{1,0:T(8,128)(2,1)S(1)} collective-permute-done((bf16[256,256]{1,0:T(8,128)(2,1)S(1)}, bf16[256,256]{1,0:T(8,128)(2,1)S(1)}, u32[]{:S(2)}, u32[]{:S(2)}) %collective-permute-start.16) | collective-permute-done | bytes 131104 | tf_op jit(solution)/shard_map/ppermute | solution.py:529
  81.6 3.0 %collective-permute-done.11 = bf16[512,256]{1,0:T(8,128)(2,1)S(1)} collective-permute-done((bf16[512,256]{1,0:T(8,128)(2,1)S(1)}, bf16[512,256]{1,0:T(8,128)(2,1)S(1)}, u32[]{:S(2)}, u32[]{:S(2)}) %collective-permute-start.11) | collective-permute-done | bytes 262176 | tf_op jit(solution)/shard_map/ppermute | solution.py:529
  (46 shorter events, 10.6 us)
Async XLA Ops:
  0.0 17.7 %copy-start.1 = (bf16[2048,128]{1,0:T(8,128)(2,1)S(1)}, bf16[2048,128]{1,0:T(8,128)(2,1)}, u32[]{:S(2)}) copy-start(bf16[2048,128]{1,0:T(8,128)(2,1)} %w_level.1) | copy-start | bytes 1572868
  10.6 1.6 %collective-permute-start = (bf16[1072,128]{1,0:T(8,128)(2,1)S(1)}, bf16[1072,128]{1,0:T(8,128)(2,1)S(1)}, u32[]{:S(2)}, u32[]{:S(2)}) collective-permute-start(bf16[1072,128]{1,0:T(8,128)(2,1)S(1)} %get-tuple-element.44.own), channel_id=1, source_target_pairs={{0,4},{4,0},{8,12},{12,8},{16,20},{20,16},{24,28},{28,24},{32,36},... | collective-permute-start | bytes 823304 | tf_op jit(solution)/shard_map/ppermute | solution.py:526
  13.0 11.3 %collective-permute-start.1 = (bf16[560,128]{1,0:T(8,128)(2,1)S(1)}, bf16[560,128]{1,0:T(8,128)(2,1)S(1)}, u32[]{:S(2)}, u32[]{:S(2)}) collective-permute-start(bf16[560,128]{1,0:T(8,128)(2,1)S(1)} %get-tuple-element.48.own), channel_id=1, source_target_pairs={{0,8},{4,12},{8,0},{12,4},{16,24},{20,28},{24,16},{28,20},{32,40},... | collective-permute-start | bytes 430088 | tf_op jit(solution)/shard_map/ppermute | solution.py:526
  14.7 9.9 %collective-permute-start.2 = (bf16[560,128]{1,0:T(8,128)(2,1)S(1)}, bf16[560,128]{1,0:T(8,128)(2,1)S(1)}, u32[]{:S(2)}, u32[]{:S(2)}) collective-permute-start(bf16[560,128]{1,0:T(8,128)(2,1)S(1)} %get-tuple-element.48.own), channel_id=1, source_target_pairs={{0,16},{4,20},{8,24},{12,28},{16,0},{20,4},{24,8},{28,12},{32,48},... | collective-permute-start | bytes 430088 | tf_op jit(solution)/shard_map/ppermute | solution.py:526
  17.6 9.3 %collective-permute-start.3 = (bf16[560,128]{1,0:T(8,128)(2,1)S(1)}, bf16[560,128]{1,0:T(8,128)(2,1)S(1)}, u32[]{:S(2)}, u32[]{:S(2)}) collective-permute-start(bf16[560,128]{1,0:T(8,128)(2,1)S(1)} %get-tuple-element.48.own), channel_id=1, source_target_pairs={{0,24},{4,28},{8,16},{12,20},{16,8},{20,12},{24,0},{28,4},{32,56},... | collective-permute-start | bytes 430088 | tf_op jit(solution)/shard_map/ppermute | solution.py:526
  17.7 14.8 %copy-start.2 = (f32[1024,16]{0,1:T(8,128)S(1)}, f32[1024,16]{0,1:T(8,128)}, u32[]{:S(2)}) copy-start(f32[1024,16]{0,1:T(8,128)} %param.15) | copy-start | bytes 196612
  17.7 14.8 %copy-start.3 = (f32[16]{0:T(128)S(1)}, f32[16]{0:T(128)}, u32[]{:S(2)}) copy-start(f32[16]{0:T(128)} %skip.1) | copy-start | bytes 196
  27.8 10.7 %collective-permute-start.5 = (bf16[560,128]{1,0:T(8,128)(2,1)S(1)}, bf16[560,128]{1,0:T(8,128)(2,1)S(1)}, u32[]{:S(2)}, u32[]{:S(2)}) collective-permute-start(bf16[560,128]{1,0:T(8,128)(2,1)S(1)} %get-tuple-element.51), channel_id=1, source_target_pairs={{0,32},{4,36},{8,40},{12,44},{16,48},{20,52},{24,56},{28,60},{32,0... | collective-permute-start | bytes 430088 | tf_op jit(solution)/shard_map/ppermute | solution.py:526
  29.3 9.1 %collective-permute-start.6 = (bf16[560,128]{1,0:T(8,128)(2,1)S(1)}, bf16[560,128]{1,0:T(8,128)(2,1)S(1)}, u32[]{:S(2)}, u32[]{:S(2)}) collective-permute-start(bf16[560,128]{1,0:T(8,128)(2,1)S(1)} %get-tuple-element.51), channel_id=1, source_target_pairs={{0,64},{4,68},{8,72},{12,76},{16,80},{20,84},{24,88},{28,92},{32,9... | collective-permute-start | bytes 430088 | tf_op jit(solution)/shard_map/ppermute | solution.py:526
  32.1 8.1 %collective-permute-start.7 = (bf16[560,128]{1,0:T(8,128)(2,1)S(1)}, bf16[560,128]{1,0:T(8,128)(2,1)S(1)}, u32[]{:S(2)}, u32[]{:S(2)}) collective-permute-start(bf16[560,128]{1,0:T(8,128)(2,1)S(1)} %get-tuple-element.51), channel_id=1, source_target_pairs={{0,96},{4,100},{8,104},{12,108},{16,112},{20,116},{24,120},{28,124... | collective-permute-start | bytes 430088 | tf_op jit(solution)/shard_map/ppermute | solution.py:526
  32.5 8.7 %collective-permute-start.4 = (bf16[1024,128]{1,0:T(8,128)(2,1)S(1)}, bf16[1024,128]{1,0:T(8,128)(2,1)S(1)}, u32[]{:S(2)}, u32[]{:S(2)}) collective-permute-start(bf16[1024,128]{1,0:T(8,128)(2,1)S(1)} %get-tuple-element.50.own), channel_id=1, source_target_pairs={{0,4},{4,0},{8,12},{12,8},{16,20},{20,16},{24,28},{28,24},{32,36},... | collective-permute-start | bytes 786440 | tf_op jit(solution)/shard_map/ppermute | solution.py:526
  40.9 2.4 %collective-permute-start.8 = (bf16[1024,128]{1,0:T(8,128)(2,1)S(1)}, bf16[1024,128]{1,0:T(8,128)(2,1)S(1)}, u32[]{:S(2)}, u32[]{:S(2)}) collective-permute-start(bf16[1024,128]{1,0:T(8,128)(2,1)S(1)} %get-tuple-element.53.refs_0_), channel_id=1, source_target_pairs={{0,4},{4,0},{8,12},{12,8},{16,20},{20,16},{24,28},{28,24},{32,36},... | collective-permute-start | bytes 786440 | tf_op jit(solution)/shard_map/ppermute | solution.py:526
  45.4 14.8 %collective-permute-start.18 = (bf16[256,512]{1,0:T(8,128)(2,1)S(1)}, bf16[256,512]{1,0:T(8,128)(2,1)S(1)}, u32[]{:S(2)}, u32[]{:S(2)}) collective-permute-start(bf16[256,512]{1,0:T(8,128)(2,1)S(1)} %get-tuple-element.68), channel_id=1, source_target_pairs={{0,1},{1,2},{2,3},{3,0},{4,5},{5,6},{6,7},{7,4},{8,9},{9,10},{10,1... | collective-permute-start | bytes 786440 | tf_op jit(solution)/shard_map/ppermute | solution.py:529
  47.4 16.8 %collective-permute-start.17 = (bf16[256,512]{1,0:T(8,128)(2,1)S(1)}, bf16[256,512]{1,0:T(8,128)(2,1)S(1)}, u32[]{:S(2)}, u32[]{:S(2)}) collective-permute-start(bf16[256,512]{1,0:T(8,128)(2,1)S(1)} %get-tuple-element.66), channel_id=1, source_target_pairs={{0,3},{1,0},{2,1},{3,2},{4,7},{5,4},{6,5},{7,6},{8,11},{9,8},{10,9... | collective-permute-start | bytes 786440 | tf_op jit(solution)/shard_map/ppermute | solution.py:529
  51.7 12.7 %collective-permute-start.14 = (bf16[256,512]{1,0:T(8,128)(2,1)S(1)}, bf16[256,512]{1,0:T(8,128)(2,1)S(1)}, u32[]{:S(2)}, u32[]{:S(2)}) collective-permute-start(bf16[256,512]{1,0:T(8,128)(2,1)S(1)} %get-tuple-element.63), channel_id=1, source_target_pairs={{0,1},{1,2},{2,3},{3,0},{4,5},{5,6},{6,7},{7,4},{8,9},{9,10},{10,1... | collective-permute-start | bytes 786440 | tf_op jit(solution)/shard_map/ppermute | solution.py:529
  51.8 15.8 %collective-permute-start.13 = (bf16[256,512]{1,0:T(8,128)(2,1)S(1)}, bf16[256,512]{1,0:T(8,128)(2,1)S(1)}, u32[]{:S(2)}, u32[]{:S(2)}) collective-permute-start(bf16[256,512]{1,0:T(8,128)(2,1)S(1)} %get-tuple-element.61), channel_id=1, source_target_pairs={{0,3},{1,0},{2,1},{3,2},{4,7},{5,4},{6,5},{7,6},{8,11},{9,8},{10,9... | collective-permute-start | bytes 786440 | tf_op jit(solution)/shard_map/ppermute | solution.py:529
  58.1 16.1 %collective-permute-start.10 = (bf16[512,512]{1,0:T(8,128)(2,1)S(1)}, bf16[512,512]{1,0:T(8,128)(2,1)S(1)}, u32[]{:S(2)}, u32[]{:S(2)}) collective-permute-start(bf16[512,512]{1,0:T(8,128)(2,1)S(1)} %get-tuple-element.58), channel_id=1, source_target_pairs={{0,1},{1,2},{2,3},{3,0},{4,5},{5,6},{6,7},{7,4},{8,9},{9,10},{10,1... | collective-permute-start | bytes 1572872 | tf_op jit(solution)/shard_map/ppermute | solution.py:529
  60.2 15.7 %collective-permute-start.9 = (bf16[512,512]{1,0:T(8,128)(2,1)S(1)}, bf16[512,512]{1,0:T(8,128)(2,1)S(1)}, u32[]{:S(2)}, u32[]{:S(2)}) collective-permute-start(bf16[512,512]{1,0:T(8,128)(2,1)S(1)} %get-tuple-element.56), channel_id=1, source_target_pairs={{0,3},{1,0},{2,1},{3,2},{4,7},{5,4},{6,5},{7,6},{8,11},{9,8},{10,9... | collective-permute-start | bytes 1572872 | tf_op jit(solution)/shard_map/ppermute | solution.py:529
  64.3 12.8 %collective-permute-start.19 = (bf16[256,256]{1,0:T(8,128)(2,1)S(1)}, bf16[256,256]{1,0:T(8,128)(2,1)S(1)}, u32[]{:S(2)}, u32[]{:S(2)}) collective-permute-start(bf16[256,256]{1,0:T(8,128)(2,1)S(1)} %get-tuple-element.79), channel_id=1, source_target_pairs={{0,1},{1,2},{2,3},{3,0},{4,5},{5,6},{6,7},{7,4},{8,9},{9,10},{10,1... | collective-permute-start | bytes 393224 | tf_op jit(solution)/shard_map/ppermute | solution.py:529
  64.4 15.5 %collective-permute-start.20 = (bf16[256,256]{1,0:T(8,128)(2,1)S(1)}, bf16[256,256]{1,0:T(8,128)(2,1)S(1)}, u32[]{:S(2)}, u32[]{:S(2)}) collective-permute-start(bf16[256,256]{1,0:T(8,128)(2,1)S(1)} %get-tuple-element.80), channel_id=1, source_target_pairs={{0,3},{1,0},{2,1},{3,2},{4,7},{5,4},{6,5},{7,6},{8,11},{9,8},{10,9... | collective-permute-start | bytes 393224 | tf_op jit(solution)/shard_map/ppermute | solution.py:529
  67.7 12.3 %collective-permute-start.15 = (bf16[256,256]{1,0:T(8,128)(2,1)S(1)}, bf16[256,256]{1,0:T(8,128)(2,1)S(1)}, u32[]{:S(2)}, u32[]{:S(2)}) collective-permute-start(bf16[256,256]{1,0:T(8,128)(2,1)S(1)} %get-tuple-element.75), channel_id=1, source_target_pairs={{0,1},{1,2},{2,3},{3,0},{4,5},{5,6},{6,7},{7,4},{8,9},{9,10},{10,1... | collective-permute-start | bytes 393224 | tf_op jit(solution)/shard_map/ppermute | solution.py:529
  74.3 7.2 %collective-permute-start.16 = (bf16[256,256]{1,0:T(8,128)(2,1)S(1)}, bf16[256,256]{1,0:T(8,128)(2,1)S(1)}, u32[]{:S(2)}, u32[]{:S(2)}) collective-permute-start(bf16[256,256]{1,0:T(8,128)(2,1)S(1)} %get-tuple-element.76), channel_id=1, source_target_pairs={{0,3},{1,0},{2,1},{3,2},{4,7},{5,4},{6,5},{7,6},{8,11},{9,8},{10,9... | collective-permute-start | bytes 393224 | tf_op jit(solution)/shard_map/ppermute | solution.py:529
  76.0 8.6 %collective-permute-start.11 = (bf16[512,256]{1,0:T(8,128)(2,1)S(1)}, bf16[512,256]{1,0:T(8,128)(2,1)S(1)}, u32[]{:S(2)}, u32[]{:S(2)}) collective-permute-start(bf16[512,256]{1,0:T(8,128)(2,1)S(1)} %get-tuple-element.71), channel_id=1, source_target_pairs={{0,1},{1,2},{2,3},{3,0},{4,5},{5,6},{6,7},{7,4},{8,9},{9,10},{10,1... | collective-permute-start | bytes 786440 | tf_op jit(solution)/shard_map/ppermute | solution.py:529
  77.1 8.3 %collective-permute-start.12 = (bf16[512,256]{1,0:T(8,128)(2,1)S(1)}, bf16[512,256]{1,0:T(8,128)(2,1)S(1)}, u32[]{:S(2)}, u32[]{:S(2)}) collective-permute-start(bf16[512,256]{1,0:T(8,128)(2,1)S(1)} %get-tuple-element.72), channel_id=1, source_target_pairs={{0,3},{1,0},{2,1},{3,2},{4,7},{5,4},{6,5},{7,6},{8,11},{9,8},{10,9... | collective-permute-start | bytes 786440 | tf_op jit(solution)/shard_map/ppermute | solution.py:529
  (1 other events, 2.1 us)
